TPU v7x, 512 devices: a whole 4x4x16 slice. The times are simulated.
512 devices in a mesh: row: 16 (over y, x), col: 16 (over z), depth: 2 (over core).
Axes of the slice: x: 4, y: 4, z: 16, core: 2. Of those that a mesh axis runs over, the one named last changes fastest.
Arguments:
- left_store: float32 [16, 2, 16, 2, 64, 1024], P('row', 'depth', 'col'), may hold values from -6 to 6
- left_home: int32 [16, 2, 16], P('row', 'depth'), may hold values from 0 to 15, each once within a row
- up_store: float32 [16, 2, 16, 2, 64, 1024], P('col', 'depth', 'row'), may hold values from -0.3125 to 0.3125
- up_home: int32 [16, 2, 16], P('col', 'depth'), may hold values from 0 to 15, each once within a row
- targets: int32 [16, 16, 2], P('row', 'col'), may hold values from 0 to 63, as said below
- sketch: float32 [16, 16, 2, 64, 1024], P('row', 'col'), may hold values from -0.1875 to 0.1875
Outputs:
- basis: float32 [16, 16, 2, 64, 1024], P('row', 'col', 'depth')
- weights: float32 [16, 16, 2, 64, 1024], P('row', 'col', 'depth')
Inputs may be any that keep to these rules, and one draw needn't show every extreme that they name: `left_home`: for each row and depth index the entries are the store positions 0 to 15, each once. `up_home`: for each col and depth index the entries are the store positions 0 to 15, each once. `targets`: the 2 entries of one row and col index are distinct.
All inputs are finite; a program needn't handle non-finite values.
Results may differ from a plain program's by a relative error of at most 0.0003.
Values sent between devices are 32-bit elements; how exact they have to be, the bound alone decides.
No kernel may reach another device: no remote copies, remote signals or barrier semaphores. Data moves between devices by JAX's collectives and lax.ppermute only.
A program may use at most 128 MiB of HBM per device.

v0:
```python
import math

import jax
import jax.numpy as jnp
from jax import lax
from jax.sharding import PartitionSpec as P

KD = 2
RB = 8
CB = 8


def split_up(shard, dim, devices):
    before, after = (shard.shape[:dim], shard.shape[dim + 1 :])
    return jnp.moveaxis(shard.reshape(*before, devices, -1, *after), dim, 0)


def sent_and_summed(shard, axis, dim):
    devices = lax.axis_size(axis)
    pieces = lax.all_to_all(split_up(shard, dim, devices), axis, 0, 0, tiled=True)
    return jnp.sum(pieces, axis=0)


def laid_out(pieces, dim):
    pieces = jnp.moveaxis(pieces, 0, dim)
    shape = pieces.shape
    return pieces.reshape(*shape[:dim], shape[dim] * shape[dim + 1], *shape[dim + 2 :])


def copy_for_each(shard, axis):
    devices = lax.axis_size(axis)
    return lax.all_to_all(
        jnp.broadcast_to(shard[None], (devices, *shard.shape)), axis, 0, 0, tiled=True
    )


def gathered_copies(shard, axis, dim):
    return laid_out(copy_for_each(shard, axis), dim)


def orthonormal(sample):
    gram_mat = jnp.einsum("pat,pbt->pab", sample, sample, precision=lax.Precision.HIGHEST)
    factor_low = jnp.linalg.cholesky(gram_mat)
    return lax.linalg.triangular_solve(factor_low, sample, left_side=True, lower=True)


def shards(left_store, left_home, up_store, up_home, targets, sketch):
    high = lax.Precision.HIGHEST
    left_local = left_store[0, 0]
    up_local = up_store[0, 0]
    left_table = left_home[0, 0]
    up_table = up_home[0, 0]
    left_all = lax.all_gather(left_local, "col", axis=0, tiled=True)
    up_all = lax.all_gather(up_local, "row", axis=0, tiled=True)
    left_pairs = jnp.take(left_all, left_table, axis=0)
    up_pairs = jnp.take(up_all, up_table, axis=0)
    chosen = targets[0, 0]
    block_row = chosen // CB
    block_col = chosen % CB
    row_pairs = jnp.take(left_pairs.reshape((RB, KD) + left_local.shape[1:]), block_row, axis=0)
    col_pairs = jnp.take(up_pairs.reshape((CB, KD) + up_local.shape[1:]), block_col, axis=0)
    row_basis = row_pairs[:, :, 0]
    row_coef = row_pairs[:, :, 1]
    col_coef = col_pairs[:, :, 0]
    col_basis = col_pairs[:, :, 1]
    test_rows = sketch[0, 0]
    middle = jnp.einsum("pkat,pkbt->pkab", row_coef, col_coef, precision=high)
    test_side = jnp.einsum("pat,pkbt->pkab", test_rows, col_basis, precision=high)
    folded = jnp.einsum("pkab,pkcb->pkac", test_side, middle, precision=high)
    sample_part = jnp.einsum("pkac,pkct->pat", folded, row_basis, precision=high)
    own_sketch = sent_and_summed(sample_part, "depth", 0)
    own_basis = orthonormal(own_sketch)
    bases = gathered_copies(own_basis, "depth", 0)
    inner_prod = jnp.einsum("pat,pkct->pkac", bases, row_basis, precision=high)
    turned = jnp.einsum("pkac,pkcb->pkab", inner_prod, middle, precision=high)
    project_part = jnp.einsum("pkab,pkbt->pat", turned, col_basis, precision=high)
    projected = sent_and_summed(project_part, "depth", 0)
    root_tile = math.sqrt(test_rows.shape[-1])
    return ((own_basis * root_tile)[None, None], (projected / root_tile)[None, None])


def solution(mesh):
    return jax.shard_map(
        shards,
        mesh=mesh,
        in_specs=(
            P("row", "depth", "col", None, None, None),
            P("row", "depth", None),
            P("col", "depth", "row", None, None, None),
            P("col", "depth", None),
            P("row", "col", None),
            P("row", "col", None, None, None),
        ),
        out_specs=(P("row", "col", "depth", None, None), P("row", "col", "depth", None, None)),
        check_vma=False,
    )
```

profile of v0, /device:TPU:1, one launch (start us, length us, event | category | flops | bytes accessed | tf_op | source)
XLA Modules:
  0.0 273.3 jit_solution(12288357249461976770)
XLA Ops:
  7.2 0.0 copy-start
  7.2 0.0 all-gather.7.cloned.1.call-start
  7.2 0.7 all-gather.7.cloned.1.call-update
  7.9 0.0 all-gather.5.cloned.1.call-start
  8.0 0.7 all-gather.5.cloned.1.call-update
  8.7 0.7 compare_select_fusion.1
  9.3 0.7 compare_and_fusion
  10.0 0.7 compare_select_fusion.3
  10.7 0.7 compare_and_fusion.1
  11.4 0.7 compare_and_fusion.3
  12.0 109.1 %all-gather.7.cloned.1.call-done = f32[16,1,1,2,64,1024]{5,4,3,2,1,0:T(8,128)} async-done(((f32[1,1,1,2,64,1024]{5,4,3,2,1,0:T(8,128)}), f32[16,1,1,2,64,1024]{5,4,3,2,1,0:T(8,128)}) %all-gather.7.cloned.1.call-update) | async-done | bytes 8388624 | tf_op jit(solution)/shard_map/all_gather | solution.py:53
  121.1 7.7 %gather_fusion.2 = f32[16,2,64,1024]{3,2,1,0:T(8,128)} fusion(f32[16,2,64,1024]{3,2,1,0:T(8,128)} %bitcast.97, s32[1024]{0:T(1024)S(1)} %pad_clamp_fusion.1), kind=kCustom, calls=%fused_computation.2.clone | custom fusion | bytes 16777280 | tf_op jit(solution)/shard_map/jit(_take)/gather | solution.py:55
  128.8 8.6 %broadcast_select_fusion = f32[16,2,64,1024]{3,2,1,0:T(8,128)} fusion(f32[16,2,64,1024]{3,2,1,0:T(8,128)} %gather_fusion.2, pred[16]{0:T(512)(128)(4,1)S(1)} %compare_and_fusion.1), kind=kLoop, calls=%fused_computation.4 | loop fusion | flops 2097152 | bytes 16777232 | tf_op jit(solution)/shard_map/jit(_take)/select_n | solution.py:55
  137.4 5.8 %gather_fusion.3 = f32[2,2,2,64,1024]{4,3,2,1,0:T(8,128)} fusion(f32[8,2,2,64,1024]{4,3,2,1,0:T(8,128)} %bitcast.94, s32[1024]{0:T(1024)S(1)} %pad_clamp_fusion), kind=kCustom, calls=%fused_computation.3.clone | custom fusion | bytes 4194312 | tf_op jit(solution)/shard_map/jit(_take)/gather | solution.py:60
  143.2 65.0 %all-gather.5.cloned.1.call-done = f32[16,1,1,2,64,1024]{5,4,3,2,1,0:T(8,128)} async-done(((f32[1,1,1,2,64,1024]{5,4,3,2,1,0:T(8,128)}), f32[16,1,1,2,64,1024]{5,4,3,2,1,0:T(8,128)}) %all-gather.5.cloned.1.call-update) | async-done | bytes 8388624 | tf_op jit(solution)/shard_map/all_gather | solution.py:54
  208.2 7.7 %gather_fusion = f32[16,2,64,1024]{3,2,1,0:T(8,128)} fusion(f32[16,2,64,1024]{3,2,1,0:T(8,128)} %bitcast.96, s32[1024]{0:T(1024)S(1)} %pad_clamp_fusion.3), kind=kCustom, calls=%fused_computation.clone | custom fusion | bytes 16777280 | tf_op jit(solution)/shard_map/jit(_take)/gather | solution.py:56
  215.8 8.6 %broadcast_select_fusion.1 = f32[16,2,64,1024]{3,2,1,0:T(8,128)} fusion(f32[16,2,64,1024]{3,2,1,0:T(8,128)} %gather_fusion, pred[16]{0:T(512)(128)(4,1)S(1)} %compare_and_fusion.3), kind=kLoop, calls=%fused_computation.5 | loop fusion | flops 2097152 | bytes 16777232 | tf_op jit(solution)/shard_map/jit(_take)/select_n | solution.py:56
  224.4 5.4 %gather_fusion.1 = f32[2,2,2,64,1024]{4,3,2,1,0:T(8,128)} fusion(f32[8,2,2,64,1024]{4,3,2,1,0:T(8,128)} %bitcast.95, s32[1024]{0:T(1024)S(1)} %pad_clamp_fusion.2), kind=kCustom, calls=%fused_computation.1.clone | custom fusion | bytes 4194312 | tf_op jit(solution)/shard_map/jit(_take)/gather | solution.py:61
  229.9 2.8 %copy_select_fusion = (f32[2,2,2,64,1024]{4,3,1,0,2:T(8,128)S(1)}, f32[2,2,2,64,1024]{4,3,1,0,2:T(8,128)S(1)}) fusion(f32[2,2,2,64,1024]{4,3,2,1,0:T(8,128)} %gather_fusion.3, pred[2]{0:T(512)(128)(4,1)S(1)} %get-tuple-element.4, f32[2,2,2,64,1024]{4,3,2,1,0:T(8,128)} %gather_fusion.1, pred[2]{0:T(512)(128)(4,1)S(1)} %get-tuple-element.8), kind=kLoop, calls=%fused_computation.6 | loop fusion | flops 1048576 | bytes 8388612 | tf_op jit(solution)/shard_map/jit(_take)/select_n | solution.py:60
  232.6 0.0 copy-start.1
  232.6 0.0 copy-done
  232.7 1.6 fusion.1
  234.3 1.1 fusion
  235.4 0.3 fusion.9
  235.7 0.0 copy-done.1
  235.7 0.7 convolution_bitcast_fusion.1
  236.4 4.6 %all_to_all.15 = f32[2,1,64,1024]{3,2,1,0:T(8,128)S(1)} all-to-all(f32[2,1,64,1024]{3,2,1,0:T(8,128)S(1)} %convolution_bitcast_fusion.1), channel_id=1, replica_groups=mesh['row'=16,'col'=16,'depth'=2] {'depth'}, dimensions={0} | all-to-all | bytes 1048576 | tf_op jit(solution)/shard_map/all_to_all | solution.py:20
  241.1 0.4 fusion.10
  241.4 0.1 copy.27
  241.5 5.8 %custom-call.7 = f32[1,64,64]{2,1,0:T(8,128)S(1)} custom-call(f32[1,64,64]{2,1,0:T(8,128)S(1)} %fusion.6), custom_call_target="Cholesky" | custom-call | tf_op jit(solution)/shard_map/jit(cholesky)/cholesky | solution.py:43
  247.4 0.6 compare_reduce_fusion
  248.1 0.7 fusion.5
  248.7 4.9 %custom-call.8 = f32[1,1,64,64]{2,3,1,0:T(8,128)S(1)} custom-call(f32[1,1,64,64]{3,2,1,0:T(8,128)S(1)} %fusion.5), custom_call_target="InvertDiagBlocksLowerTriangular" | custom-call | tf_op jit(solution)/shard_map/triangular_solve | solution.py:44
  253.6 0.0 copy-start.2
  253.6 0.4 fusion.7
  254.1 0.7 multiply_bitcast_fusion.1
  254.8 4.2 %all_to_all.16 = f32[2,1,64,1024]{3,2,1,0:T(8,128)S(1)} all-to-all(f32[2,1,64,1024]{3,2,1,0:T(8,128)S(1)} %broadcast_in_dim.33), channel_id=1, replica_groups=mesh['row'=16,'col'=16,'depth'=2] {'depth'}, dimensions={0} | all-to-all | bytes 1048576 | tf_op jit(solution)/shard_map/all_to_all | solution.py:32
  259.0 0.0 copy-done.2
  259.0 1.6 fusion.2
  260.6 0.3 fusion.11
  260.9 0.7 convolution_bitcast_fusion
  261.6 4.2 %all_to_all.17 = f32[2,1,64,1024]{3,2,1,0:T(8,128)S(1)} all-to-all(f32[2,1,64,1024]{3,2,1,0:T(8,128)S(1)} %convolution_bitcast_fusion), channel_id=1, replica_groups=mesh['row'=16,'col'=16,'depth'=2] {'depth'}, dimensions={0} | all-to-all | bytes 1048576 | tf_op jit(solution)/shard_map/all_to_all | solution.py:20
  265.8 0.7 multiply_bitcast_fusion
  (9 shorter events, 0.2 us)
Async XLA Ops:
  7.2 225.5 %copy-start = (f32[1,1,2,64,1024]{4,3,2,1,0:T(8,128)S(1)}, f32[1,1,2,64,1024]{4,3,2,1,0:T(8,128)}, u32[]{:S(2)}) copy-start(f32[1,1,2,64,1024]{4,3,2,1,0:T(8,128)} %param.15) | copy-start | bytes 1572868
  7.2 113.9 %all-gather.7.cloned.1.call-start = ((), (), s32[]{:S(2)}) async-start(), calls=%async_computation.4 | async-start | bytes 8912896 | tf_op jit(solution)/shard_map/all_gather | solution.py:53
  7.9 200.3 %all-gather.5.cloned.1.call-start = ((), (), s32[]{:S(2)}) async-start(), calls=%async_computation.3 | async-start | bytes 8912896 | tf_op jit(solution)/shard_map/all_gather | solution.py:54
  232.6 3.1 %copy-start.1 = (f32[2,2,2,64,1024]{4,3,1,0,2:T(8,128)}, f32[2,2,2,64,1024]{4,3,1,0,2:T(8,128)S(1)}, u32[]{:S(2)}) copy-start(f32[2,2,2,64,1024]{4,3,1,0,2:T(8,128)S(1)} %get-tuple-element.10) | copy-start | bytes 6291460
  253.6 5.4 %copy-start.2 = (f32[2,2,2,64,1024]{4,3,1,0,2:T(8,128)S(1)}, f32[2,2,2,64,1024]{4,3,1,0,2:T(8,128)}, u32[]{:S(2)}) copy-start(f32[2,2,2,64,1024]{4,3,1,0,2:T(8,128)} %copy-done.1) | copy-start | bytes 6291460
Sparse Core Ops, SparseCore 0:
  10.1 110.9 all-gather.6
  124.1 84.0 all-gather.4
where the time goes:
time: 274 us; the launch traced here: 273 us
  waiting for transfers between devices  175 us (64%)
  other arithmetic  36.9 us (13%)
  local copies, waits for them, and re-layouts  26.7 us (10%)
  between operations  14.2 us (5%)
  blocking collectives  12.9 us (5%)
  matrix products  7.07 us (3%)
    all_gather x1, waiting for transfers between devices, shards(): left_all = lax.all_gather(left_local, 'col', axis=0, tiled=True)  109 us
    all_gather x1, waiting for transfers between devices, shards(): up_all = lax.all_gather(up_local, 'row', axis=0, tiled=True)  65 us
    select_n x2, other arithmetic, shards(): left_pairs = jnp.take(left_all, left_table, axis=0)  9.27 us
    select_n x2, other arithmetic, shards(): up_pairs = jnp.take(up_all, up_table, axis=0)  9.26 us
    all_to_all x2, blocking collectives, sent_and_summed(): lax.all_to_all(split_up(shard, dim, devices), axis, 0, 0, tiled=True)  8.78 us
    gather x1, local copies, waits for them, and re-layouts, shards(): left_pairs = jnp.take(left_all, left_table, axis=0)  7.68 us
    gather x1, local copies, waits for them, and re-layouts, shards(): up_pairs = jnp.take(up_all, up_table, axis=0)  7.67 us
    another operation x3, other arithmetic, orthonormal(): factor_low = jnp.linalg.cholesky(gram_mat)  6.52 us
  transfers between devices with their start and end apart: 2, of which 2 were waited for; matrix products, arithmetic and copies ran while one was open for 9% of the time, Pallas kernels for 0%

commit v1 on v0

v1 whole, which is shorter than its diff:
```python
import math

import jax
import jax.numpy as jnp
from jax import lax
from jax.experimental import pallas as pl
from jax.experimental.pallas import tpu as pltpu
from jax.sharding import PartitionSpec as P


KD = 2
CB = 8
SIDE = 4
HIGH = lax.Precision.HIGHEST
UP_AT, TARGET_AT, ROW_AT, COL_AT, DEPTH_AT = 16, 32, 34, 35, 36


def z_shift(n_col):
    return [(c * 2 + d, ((c + (1 - 2 * d)) % n_col) * 2 + d) for c in range(n_col) for d in (0, 1)]


def xy_shift(step, phase):
    pairs = []
    for r in range(SIDE * SIDE):
        y, x = divmod(r, SIDE)
        for d in (0, 1):
            if (d + phase) % 2 == 0:
                to = y * SIDE + (x + step) % SIDE
            else:
                to = (y + step) % SIDE * SIDE + x
            pairs.append((r * 2 + d, to * 2 + d))
    return pairs


SWAP = [(0, 1), (1, 0)]


def ring_steps(info, position):
    way = info[COL_AT] - position
    return jnp.where(info[DEPTH_AT] == 0, way, -way) & 15


def up_place(info, position):
    row = info[ROW_AT]
    dy = (row // SIDE - position // SIDE) & (SIDE - 1)
    dx = (row - position) & (SIDE - 1)
    first = info[DEPTH_AT] == 0
    return jnp.where(first, dy, dx), jnp.where(first, dx, dy)


def up_choice_kernel(info, u0, u1, u2, u3, out, sems):
    ups = (u0, u1, u2, u3)
    tile = info[TARGET_AT + 1 - info[DEPTH_AT]]
    j = tile % CB
    for k in range(KD):
        t, s = up_place(info, info[UP_AT + j * KD + k])
        for i in range(SIDE):

            @pl.when(t == i)
            def _():
                pltpu.make_async_copy(ups[i].at[s], out.at[k], sems.at[k]).start()

    for k in range(KD):
        pltpu.make_async_copy(u0.at[0], out.at[k], sems.at[k]).wait()


def left_choice_kernel(info, other, *refs):
    own, across, out, sems = refs[:7], refs[7:14], refs[14], refs[15]
    tile = info[TARGET_AT + 1 - info[DEPTH_AT]]
    b = tile // CB
    for kind, (table, pieces) in enumerate(((info, own), (other, across))):
        for k in range(KD):
            slot = (1 - kind) * KD + k
            s = ring_steps(info, table[b * KD + k])
            for i in range(7):

                @pl.when(s == i + 1)
                def _():
                    pltpu.make_async_copy(pieces[i], out.at[slot], sems.at[slot]).start()

            @pl.when((s >= 1) & (s <= 7))
            def _():
                pltpu.make_async_copy(pieces[0], out.at[slot], sems.at[slot]).wait()


def dot(a, b, contract):
    return lax.dot_general(a, b, ((contract[:1], contract[1:]), ((), ())), precision=HIGH, preferred_element_type=jnp.float32)


def inverse_factor(gram):
    n = gram.shape[0]
    row_id = lax.broadcasted_iota(jnp.int32, (n, n), 0)
    lane_id = lax.broadcasted_iota(jnp.int32, (n, n), 1)
    eye = jnp.where(row_id == lane_id, jnp.float32(1), jnp.float32(0))
    work = jnp.concatenate([gram, eye], axis=1)
    blocks = [work[8 * i : 8 * i + 8] for i in range(n // 8)]
    sub = lax.broadcasted_iota(jnp.int32, (8, 2 * n), 0)
    for k in range(n):
        at, within = divmod(k, 8)
        row = blocks[at][within : within + 1]
        scale = lax.rsqrt(row[:, k : k + 1])
        row = row * scale
        for i in range(at, n // 8):
            change = (blocks[i][:, k : k + 1] * scale) * row
            if i == at:
                blocks[i] = jnp.where(sub > within, blocks[i] - change, jnp.where(sub == within, row, blocks[i]))
            else:
                blocks[i] = blocks[i] - change
    return jnp.concatenate(blocks, axis=0)[:, n:]


def tile_kernel(info, other, *refs):
    own, across = refs[:9], refs[9:17]
    left_in, last_in = refs[17:19]
    ups, up_in, sketch = refs[19:23], refs[23], refs[24]
    basis_out, weights_out = refs[25:27]
    xs, ys, ps, qs, ws, left_sems, up_sems, sketch_sem = refs[27:]
    depth = info[DEPTH_AT]
    tile = info[TARGET_AT + depth]
    b, j = tile // CB, tile % CB
    n, size = ws.shape

    def left_copies(source, slot):
        return (
            pltpu.make_async_copy(source.at[0], xs.at[slot], left_sems.at[slot, 0]),
            pltpu.make_async_copy(source.at[1], ys.at[slot], left_sems.at[slot, 1]),
        )

    def up_copies(source, slot):
        return (
            pltpu.make_async_copy(source.at[0], ps.at[slot], up_sems.at[slot, 0]),
            pltpu.make_async_copy(source.at[1], qs.at[slot], up_sems.at[slot, 1]),
        )

    def start(condition, copies):
        @pl.when(condition)
        def _():
            for copy in copies:
                copy.start()

    pltpu.make_async_copy(sketch.at[depth], ws, sketch_sem).start()
    for kind, (table, pieces) in enumerate(((info, own), (other, across))):
        for k in range(KD):
            slot = kind * KD + k
            s = ring_steps(info, table[b * KD + k])
            for i, piece in enumerate(pieces):
                start(s == i, left_copies(piece, slot))
            if kind == 1:
                start(s == 8, left_copies(last_in, slot))
            start(s > 8, left_copies(left_in.at[slot], slot))
            if kind == 0:
                t, s = up_place(info, table[UP_AT + j * KD + k])
                for i in range(SIDE):
                    start(t == i, up_copies(ups[i].at[s], slot))
            else:
                for copy in up_copies(up_in.at[k], slot):
                    copy.start()
    pltpu.make_async_copy(sketch.at[0], ws, sketch_sem).wait()
    slots = 2 * KD
    for slot in range(slots):
        for copy in (*up_copies(up_in.at[0], slot), *left_copies(own[0], slot)):
            copy.wait()
    x_all = xs[...].reshape(slots * n, size)
    q_all = qs[...].reshape(slots * n, size)
    tested = dot(ws[...], q_all, (1, 1))
    middles = [dot(ys[i], ps[i], (1, 1)) for i in range(slots)]
    folded = jnp.concatenate([dot(tested[:, i * n : i * n + n], middles[i], (1, 1)) for i in range(slots)], axis=1)
    sample = dot(folded, x_all, (1, 0))
    inverse = inverse_factor(dot(sample, sample, (1, 1)))
    bases = dot(inverse, sample, (1, 0))
    root = math.sqrt(size)
    basis_out[...] = bases * root
    inner = dot(bases, x_all, (1, 1))
    turned = jnp.concatenate([dot(inner[:, i * n : i * n + n], middles[i], (1, 0)) for i in range(slots)], axis=1)
    weights_out[...] = dot(turned, q_all, (1, 0)) * (1 / root)


def local_kernel(kernel, n_scalar, n_any, out_shape, out_space, scratch, mebibytes=1):
    return pl.pallas_call(
        kernel,
        out_shape=out_shape,
        in_specs=[pl.BlockSpec(memory_space=pltpu.SMEM)] * n_scalar + [pl.BlockSpec(memory_space=pltpu.HBM)] * n_any,
        out_specs=jax.tree.map(lambda _: pl.BlockSpec(memory_space=out_space), out_shape),
        scratch_shapes=scratch,
        compiler_params=pltpu.CompilerParams(vmem_limit_bytes=mebibytes << 20),
    )


def pieces_and_tile(left_store, left_home, up_store, up_home, targets, sketch):
    n_col = lax.axis_size("col")
    own, up, test = left_store[0, 0, 0], up_store[0, 0, 0], sketch[0, 0]
    pair = own.shape
    places = jnp.stack([lax.axis_index(a).astype(jnp.int32) for a in ("row", "col", "depth")])
    info = jnp.concatenate([left_home[0, 0], up_home[0, 0], targets[0, 0], places])
    across = lax.ppermute(own, "depth", SWAP)
    own_pieces, across_pieces = [own], [across]
    shift = z_shift(n_col)
    half = n_col // 2
    for step in range(1, half + 1):
        own_pieces.append(lax.ppermute(own_pieces[-1], ("col", "depth"), shift))
        if step < half:
            across_pieces.append(lax.ppermute(across_pieces[-1], ("col", "depth"), shift))
    block = jnp.stack([up] + [lax.ppermute(up, ("row", "depth"), xy_shift(s, 0)) for s in range(1, SIDE)])
    ups = [block] + [lax.ppermute(block, ("row", "depth"), xy_shift(s, 1)) for s in range(1, SIDE)]
    other = lax.ppermute(info, "depth", SWAP)

    f32 = jnp.float32
    up_choice = local_kernel(up_choice_kernel, 1, SIDE, jax.ShapeDtypeStruct((KD, *pair), f32), pltpu.HBM, [pltpu.SemaphoreType.DMA((KD,))])
    up_in = lax.ppermute(up_choice(info, *ups), "depth", SWAP)
    left_choice = local_kernel(left_choice_kernel, 2, 14, jax.ShapeDtypeStruct((2 * KD, *pair), f32), pltpu.HBM, [pltpu.SemaphoreType.DMA((2 * KD,))])
    left_in = lax.ppermute(left_choice(info, other, *own_pieces[1:8], *across_pieces[1:8]), "depth", SWAP)
    last_in = lax.ppermute(own_pieces[8], "depth", SWAP)

    flat = pair[1:]
    tile = jax.ShapeDtypeStruct(flat, f32)
    stack = pltpu.VMEM((2 * KD, *flat), f32)
    sems = pltpu.SemaphoreType.DMA((2 * KD, 2))
    whole = local_kernel(tile_kernel, 2, 25, (tile, tile), pltpu.VMEM, [stack] * 4 + [pltpu.VMEM(flat, f32), sems, sems, pltpu.SemaphoreType.DMA], 12)
    basis, weights = whole(info, other, *own_pieces, *across_pieces, left_in, last_in, *ups, up_in, test)
    return basis[None, None, None], weights[None, None, None]


def solution(mesh):
    return jax.shard_map(
        pieces_and_tile,
        mesh=mesh,
        in_specs=(
            P("row", "depth", "col", None, None, None),
            P("row", "depth", None),
            P("col", "depth", "row", None, None, None),
            P("col", "depth", None),
            P("row", "col", None),
            P("row", "col", None, None, None),
        ),
        out_specs=(P("row", "col", "depth", None, None), P("row", "col", "depth", None, None)),
        check_vma=False,
    )
```

time: 274 us -> 166 us (0.61)
  waiting for transfers between devices: 175 us -> 36.6 us
  starting transfers between devices: 0.08 us -> 108 us
  other arithmetic: 36.9 us -> 1.65 us
  local copies, waits for them, and re-layouts: 26.7 us -> 1.58 us
  Pallas kernels: 0 us -> 16.4 us
  between operations: 14.2 us -> 1.13 us
  blocking collectives: 12.9 us -> 0 us
  matrix products: 7.07 us -> 0 us
    all_gather x2 -> x0, waiting for transfers between devices: 174 us -> none  [the longest x1 109 us: shards(): left_all = lax.all_gather(left_local, 'col', axis=0, tiled=True)]
    ppermute x0 -> x26, starting transfers between devices: none -> 108 us  [the longest x8 32.5 us: pieces_and_tile(): own_pieces.append(lax.ppermute(own_pieces[-1], ('col', 'depth'), shift))]
    ppermute x0 -> x26, waiting for transfers between devices: none -> 36.6 us  [the longest x8 17.8 us: pieces_and_tile(): own_pieces.append(lax.ppermute(own_pieces[-1], ('col', 'depth'), shift))]
    gather x4 -> x0, local copies, waits for them, and re-layouts: 26.6 us -> none  [the longest x1 7.68 us: shards(): left_pairs = jnp.take(left_all, left_table, axis=0)]
    select_n x5 -> x0, other arithmetic: 21.3 us -> none  [the longest x2 9.27 us: shards(): left_pairs = jnp.take(left_all, left_table, axis=0)]
    pallas_call x0 -> x3, Pallas kernels: none -> 16.4 us  [the longest x1 14.9 us: pieces_and_tile(): whole(info, other, *own_pieces, *across_pieces, left_in, last_in, *ups, u...]
    all_to_all x3 -> x0, blocking collectives: 12.9 us -> none  [the longest x2 8.78 us: sent_and_summed(): lax.all_to_all(split_up(shard, dim, devices), axis, 0, 0, tiled=True)]
    another operation x5 -> x1, other arithmetic: 12.1 us -> 1.65 us  [pieces_and_tile(): jnp.stack([up] + [lax.ppermute(up, ('row', 'depth'), xy_shift(s, 0)) for...]
  transfers between devices with their start and end apart: 2 -> 26, of which waited for: 2 -> 16; matrix products, arithmetic and copies ran while one was open for 9% -> 1% of each run, Pallas kernels for 0% -> 1%
where the time goes in v1:
time: 166 us; the launch traced here: 165 us
  starting transfers between devices  108 us (65%)
  waiting for transfers between devices  36.6 us (22%)
  Pallas kernels  16.4 us (10%)
    ppermute x8, starting transfers between devices, pieces_and_tile(): own_pieces.append(lax.ppermute(own_pieces[-1], ('col', 'depth'), shift))  32.5 us
    ppermute x7, starting transfers between devices, pieces_and_tile(): lax.ppermute(across_pieces[-1], ('col', 'depth'), shift)  26.7 us
    ppermute x8, waiting for transfers between devices, pieces_and_tile(): own_pieces.append(lax.ppermute(own_pieces[-1], ('col', 'depth'), shift))  17.8 us
    pallas_call x1, Pallas kernels, pieces_and_tile(): whole(info, other, *own_pieces, *across_pieces, left_in, last_in, *ups, u...  14.9 us
    ppermute x3, starting transfers between devices, pieces_and_tile(): lax.ppermute(block, ('row', 'depth'), xy_shift(s, 1))  10.5 us
    ppermute x3, starting transfers between devices, pieces_and_tile(): lax.ppermute(up, ('row', 'depth'), xy_shift(s, 0))  10.1 us
    ppermute x7, waiting for transfers between devices, pieces_and_tile(): lax.ppermute(across_pieces[-1], ('col', 'depth'), shift)  9.9 us
    ppermute x1, starting transfers between devices, pieces_and_tile(): lax.ppermute(left_choice(info, other, *own_pieces[1:8], *across_pieces[1:...  8.75 us
  transfers between devices with their start and end apart: 26, of which 16 were waited for; matrix products, arithmetic and copies ran while one was open for 1% of the time, Pallas kernels for 1%

profile of v1, /device:TPU:1, one launch (start us, length us, event | category | flops | bytes accessed | tf_op | source)
XLA Modules:
  0.0 165.1 jit_solution(13935913734243063396)
XLA Ops:
  0.6 8.7 %collective-permute-start.9 = (f32[2,64,1024]{2,1,0:T(8,128)}, f32[2,64,1024]{2,1,0:T(8,128)S(1)}, u32[]{:S(2)}, u32[]{:S(2)}) collective-permute-start(f32[2,64,1024]{2,1,0:T(8,128)} %bitcast.15), channel_id=1, source_target_pairs={{0,1},{1,0},{2,3},{3,2},{4,5},{5,4},{6,7},{7,6},{8,9},{9,8},{10,11... | collective-permute-start | bytes 1572872 | tf_op jit(solution)/shard_map/ppermute | solution.py:195
  9.4 5.8 %collective-permute-start.1 = (f32[2,64,1024]{2,1,0:T(8,128)}, f32[2,64,1024]{2,1,0:T(8,128)S(1)}, u32[]{:S(2)}, u32[]{:S(2)}) collective-permute-start(f32[2,64,1024]{2,1,0:T(8,128)} %bitcast.16), channel_id=1, source_target_pairs={{0,2},{1,31},{2,4},{3,1},{4,6},{5,3},{6,8},{7,5},{8,10},{9,7},{10,... | collective-permute-start | bytes 1572872 | tf_op jit(solution)/shard_map/ppermute | solution.py:200
  15.2 0.0 collective-permute-done.9.refs_9_
  15.2 2.6 %collective-permute-start.10 = (f32[2,64,1024]{2,1,0:T(8,128)S(1)}, f32[2,64,1024]{2,1,0:T(8,128)S(1)}, u32[]{:S(2)}, u32[]{:S(2)}) collective-permute-start(f32[2,64,1024]{2,1,0:T(8,128)S(1)} %collective-permute-done.9.refs_9_), channel_id=1, source_target_pairs={{0,2},{1,31},{2,4},{3,1},{4,6},{5,3},{6,8},{7,5},{8,10},{9,7},{10,... | collective-permute-start | bytes 1572872 | tf_op jit(solution)/shard_map/ppermute | solution.py:202
  17.8 0.0 copy-start.2
  17.8 0.8 copy-done.2
  18.6 3.0 %collective-permute-done.1.refs_0_.refs_1_ = f32[2,64,1024]{2,1,0:T(8,128)S(1)} collective-permute-done((f32[2,64,1024]{2,1,0:T(8,128)}, f32[2,64,1024]{2,1,0:T(8,128)S(1)}, u32[]{:S(2)}, u32[]{:S(2)}) %collective-permute-start.1) | collective-permute-done | bytes 524320 | tf_op jit(solution)/shard_map/ppermute | solution.py:200
  21.6 4.9 %collective-permute-start.2 = (f32[2,64,1024]{2,1,0:T(8,128)S(1)}, f32[2,64,1024]{2,1,0:T(8,128)S(1)}, u32[]{:S(2)}, u32[]{:S(2)}) collective-permute-start(f32[2,64,1024]{2,1,0:T(8,128)S(1)} %collective-permute-done.1.refs_0_.refs_1_), channel_id=1, source_target_pairs={{0,2},{1,31},{2,4},{3,1},{4,6},{5,3},{6,8},{7,5},{8,10},{9,7},{10,... | collective-permute-start | bytes 1572872 | tf_op jit(solution)/shard_map/ppermute | solution.py:200
  26.5 0.6 collective-permute-done.10.refs_7_.refs_10_
  27.1 5.0 %collective-permute-start.11 = (f32[2,64,1024]{2,1,0:T(8,128)S(1)}, f32[2,64,1024]{2,1,0:T(8,128)S(1)}, u32[]{:S(2)}, u32[]{:S(2)}) collective-permute-start(f32[2,64,1024]{2,1,0:T(8,128)S(1)} %collective-permute-done.10.refs_7_.refs_10_), channel_id=1, source_target_pairs={{0,2},{1,31},{2,4},{3,1},{4,6},{5,3},{6,8},{7,5},{8,10},{9,7},{10,... | collective-permute-start | bytes 1572872 | tf_op jit(solution)/shard_map/ppermute | solution.py:202
  32.1 0.6 collective-permute-done.2.refs_1_.refs_2_
  32.7 5.0 %collective-permute-start.3 = (f32[2,64,1024]{2,1,0:T(8,128)S(1)}, f32[2,64,1024]{2,1,0:T(8,128)S(1)}, u32[]{:S(2)}, u32[]{:S(2)}) collective-permute-start(f32[2,64,1024]{2,1,0:T(8,128)S(1)} %collective-permute-done.2.refs_1_.refs_2_), channel_id=1, source_target_pairs={{0,2},{1,31},{2,4},{3,1},{4,6},{5,3},{6,8},{7,5},{8,10},{9,7},{10,... | collective-permute-start | bytes 1572872 | tf_op jit(solution)/shard_map/ppermute | solution.py:200
  37.7 0.6 collective-permute-done.11.refs_8_.refs_11_
  38.3 5.0 %collective-permute-start.12 = (f32[2,64,1024]{2,1,0:T(8,128)S(1)}, f32[2,64,1024]{2,1,0:T(8,128)S(1)}, u32[]{:S(2)}, u32[]{:S(2)}) collective-permute-start(f32[2,64,1024]{2,1,0:T(8,128)S(1)} %collective-permute-done.11.refs_8_.refs_11_), channel_id=1, source_target_pairs={{0,2},{1,31},{2,4},{3,1},{4,6},{5,3},{6,8},{7,5},{8,10},{9,7},{10,... | collective-permute-start | bytes 1572872 | tf_op jit(solution)/shard_map/ppermute | solution.py:202
  43.4 0.6 collective-permute-done.3.refs_2_.refs_3_
  44.0 5.0 %collective-permute-start.4 = (f32[2,64,1024]{2,1,0:T(8,128)S(1)}, f32[2,64,1024]{2,1,0:T(8,128)}, u32[]{:S(2)}, u32[]{:S(2)}) collective-permute-start(f32[2,64,1024]{2,1,0:T(8,128)S(1)} %collective-permute-done.3.refs_2_.refs_3_), channel_id=1, source_target_pairs={{0,2},{1,31},{2,4},{3,1},{4,6},{5,3},{6,8},{7,5},{8,10},{9,7},{10,... | collective-permute-start | bytes 1572872 | tf_op jit(solution)/shard_map/ppermute | solution.py:200
  49.0 0.6 collective-permute-done.12.refs_9_.refs_12_
  49.6 5.0 %collective-permute-start.13 = (f32[2,64,1024]{2,1,0:T(8,128)S(1)}, f32[2,64,1024]{2,1,0:T(8,128)}, u32[]{:S(2)}, u32[]{:S(2)}) collective-permute-start(f32[2,64,1024]{2,1,0:T(8,128)S(1)} %collective-permute-done.12.refs_9_.refs_12_), channel_id=1, source_target_pairs={{0,2},{1,31},{2,4},{3,1},{4,6},{5,3},{6,8},{7,5},{8,10},{9,7},{10,... | collective-permute-start | bytes 1572872 | tf_op jit(solution)/shard_map/ppermute | solution.py:202
  54.6 4.8 %collective-permute-start.20 = (f32[2,64,1024]{2,1,0:T(8,128)}, f32[2,64,1024]{2,1,0:T(8,128)}, u32[]{:S(2)}, u32[]{:S(2)}) collective-permute-start(f32[2,64,1024]{2,1,0:T(8,128)} %bitcast.19), channel_id=1, source_target_pairs={{0,64},{1,257},{32,96},{33,289},{64,0},{65,321},{96,32},{97,353},{... | collective-permute-start | bytes 1572872 | tf_op jit(solution)/shard_map/ppermute | solution.py:203
  59.4 2.7 %collective-permute-start.21 = (f32[2,64,1024]{2,1,0:T(8,128)}, f32[2,64,1024]{2,1,0:T(8,128)}, u32[]{:S(2)}, u32[]{:S(2)}) collective-permute-start(f32[2,64,1024]{2,1,0:T(8,128)} %bitcast.20), channel_id=1, source_target_pairs={{0,96},{1,385},{32,0},{33,417},{64,32},{65,449},{96,64},{97,481},{... | collective-permute-start | bytes 1572872 | tf_op jit(solution)/shard_map/ppermute | solution.py:203
  62.1 2.6 %collective-permute-start.19 = (f32[2,64,1024]{2,1,0:T(8,128)}, f32[2,64,1024]{2,1,0:T(8,128)}, u32[]{:S(2)}, u32[]{:S(2)}) collective-permute-start(f32[2,64,1024]{2,1,0:T(8,128)} %bitcast.21), channel_id=1, source_target_pairs={{0,32},{1,129},{32,64},{33,161},{64,96},{65,193},{96,0},{97,225},{... | collective-permute-start | bytes 1572872 | tf_op jit(solution)/shard_map/ppermute | solution.py:203
  64.7 0.0 collective-permute-done.4.refs_3_.refs_4_
  64.7 1.9 %collective-permute-start.5 = (f32[2,64,1024]{2,1,0:T(8,128)}, f32[2,64,1024]{2,1,0:T(8,128)}, u32[]{:S(2)}, u32[]{:S(2)}) collective-permute-start(f32[2,64,1024]{2,1,0:T(8,128)} %collective-permute-done.4.refs_3_.refs_4_), channel_id=1, source_target_pairs={{0,2},{1,31},{2,4},{3,1},{4,6},{5,3},{6,8},{7,5},{8,10},{9,7},{10,... | collective-permute-start | bytes 1572872 | tf_op jit(solution)/shard_map/ppermute | solution.py:200
  66.7 0.0 collective-permute-done.13.refs_10_.refs_13_
  66.7 2.4 %collective-permute-start.14 = (f32[2,64,1024]{2,1,0:T(8,128)}, f32[2,64,1024]{2,1,0:T(8,128)}, u32[]{:S(2)}, u32[]{:S(2)}) collective-permute-start(f32[2,64,1024]{2,1,0:T(8,128)} %collective-permute-done.13.refs_10_.refs_13_), channel_id=1, source_target_pairs={{0,2},{1,31},{2,4},{3,1},{4,6},{5,3},{6,8},{7,5},{8,10},{9,7},{10,... | collective-permute-start | bytes 1572872 | tf_op jit(solution)/shard_map/ppermute | solution.py:202
  69.1 0.8 concatenate.3.info
  69.9 0.0 collective-permute-done.20
  69.9 2.4 %collective-permute-start = (s32[37]{0:T(128)S(1)}, s32[37]{0:T(128)S(1)}, u32[]{:S(2)}, u32[]{:S(2)}) collective-permute-start(s32[37]{0:T(128)S(1)} %concatenate.3.info), channel_id=1, source_target_pairs={{0,1},{1,0},{2,3},{3,2},{4,5},{5,4},{6,7},{7,6},{8,9},{9,8},{10,11... | collective-permute-start | bytes 452 | tf_op jit(solution)/shard_map/ppermute | solution.py:205
  72.3 0.4 collective-permute-done.21
  72.6 1.2 collective-permute-done.19
  73.9 1.7 %pad_maximum_fusion.u0.refs_19_ = f32[4,2,64,1024]{3,2,1,0:T(8,128)S(1)} fusion(f32[1,2,64,1024]{3,2,1,0:T(8,128)} %bitcast.11, f32[1,2,64,1024]{3,2,1,0:T(8,128)} %bitcast.10, f32[1,2,64,1024]{3,2,1,0:T(8,128)} %bitcast.9, f32[1,2,64,1024]{3,2,1,0:T(8,128)} %bitcast.22), kind=kLoop, calls=%fused_computation | loop fusion | flops 1572864 | bytes 4194304 | tf_op jit(solution)/shard_map/stack | solution.py:203
  75.5 3.1 %collective-permute-start.22 = (f32[4,2,64,1024]{3,2,1,0:T(8,128)S(1)}, f32[4,2,64,1024]{3,2,1,0:T(8,128)S(1)}, u32[]{:S(2)}, u32[]{:S(2)}) collective-permute-start(f32[4,2,64,1024]{3,2,1,0:T(8,128)S(1)} %pad_maximum_fusion.u0.refs_19_), channel_id=1, source_target_pairs={{0,128},{1,33},{32,160},{33,65},{64,192},{65,97},{96,224},{97,1},{... | collective-permute-start | bytes 6291464 | tf_op jit(solution)/shard_map/ppermute | solution.py:204
  78.7 4.4 %collective-permute-start.23 = (f32[4,2,64,1024]{3,2,1,0:T(8,128)S(1)}, f32[4,2,64,1024]{3,2,1,0:T(8,128)S(1)}, u32[]{:S(2)}, u32[]{:S(2)}) collective-permute-start(f32[4,2,64,1024]{3,2,1,0:T(8,128)S(1)} %pad_maximum_fusion.u0.refs_19_), channel_id=1, source_target_pairs={{0,256},{1,65},{32,288},{33,97},{64,320},{65,1},{96,352},{97,33},{... | collective-permute-start | bytes 6291464 | tf_op jit(solution)/shard_map/ppermute | solution.py:204
  83.0 0.0 collective-permute-done.other
  83.0 3.1 %collective-permute-start.24 = (f32[4,2,64,1024]{3,2,1,0:T(8,128)S(1)}, f32[4,2,64,1024]{3,2,1,0:T(8,128)S(1)}, u32[]{:S(2)}, u32[]{:S(2)}) collective-permute-start(f32[4,2,64,1024]{3,2,1,0:T(8,128)S(1)} %pad_maximum_fusion.u0.refs_19_), channel_id=1, source_target_pairs={{0,384},{1,97},{32,416},{33,1},{64,448},{65,33},{96,480},{97,65},{... | collective-permute-start | bytes 6291464 | tf_op jit(solution)/shard_map/ppermute | solution.py:204
  86.1 0.0 collective-permute-done.5.refs_4_.refs_5_
  86.1 1.9 %collective-permute-start.6 = (f32[2,64,1024]{2,1,0:T(8,128)}, f32[2,64,1024]{2,1,0:T(8,128)S(1)}, u32[]{:S(2)}, u32[]{:S(2)}) collective-permute-start(f32[2,64,1024]{2,1,0:T(8,128)} %collective-permute-done.5.refs_4_.refs_5_), channel_id=1, source_target_pairs={{0,2},{1,31},{2,4},{3,1},{4,6},{5,3},{6,8},{7,5},{8,10},{9,7},{10,... | collective-permute-start | bytes 1572872 | tf_op jit(solution)/shard_map/ppermute | solution.py:200
  88.0 0.0 collective-permute-done.14.refs_11_.refs_14_
  88.1 3.4 %collective-permute-start.15 = (f32[2,64,1024]{2,1,0:T(8,128)}, f32[2,64,1024]{2,1,0:T(8,128)S(1)}, u32[]{:S(2)}, u32[]{:S(2)}) collective-permute-start(f32[2,64,1024]{2,1,0:T(8,128)} %collective-permute-done.14.refs_11_.refs_14_), channel_id=1, source_target_pairs={{0,2},{1,31},{2,4},{3,1},{4,6},{5,3},{6,8},{7,5},{8,10},{9,7},{10,... | collective-permute-start | bytes 1572872 | tf_op jit(solution)/shard_map/ppermute | solution.py:202
  91.5 5.0 %collective-permute-done.6.refs_5_.refs_6_ = f32[2,64,1024]{2,1,0:T(8,128)S(1)} collective-permute-done((f32[2,64,1024]{2,1,0:T(8,128)}, f32[2,64,1024]{2,1,0:T(8,128)S(1)}, u32[]{:S(2)}, u32[]{:S(2)}) %collective-permute-start.6) | collective-permute-done | bytes 524320 | tf_op jit(solution)/shard_map/ppermute | solution.py:200
  96.5 3.1 %collective-permute-start.7 = (f32[2,64,1024]{2,1,0:T(8,128)S(1)}, f32[2,64,1024]{2,1,0:T(8,128)S(1)}, u32[]{:S(2)}, u32[]{:S(2)}) collective-permute-start(f32[2,64,1024]{2,1,0:T(8,128)S(1)} %collective-permute-done.6.refs_5_.refs_6_), channel_id=1, source_target_pairs={{0,2},{1,31},{2,4},{3,1},{4,6},{5,3},{6,8},{7,5},{8,10},{9,7},{10,... | collective-permute-start | bytes 1572872 | tf_op jit(solution)/shard_map/ppermute | solution.py:200
  99.7 2.5 %collective-permute-done.15.refs_12_.refs_15_ = f32[2,64,1024]{2,1,0:T(8,128)S(1)} collective-permute-done((f32[2,64,1024]{2,1,0:T(8,128)}, f32[2,64,1024]{2,1,0:T(8,128)S(1)}, u32[]{:S(2)}, u32[]{:S(2)}) %collective-permute-start.15) | collective-permute-done | bytes 524320 | tf_op jit(solution)/shard_map/ppermute | solution.py:202
  102.2 3.1 %collective-permute-start.16 = (f32[2,64,1024]{2,1,0:T(8,128)S(1)}, f32[2,64,1024]{2,1,0:T(8,128)S(1)}, u32[]{:S(2)}, u32[]{:S(2)}) collective-permute-start(f32[2,64,1024]{2,1,0:T(8,128)S(1)} %collective-permute-done.15.refs_12_.refs_15_), channel_id=1, source_target_pairs={{0,2},{1,31},{2,4},{3,1},{4,6},{5,3},{6,8},{7,5},{8,10},{9,7},{10,... | collective-permute-start | bytes 1572872 | tf_op jit(solution)/shard_map/ppermute | solution.py:202
  105.3 2.5 %collective-permute-done.7.refs_6_.refs_7_ = f32[2,64,1024]{2,1,0:T(8,128)S(1)} collective-permute-done((f32[2,64,1024]{2,1,0:T(8,128)S(1)}, f32[2,64,1024]{2,1,0:T(8,128)S(1)}, u32[]{:S(2)}, u32[]{:S(2)}) %collective-permute-start.7) | collective-permute-done | bytes 524320 | tf_op jit(solution)/shard_map/ppermute | solution.py:200
  107.8 5.6 %collective-permute-done.16.refs_13_.refs_16_ = f32[2,64,1024]{2,1,0:T(8,128)S(1)} collective-permute-done((f32[2,64,1024]{2,1,0:T(8,128)S(1)}, f32[2,64,1024]{2,1,0:T(8,128)S(1)}, u32[]{:S(2)}, u32[]{:S(2)}) %collective-permute-start.16) | collective-permute-done | bytes 524320 | tf_op jit(solution)/shard_map/ppermute | solution.py:202
  113.4 0.8 shard_map.77
  114.2 0.0 copy-start
  114.2 0.0 copy-start.1
  114.2 0.0 copy-start.3
  114.2 8.8 %collective-permute-start.17 = (f32[4,2,64,1024]{3,2,1,0:T(8,128)S(1)}, f32[4,2,64,1024]{3,2,1,0:T(8,128)S(1)}, u32[]{:S(2)}, u32[]{:S(2)}) collective-permute-start(f32[4,2,64,1024]{3,2,1,0:T(8,128)S(1)} %shard_map.77), channel_id=1, source_target_pairs={{0,1},{1,0},{2,3},{3,2},{4,5},{5,4},{6,7},{7,6},{8,9},{9,8},{10,11... | collective-permute-start | bytes 6291464 | tf_op jit(solution)/shard_map/ppermute | solution.py:211
  123.0 0.0 collective-permute-done.22.u1.refs_20_
  123.0 4.3 %collective-permute-done.23.u2.refs_21_ = f32[4,2,64,1024]{3,2,1,0:T(8,128)S(1)} collective-permute-done((f32[4,2,64,1024]{3,2,1,0:T(8,128)S(1)}, f32[4,2,64,1024]{3,2,1,0:T(8,128)S(1)}, u32[]{:S(2)}, u32[]{:S(2)}) %collective-permute-start.23) | collective-permute-done | bytes 2097184 | tf_op jit(solution)/shard_map/ppermute | solution.py:204
  127.3 1.6 collective-permute-done.24.u3.refs_22_
  128.8 0.7 shard_map.78
  129.5 4.7 %collective-permute-start.25 = (f32[2,2,64,1024]{3,2,1,0:T(8,128)S(1)}, f32[2,2,64,1024]{3,2,1,0:T(8,128)S(1)}, u32[]{:S(2)}, u32[]{:S(2)}) collective-permute-start(f32[2,2,64,1024]{3,2,1,0:T(8,128)S(1)} %shard_map.78), channel_id=1, source_target_pairs={{0,1},{1,0},{2,3},{3,2},{4,5},{5,4},{6,7},{7,6},{8,9},{9,8},{10,11... | collective-permute-start | bytes 3145736 | tf_op jit(solution)/shard_map/ppermute | solution.py:209
  134.2 4.9 %collective-permute-start.8 = (f32[2,64,1024]{2,1,0:T(8,128)S(1)}, f32[2,64,1024]{2,1,0:T(8,128)S(1)}, u32[]{:S(2)}, u32[]{:S(2)}) collective-permute-start(f32[2,64,1024]{2,1,0:T(8,128)S(1)} %collective-permute-done.7.refs_6_.refs_7_), channel_id=1, source_target_pairs={{0,2},{1,31},{2,4},{3,1},{4,6},{5,3},{6,8},{7,5},{8,10},{9,7},{10,... | collective-permute-start | bytes 1572872 | tf_op jit(solution)/shard_map/ppermute | solution.py:200
  139.1 6.1 %collective-permute-done.8.refs_8_ = f32[2,64,1024]{2,1,0:T(8,128)S(1)} collective-permute-done((f32[2,64,1024]{2,1,0:T(8,128)S(1)}, f32[2,64,1024]{2,1,0:T(8,128)S(1)}, u32[]{:S(2)}, u32[]{:S(2)}) %collective-permute-start.8) | collective-permute-done | bytes 524320 | tf_op jit(solution)/shard_map/ppermute | solution.py:200
  145.2 3.2 %collective-permute-start.18 = (f32[2,64,1024]{2,1,0:T(8,128)S(1)}, f32[2,64,1024]{2,1,0:T(8,128)S(1)}, u32[]{:S(2)}, u32[]{:S(2)}) collective-permute-start(f32[2,64,1024]{2,1,0:T(8,128)S(1)} %collective-permute-done.8.refs_8_), channel_id=1, source_target_pairs={{0,1},{1,0},{2,3},{3,2},{4,5},{5,4},{6,7},{7,6},{8,9},{9,8},{10,11... | collective-permute-start | bytes 1572872 | tf_op jit(solution)/shard_map/ppermute | solution.py:212
  148.4 0.0 collective-permute-done.25.refs_23_
  148.4 1.5 collective-permute-done.18.refs_18_
  149.9 0.0 collective-permute-done.17.refs_17_
  149.9 0.0 copy-done
  150.0 0.0 copy-done.1
  150.0 14.9 %shard_map.79 = (f32[64,1024]{1,0:T(8,128)}, f32[64,1024]{1,0:T(8,128)}) custom-call(s32[37]{0:T(128)S(1)} %concatenate.3.info, s32[37]{0:T(128)S(1)} %collective-permute-done.other, f32[2,64,1024]{2,1,0:T(8,128)S(1)} %bitcast.17, f32[2,64,1024]{2,1,0:T(8,128)S(1)} %collective-permute-done.1.refs_0_.refs_1_, ...), custom_call_target="tpu_custom_call" | custom-call | tf_op jit(solution)/shard_map/pallas_call | solution.py:219
  (1 shorter events, 0.0 us)
Async XLA Ops:
  0.6 14.5 %collective-permute-start.9 = (f32[2,64,1024]{2,1,0:T(8,128)}, f32[2,64,1024]{2,1,0:T(8,128)S(1)}, u32[]{:S(2)}, u32[]{:S(2)}) collective-permute-start(f32[2,64,1024]{2,1,0:T(8,128)} %bitcast.15), channel_id=1, source_target_pairs={{0,1},{1,0},{2,3},{3,2},{4,5},{5,4},{6,7},{7,6},{8,9},{9,8},{10,11... | collective-permute-start | bytes 1572872 | tf_op jit(solution)/shard_map/ppermute | solution.py:195
  9.4 12.2 %collective-permute-start.1 = (f32[2,64,1024]{2,1,0:T(8,128)}, f32[2,64,1024]{2,1,0:T(8,128)S(1)}, u32[]{:S(2)}, u32[]{:S(2)}) collective-permute-start(f32[2,64,1024]{2,1,0:T(8,128)} %bitcast.16), channel_id=1, source_target_pairs={{0,2},{1,31},{2,4},{3,1},{4,6},{5,3},{6,8},{7,5},{8,10},{9,7},{10,... | collective-permute-start | bytes 1572872 | tf_op jit(solution)/shard_map/ppermute | solution.py:200
  15.2 11.9 %collective-permute-start.10 = (f32[2,64,1024]{2,1,0:T(8,128)S(1)}, f32[2,64,1024]{2,1,0:T(8,128)S(1)}, u32[]{:S(2)}, u32[]{:S(2)}) collective-permute-start(f32[2,64,1024]{2,1,0:T(8,128)S(1)} %collective-permute-done.9.refs_9_), channel_id=1, source_target_pairs={{0,2},{1,31},{2,4},{3,1},{4,6},{5,3},{6,8},{7,5},{8,10},{9,7},{10,... | collective-permute-start | bytes 1572872 | tf_op jit(solution)/shard_map/ppermute | solution.py:202
  17.8 0.8 copy-start.2
  21.6 11.1 %collective-permute-start.2 = (f32[2,64,1024]{2,1,0:T(8,128)S(1)}, f32[2,64,1024]{2,1,0:T(8,128)S(1)}, u32[]{:S(2)}, u32[]{:S(2)}) collective-permute-start(f32[2,64,1024]{2,1,0:T(8,128)S(1)} %collective-permute-done.1.refs_0_.refs_1_), channel_id=1, source_target_pairs={{0,2},{1,31},{2,4},{3,1},{4,6},{5,3},{6,8},{7,5},{8,10},{9,7},{10,... | collective-permute-start | bytes 1572872 | tf_op jit(solution)/shard_map/ppermute | solution.py:200
  27.1 11.2 %collective-permute-start.11 = (f32[2,64,1024]{2,1,0:T(8,128)S(1)}, f32[2,64,1024]{2,1,0:T(8,128)S(1)}, u32[]{:S(2)}, u32[]{:S(2)}) collective-permute-start(f32[2,64,1024]{2,1,0:T(8,128)S(1)} %collective-permute-done.10.refs_7_.refs_10_), channel_id=1, source_target_pairs={{0,2},{1,31},{2,4},{3,1},{4,6},{5,3},{6,8},{7,5},{8,10},{9,7},{10,... | collective-permute-start | bytes 1572872 | tf_op jit(solution)/shard_map/ppermute | solution.py:202
  32.7 11.2 %collective-permute-start.3 = (f32[2,64,1024]{2,1,0:T(8,128)S(1)}, f32[2,64,1024]{2,1,0:T(8,128)S(1)}, u32[]{:S(2)}, u32[]{:S(2)}) collective-permute-start(f32[2,64,1024]{2,1,0:T(8,128)S(1)} %collective-permute-done.2.refs_1_.refs_2_), channel_id=1, source_target_pairs={{0,2},{1,31},{2,4},{3,1},{4,6},{5,3},{6,8},{7,5},{8,10},{9,7},{10,... | collective-permute-start | bytes 1572872 | tf_op jit(solution)/shard_map/ppermute | solution.py:200
  38.3 11.2 %collective-permute-start.12 = (f32[2,64,1024]{2,1,0:T(8,128)S(1)}, f32[2,64,1024]{2,1,0:T(8,128)S(1)}, u32[]{:S(2)}, u32[]{:S(2)}) collective-permute-start(f32[2,64,1024]{2,1,0:T(8,128)S(1)} %collective-permute-done.11.refs_8_.refs_11_), channel_id=1, source_target_pairs={{0,2},{1,31},{2,4},{3,1},{4,6},{5,3},{6,8},{7,5},{8,10},{9,7},{10,... | collective-permute-start | bytes 1572872 | tf_op jit(solution)/shard_map/ppermute | solution.py:202
  44.0 20.8 %collective-permute-start.4 = (f32[2,64,1024]{2,1,0:T(8,128)S(1)}, f32[2,64,1024]{2,1,0:T(8,128)}, u32[]{:S(2)}, u32[]{:S(2)}) collective-permute-start(f32[2,64,1024]{2,1,0:T(8,128)S(1)} %collective-permute-done.3.refs_2_.refs_3_), channel_id=1, source_target_pairs={{0,2},{1,31},{2,4},{3,1},{4,6},{5,3},{6,8},{7,5},{8,10},{9,7},{10,... | collective-permute-start | bytes 1572872 | tf_op jit(solution)/shard_map/ppermute | solution.py:200
  49.6 17.1 %collective-permute-start.13 = (f32[2,64,1024]{2,1,0:T(8,128)S(1)}, f32[2,64,1024]{2,1,0:T(8,128)}, u32[]{:S(2)}, u32[]{:S(2)}) collective-permute-start(f32[2,64,1024]{2,1,0:T(8,128)S(1)} %collective-permute-done.12.refs_9_.refs_12_), channel_id=1, source_target_pairs={{0,2},{1,31},{2,4},{3,1},{4,6},{5,3},{6,8},{7,5},{8,10},{9,7},{10,... | collective-permute-start | bytes 1572872 | tf_op jit(solution)/shard_map/ppermute | solution.py:202
  54.6 15.3 %collective-permute-start.20 = (f32[2,64,1024]{2,1,0:T(8,128)}, f32[2,64,1024]{2,1,0:T(8,128)}, u32[]{:S(2)}, u32[]{:S(2)}) collective-permute-start(f32[2,64,1024]{2,1,0:T(8,128)} %bitcast.19), channel_id=1, source_target_pairs={{0,64},{1,257},{32,96},{33,289},{64,0},{65,321},{96,32},{97,353},{... | collective-permute-start | bytes 1572872 | tf_op jit(solution)/shard_map/ppermute | solution.py:203
  59.4 13.2 %collective-permute-start.21 = (f32[2,64,1024]{2,1,0:T(8,128)}, f32[2,64,1024]{2,1,0:T(8,128)}, u32[]{:S(2)}, u32[]{:S(2)}) collective-permute-start(f32[2,64,1024]{2,1,0:T(8,128)} %bitcast.20), channel_id=1, source_target_pairs={{0,96},{1,385},{32,0},{33,417},{64,32},{65,449},{96,64},{97,481},{... | collective-permute-start | bytes 1572872 | tf_op jit(solution)/shard_map/ppermute | solution.py:203
  62.1 11.7 %collective-permute-start.19 = (f32[2,64,1024]{2,1,0:T(8,128)}, f32[2,64,1024]{2,1,0:T(8,128)}, u32[]{:S(2)}, u32[]{:S(2)}) collective-permute-start(f32[2,64,1024]{2,1,0:T(8,128)} %bitcast.21), channel_id=1, source_target_pairs={{0,32},{1,129},{32,64},{33,161},{64,96},{65,193},{96,0},{97,225},{... | collective-permute-start | bytes 1572872 | tf_op jit(solution)/shard_map/ppermute | solution.py:203
  64.7 21.4 %collective-permute-start.5 = (f32[2,64,1024]{2,1,0:T(8,128)}, f32[2,64,1024]{2,1,0:T(8,128)}, u32[]{:S(2)}, u32[]{:S(2)}) collective-permute-start(f32[2,64,1024]{2,1,0:T(8,128)} %collective-permute-done.4.refs_3_.refs_4_), channel_id=1, source_target_pairs={{0,2},{1,31},{2,4},{3,1},{4,6},{5,3},{6,8},{7,5},{8,10},{9,7},{10,... | collective-permute-start | bytes 1572872 | tf_op jit(solution)/shard_map/ppermute | solution.py:200
  66.7 21.4 %collective-permute-start.14 = (f32[2,64,1024]{2,1,0:T(8,128)}, f32[2,64,1024]{2,1,0:T(8,128)}, u32[]{:S(2)}, u32[]{:S(2)}) collective-permute-start(f32[2,64,1024]{2,1,0:T(8,128)} %collective-permute-done.13.refs_10_.refs_13_), channel_id=1, source_target_pairs={{0,2},{1,31},{2,4},{3,1},{4,6},{5,3},{6,8},{7,5},{8,10},{9,7},{10,... | collective-permute-start | bytes 1572872 | tf_op jit(solution)/shard_map/ppermute | solution.py:202
  69.9 13.1 %collective-permute-start = (s32[37]{0:T(128)S(1)}, s32[37]{0:T(128)S(1)}, u32[]{:S(2)}, u32[]{:S(2)}) collective-permute-start(s32[37]{0:T(128)S(1)} %concatenate.3.info), channel_id=1, source_target_pairs={{0,1},{1,0},{2,3},{3,2},{4,5},{5,4},{6,7},{7,6},{8,9},{9,8},{10,11... | collective-permute-start | bytes 452 | tf_op jit(solution)/shard_map/ppermute | solution.py:205
  75.5 47.5 %collective-permute-start.22 = (f32[4,2,64,1024]{3,2,1,0:T(8,128)S(1)}, f32[4,2,64,1024]{3,2,1,0:T(8,128)S(1)}, u32[]{:S(2)}, u32[]{:S(2)}) collective-permute-start(f32[4,2,64,1024]{3,2,1,0:T(8,128)S(1)} %pad_maximum_fusion.u0.refs_19_), channel_id=1, source_target_pairs={{0,128},{1,33},{32,160},{33,65},{64,192},{65,97},{96,224},{97,1},{... | collective-permute-start | bytes 6291464 | tf_op jit(solution)/shard_map/ppermute | solution.py:204
  78.7 48.6 %collective-permute-start.23 = (f32[4,2,64,1024]{3,2,1,0:T(8,128)S(1)}, f32[4,2,64,1024]{3,2,1,0:T(8,128)S(1)}, u32[]{:S(2)}, u32[]{:S(2)}) collective-permute-start(f32[4,2,64,1024]{3,2,1,0:T(8,128)S(1)} %pad_maximum_fusion.u0.refs_19_), channel_id=1, source_target_pairs={{0,256},{1,65},{32,288},{33,97},{64,320},{65,1},{96,352},{97,33},{... | collective-permute-start | bytes 6291464 | tf_op jit(solution)/shard_map/ppermute | solution.py:204
  83.0 45.8 %collective-permute-start.24 = (f32[4,2,64,1024]{3,2,1,0:T(8,128)S(1)}, f32[4,2,64,1024]{3,2,1,0:T(8,128)S(1)}, u32[]{:S(2)}, u32[]{:S(2)}) collective-permute-start(f32[4,2,64,1024]{3,2,1,0:T(8,128)S(1)} %pad_maximum_fusion.u0.refs_19_), channel_id=1, source_target_pairs={{0,384},{1,97},{32,416},{33,1},{64,448},{65,33},{96,480},{97,65},{... | collective-permute-start | bytes 6291464 | tf_op jit(solution)/shard_map/ppermute | solution.py:204
  86.1 10.4 %collective-permute-start.6 = (f32[2,64,1024]{2,1,0:T(8,128)}, f32[2,64,1024]{2,1,0:T(8,128)S(1)}, u32[]{:S(2)}, u32[]{:S(2)}) collective-permute-start(f32[2,64,1024]{2,1,0:T(8,128)} %collective-permute-done.5.refs_4_.refs_5_), channel_id=1, source_target_pairs={{0,2},{1,31},{2,4},{3,1},{4,6},{5,3},{6,8},{7,5},{8,10},{9,7},{10,... | collective-permute-start | bytes 1572872 | tf_op jit(solution)/shard_map/ppermute | solution.py:200
  88.1 14.1 %collective-permute-start.15 = (f32[2,64,1024]{2,1,0:T(8,128)}, f32[2,64,1024]{2,1,0:T(8,128)S(1)}, u32[]{:S(2)}, u32[]{:S(2)}) collective-permute-start(f32[2,64,1024]{2,1,0:T(8,128)} %collective-permute-done.14.refs_11_.refs_14_), channel_id=1, source_target_pairs={{0,2},{1,31},{2,4},{3,1},{4,6},{5,3},{6,8},{7,5},{8,10},{9,7},{10,... | collective-permute-start | bytes 1572872 | tf_op jit(solution)/shard_map/ppermute | solution.py:202
  96.5 11.2 %collective-permute-start.7 = (f32[2,64,1024]{2,1,0:T(8,128)S(1)}, f32[2,64,1024]{2,1,0:T(8,128)S(1)}, u32[]{:S(2)}, u32[]{:S(2)}) collective-permute-start(f32[2,64,1024]{2,1,0:T(8,128)S(1)} %collective-permute-done.6.refs_5_.refs_6_), channel_id=1, source_target_pairs={{0,2},{1,31},{2,4},{3,1},{4,6},{5,3},{6,8},{7,5},{8,10},{9,7},{10,... | collective-permute-start | bytes 1572872 | tf_op jit(solution)/shard_map/ppermute | solution.py:200
  102.2 11.2 %collective-permute-start.16 = (f32[2,64,1024]{2,1,0:T(8,128)S(1)}, f32[2,64,1024]{2,1,0:T(8,128)S(1)}, u32[]{:S(2)}, u32[]{:S(2)}) collective-permute-start(f32[2,64,1024]{2,1,0:T(8,128)S(1)} %collective-permute-done.15.refs_12_.refs_15_), channel_id=1, source_target_pairs={{0,2},{1,31},{2,4},{3,1},{4,6},{5,3},{6,8},{7,5},{8,10},{9,7},{10,... | collective-permute-start | bytes 1572872 | tf_op jit(solution)/shard_map/ppermute | solution.py:202
  114.2 35.7 %copy-start = (f32[1,1,1,2,64,1024]{5,4,3,2,1,0:T(8,128)S(1)}, f32[1,1,1,2,64,1024]{5,4,3,2,1,0:T(8,128)}, u32[]{:S(2)}) copy-start(f32[1,1,1,2,64,1024]{5,4,3,2,1,0:T(8,128)} %param.6) | copy-start | bytes 1572868
  114.2 35.7 %copy-start.1 = (f32[1,1,2,64,1024]{4,3,2,1,0:T(8,128)S(1)}, f32[1,1,2,64,1024]{4,3,2,1,0:T(8,128)}, u32[]{:S(2)}) copy-start(f32[1,1,2,64,1024]{4,3,2,1,0:T(8,128)} %param.11) | copy-start | bytes 1572868
  114.2 35.7 %copy-start.3 = (f32[2,64,1024]{2,1,0:T(8,128)S(1)}, f32[2,64,1024]{2,1,0:T(8,128)}, u32[]{:S(2)}) copy-start(f32[2,64,1024]{2,1,0:T(8,128)} %copy-done.2) | copy-start | bytes 1572868
  114.2 35.7 %collective-permute-start.17 = (f32[4,2,64,1024]{3,2,1,0:T(8,128)S(1)}, f32[4,2,64,1024]{3,2,1,0:T(8,128)S(1)}, u32[]{:S(2)}, u32[]{:S(2)}) collective-permute-start(f32[4,2,64,1024]{3,2,1,0:T(8,128)S(1)} %shard_map.77), channel_id=1, source_target_pairs={{0,1},{1,0},{2,3},{3,2},{4,5},{5,4},{6,7},{7,6},{8,9},{9,8},{10,11... | collective-permute-start | bytes 6291464 | tf_op jit(solution)/shard_map/ppermute | solution.py:211
  129.5 18.9 %collective-permute-start.25 = (f32[2,2,64,1024]{3,2,1,0:T(8,128)S(1)}, f32[2,2,64,1024]{3,2,1,0:T(8,128)S(1)}, u32[]{:S(2)}, u32[]{:S(2)}) collective-permute-start(f32[2,2,64,1024]{3,2,1,0:T(8,128)S(1)} %shard_map.78), channel_id=1, source_target_pairs={{0,1},{1,0},{2,3},{3,2},{4,5},{5,4},{6,7},{7,6},{8,9},{9,8},{10,11... | collective-permute-start | bytes 3145736 | tf_op jit(solution)/shard_map/ppermute | solution.py:209
  134.2 11.0 %collective-permute-start.8 = (f32[2,64,1024]{2,1,0:T(8,128)S(1)}, f32[2,64,1024]{2,1,0:T(8,128)S(1)}, u32[]{:S(2)}, u32[]{:S(2)}) collective-permute-start(f32[2,64,1024]{2,1,0:T(8,128)S(1)} %collective-permute-done.7.refs_6_.refs_7_), channel_id=1, source_target_pairs={{0,2},{1,31},{2,4},{3,1},{4,6},{5,3},{6,8},{7,5},{8,10},{9,7},{10,... | collective-permute-start | bytes 1572872 | tf_op jit(solution)/shard_map/ppermute | solution.py:200
  145.2 4.8 %collective-permute-start.18 = (f32[2,64,1024]{2,1,0:T(8,128)S(1)}, f32[2,64,1024]{2,1,0:T(8,128)S(1)}, u32[]{:S(2)}, u32[]{:S(2)}) collective-permute-start(f32[2,64,1024]{2,1,0:T(8,128)S(1)} %collective-permute-done.8.refs_8_), channel_id=1, source_target_pairs={{0,1},{1,0},{2,3},{3,2},{4,5},{5,4},{6,7},{7,6},{8,9},{9,8},{10,11... | collective-permute-start | bytes 1572872 | tf_op jit(solution)/shard_map/ppermute | solution.py:212

commit v2 on v1

--- a/solution.py
+++ b/solution.py
@@ -93,93 +93,119 @@
     lane_id = lax.broadcasted_iota(jnp.int32, (n, n), 1)
     eye = jnp.where(row_id == lane_id, jnp.float32(1), jnp.float32(0))
     work = jnp.concatenate([gram, eye], axis=1)
-    blocks = [work[8 * i : 8 * i + 8] for i in range(n // 8)]
-    sub = lax.broadcasted_iota(jnp.int32, (8, 2 * n), 0)
-    for k in range(n):
-        at, within = divmod(k, 8)
-        row = blocks[at][within : within + 1]
-        scale = lax.rsqrt(row[:, k : k + 1])
-        row = row * scale
-        for i in range(at, n // 8):
-            change = (blocks[i][:, k : k + 1] * scale) * row
-            if i == at:
-                blocks[i] = jnp.where(sub > within, blocks[i] - change, jnp.where(sub == within, row, blocks[i]))
-            else:
-                blocks[i] = blocks[i] - change
+    tall, wide = 8, 2 * n
+    blocks = [work[tall * i : tall * i + tall] for i in range(n // tall)]
+    sub = lax.broadcasted_iota(jnp.int32, (tall, wide), 0)
+    spread = lambda x: jnp.broadcast_to(x, (tall, wide))
+    for at in range(n // tall):
+        below = n // tall - at
+        columns = [[spread(blocks[at + i][:, tall * at + j : tall * at + j + 1]) for i in range(below)] for j in range(tall)]
+        rows, scales, block = [], [], blocks[at]
+        for w in range(tall):
+            scale = lax.rsqrt(spread(columns[w][0][w : w + 1]))
+            inverse = scale * scale
+            row = spread(block[w : w + 1]) * inverse
+            block = jnp.where(sub > w, block - columns[w][0] * row, block)
+            rows.append(row)
+            scales.append(scale)
+            for j in range(w + 1, tall):
+                part = spread(columns[j][0][w : w + 1]) * inverse
+                for i in range(below):
+                    new = columns[j][i] - columns[w][i] * part
+                    columns[j][i] = new if i else jnp.where(sub > w, new, columns[j][i])
+        scale = scales[-1]
+        for w in range(tall - 1):
+            scale = jnp.where(sub == w, scales[w], scale)
+        blocks[at] = block * scale
+        for i in range(1, below):
+            for w in range(tall):
+                blocks[at + i] = blocks[at + i] - columns[w][i] * rows[w]
     return jnp.concatenate(blocks, axis=0)[:, n:]
 
 
-def tile_kernel(info, other, *refs):
-    own, across = refs[:9], refs[9:17]
-    left_in, last_in = refs[17:19]
-    ups, up_in, sketch = refs[19:23], refs[23], refs[24]
-    basis_out, weights_out = refs[25:27]
-    xs, ys, ps, qs, ws, left_sems, up_sems, sketch_sem = refs[27:]
+def up_kernel(info, u0, u1, u2, u3, up_in, sketch, ps, qs, tested, ws, up_sems, sketch_sem):
+    ups = (u0, u1, u2, u3)
     depth = info[DEPTH_AT]
-    tile = info[TARGET_AT + depth]
-    b, j = tile // CB, tile % CB
+    j = info[TARGET_AT + depth] % CB
     n, size = ws.shape
-
-    def left_copies(source, slot):
-        return (
-            pltpu.make_async_copy(source.at[0], xs.at[slot], left_sems.at[slot, 0]),
-            pltpu.make_async_copy(source.at[1], ys.at[slot], left_sems.at[slot, 1]),
-        )
-
-    def up_copies(source, slot):
+    slots = 2 * KD
+
+    def copies(source, slot):
         return (
             pltpu.make_async_copy(source.at[0], ps.at[slot], up_sems.at[slot, 0]),
             pltpu.make_async_copy(source.at[1], qs.at[slot], up_sems.at[slot, 1]),
         )
 
-    def start(condition, copies):
+    pltpu.make_async_copy(sketch.at[depth], ws, sketch_sem).start()
+    for k in range(KD):
+        t, s = up_place(info, info[UP_AT + j * KD + k])
+        for i in range(SIDE):
+
+            @pl.when(t == i)
+            def _():
+                for copy in copies(ups[i].at[s], k):
+                    copy.start()
+
+        for copy in copies(up_in.at[k], KD + k):
+            copy.start()
+    pltpu.make_async_copy(sketch.at[0], ws, sketch_sem).wait()
+    for slot in range(slots):
+        for copy in copies(up_in.at[0], slot):
+            copy.wait()
+    tested[...] = dot(ws[...], qs[...].reshape(slots * n, size), (1, 1))
+
+
+def tile_kernel(info, other, *refs):
+    own, across = refs[:9], refs[9:17]
+    left_in, last_in, ps, qs, tested = refs[17:22]
+    basis_out, weights_out = refs[22:24]
+    xs, ys, left_sems = refs[24:]
+    b = info[TARGET_AT + info[DEPTH_AT]] // CB
+    slots, n, size = xs.shape
+
+    def copies(source, slot):
+        return (
+            pltpu.make_async_copy(source.at[1], ys.at[slot], left_sems.at[slot, 1]),
+            pltpu.make_async_copy(source.at[0], xs.at[slot], left_sems.at[slot, 0]),
+        )
+
+    def start(condition, source, slot):
         @pl.when(condition)
         def _():
-            for copy in copies:
+            for copy in copies(source, slot):
                 copy.start()
 
-    pltpu.make_async_copy(sketch.at[depth], ws, sketch_sem).start()
     for kind, (table, pieces) in enumerate(((info, own), (other, across))):
         for k in range(KD):
             slot = kind * KD + k
             s = ring_steps(info, table[b * KD + k])
             for i, piece in enumerate(pieces):
-                start(s == i, left_copies(piece, slot))
+                start(s == i, piece, slot)
             if kind == 1:
-                start(s == 8, left_copies(last_in, slot))
-            start(s > 8, left_copies(left_in.at[slot], slot))
-            if kind == 0:
-                t, s = up_place(info, table[UP_AT + j * KD + k])
-                for i in range(SIDE):
-                    start(t == i, up_copies(ups[i].at[s], slot))
-            else:
-                for copy in up_copies(up_in.at[k], slot):
-                    copy.start()
-    pltpu.make_async_copy(sketch.at[0], ws, sketch_sem).wait()
-    slots = 2 * KD
+                start(s == 8, last_in, slot)
+            start(s > 8, left_in.at[slot], slot)
     for slot in range(slots):
-        for copy in (*up_copies(up_in.at[0], slot), *left_copies(own[0], slot)):
+        for copy in copies(own[0], slot):
             copy.wait()
     x_all = xs[...].reshape(slots * n, size)
     q_all = qs[...].reshape(slots * n, size)
-    tested = dot(ws[...], q_all, (1, 1))
     middles = [dot(ys[i], ps[i], (1, 1)) for i in range(slots)]
     folded = jnp.concatenate([dot(tested[:, i * n : i * n + n], middles[i], (1, 1)) for i in range(slots)], axis=1)
     sample = dot(folded, x_all, (1, 0))
+    inner = dot(sample, x_all, (1, 1))
+    turned = jnp.concatenate([dot(inner[:, i * n : i * n + n], middles[i], (1, 0)) for i in range(slots)], axis=1)
+    project = dot(turned, q_all, (1, 0))
     inverse = inverse_factor(dot(sample, sample, (1, 1)))
-    bases = dot(inverse, sample, (1, 0))
     root = math.sqrt(size)
-    basis_out[...] = bases * root
-    inner = dot(bases, x_all, (1, 1))
-    turned = jnp.concatenate([dot(inner[:, i * n : i * n + n], middles[i], (1, 0)) for i in range(slots)], axis=1)
-    weights_out[...] = dot(turned, q_all, (1, 0)) * (1 / root)
-
-
-def local_kernel(kernel, n_scalar, n_any, out_shape, out_space, scratch, mebibytes=1):
+    basis_out[...] = dot(inverse * root, sample, (1, 0))
+    weights_out[...] = dot(inverse * (1 / root), project, (1, 0))
+
+
+def local_kernel(kernel, in_spaces, out_shape, out_space, scratch, mebibytes=1):
     return pl.pallas_call(
         kernel,
         out_shape=out_shape,
-        in_specs=[pl.BlockSpec(memory_space=pltpu.SMEM)] * n_scalar + [pl.BlockSpec(memory_space=pltpu.HBM)] * n_any,
+        in_specs=[pl.BlockSpec(memory_space=space) for space in in_spaces],
         out_specs=jax.tree.map(lambda _: pl.BlockSpec(memory_space=out_space), out_shape),
         scratch_shapes=scratch,
         compiler_params=pltpu.CompilerParams(vmem_limit_bytes=mebibytes << 20),
@@ -204,19 +230,29 @@
     ups = [block] + [lax.ppermute(block, ("row", "depth"), xy_shift(s, 1)) for s in range(1, SIDE)]
     other = lax.ppermute(info, "depth", SWAP)
 
+    early = lambda pieces: [pltpu.with_memory_space_constraint(x, pltpu.HBM) for x in pieces[:7]] + pieces[7:]
+    own_held, across_held = early(own_pieces), early(across_pieces)
     f32 = jnp.float32
-    up_choice = local_kernel(up_choice_kernel, 1, SIDE, jax.ShapeDtypeStruct((KD, *pair), f32), pltpu.HBM, [pltpu.SemaphoreType.DMA((KD,))])
+    smem, hbm, vmem = pltpu.SMEM, pltpu.HBM, pltpu.VMEM
+    slots = 2 * KD
+    dma = pltpu.SemaphoreType.DMA
+    choice = jax.ShapeDtypeStruct((KD, *pair), f32)
+    up_choice = local_kernel(up_choice_kernel, [smem] + [hbm] * SIDE, choice, hbm, [dma((KD,))])
     up_in = lax.ppermute(up_choice(info, *ups), "depth", SWAP)
-    left_choice = local_kernel(left_choice_kernel, 2, 14, jax.ShapeDtypeStruct((2 * KD, *pair), f32), pltpu.HBM, [pltpu.SemaphoreType.DMA((2 * KD,))])
-    left_in = lax.ppermute(left_choice(info, other, *own_pieces[1:8], *across_pieces[1:8]), "depth", SWAP)
+    choice = jax.ShapeDtypeStruct((slots, *pair), f32)
+    left_choice = local_kernel(left_choice_kernel, [smem] * 2 + [hbm] * 14, choice, hbm, [dma((slots,))])
+    left_in = lax.ppermute(left_choice(info, other, *own_held[1:8], *across_held[1:8]), "depth", SWAP)
     last_in = lax.ppermute(own_pieces[8], "depth", SWAP)
 
     flat = pair[1:]
-    tile = jax.ShapeDtypeStruct(flat, f32)
-    stack = pltpu.VMEM((2 * KD, *flat), f32)
-    sems = pltpu.SemaphoreType.DMA((2 * KD, 2))
-    whole = local_kernel(tile_kernel, 2, 25, (tile, tile), pltpu.VMEM, [stack] * 4 + [pltpu.VMEM(flat, f32), sems, sems, pltpu.SemaphoreType.DMA], 12)
-    basis, weights = whole(info, other, *own_pieces, *across_pieces, left_in, last_in, *ups, up_in, test)
+    tile, stack = jax.ShapeDtypeStruct(flat, f32), jax.ShapeDtypeStruct((slots, *flat), f32)
+    square = jax.ShapeDtypeStruct((flat[0], slots * flat[0]), f32)
+    scratch = [vmem(flat, f32), dma((slots, 2)), dma]
+    up_part = local_kernel(up_kernel, [smem] + [hbm] * (SIDE + 2), (stack, stack, square), vmem, scratch, 6)
+    up_sides = up_part(info, *ups, up_in, test)
+    scratch = [vmem(stack.shape, f32)] * 2 + [dma((slots, 2))]
+    whole = local_kernel(tile_kernel, [smem] * 2 + [hbm] * 19 + [vmem] * 3, (tile, tile), vmem, scratch, 12)
+    basis, weights = whole(info, other, *own_held, *across_held, left_in, last_in, *up_sides)
     return basis[None, None, None], weights[None, None, None]
 
 

time: 166 us -> 162 us (0.976)
  starting transfers between devices: 108 us -> 106 us
    ppermute x1, starting transfers between devices: 8.75 us -> 6.77 us  [pieces_and_tile(): lax.ppermute(left_choice(info, other, *own_held[1:8], *across_held[1:8]),...]
    pallas_call x2 -> x3, Pallas kernels: 15.7 us -> 15.4 us  [the longest x1 10.8 us: pieces_and_tile(): whole(info, other, *own_held, *across_held, left_in, last_in, *up_sides)]
  transfers between devices with their start and end apart: 26 -> 26, of which waited for: 16 -> 15; matrix products, arithmetic and copies ran while one was open for 1% -> 1% of each run, Pallas kernels for 1% -> 3%
where the time goes in v2:
time: 162 us; the launch traced here: 161 us
  starting transfers between devices  106 us (65%)
  waiting for transfers between devices  36 us (22%)
  Pallas kernels  16.1 us (10%)
  other arithmetic  1.65 us (1%)
    ppermute x8, starting transfers between devices, pieces_and_tile(): own_pieces.append(lax.ppermute(own_pieces[-1], ('col', 'depth'), shift))  32.5 us
    ppermute x7, starting transfers between devices, pieces_and_tile(): lax.ppermute(across_pieces[-1], ('col', 'depth'), shift)  26.7 us
    ppermute x8, waiting for transfers between devices, pieces_and_tile(): own_pieces.append(lax.ppermute(own_pieces[-1], ('col', 'depth'), shift))  18.6 us
    pallas_call x1, Pallas kernels, pieces_and_tile(): whole(info, other, *own_held, *across_held, left_in, last_in, *up_sides)  10.8 us
    ppermute x3, starting transfers between devices, pieces_and_tile(): lax.ppermute(block, ('row', 'depth'), xy_shift(s, 1))  10.5 us
    ppermute x3, starting transfers between devices, pieces_and_tile(): lax.ppermute(up, ('row', 'depth'), xy_shift(s, 0))  10.1 us
    ppermute x7, waiting for transfers between devices, pieces_and_tile(): lax.ppermute(across_pieces[-1], ('col', 'depth'), shift)  9.89 us
    ppermute x1, starting transfers between devices, pieces_and_tile(): across = lax.ppermute(own, 'depth', SWAP)  8.75 us
  transfers between devices with their start and end apart: 26, of which 15 were waited for; matrix products, arithmetic and copies ran while one was open for 1% of the time, Pallas kernels for 3%

profile of v2, /device:TPU:1, one launch (start us, length us, event | category | flops | bytes accessed | tf_op | source)
XLA Modules:
  0.0 161.3 jit_solution(9203631688574431762)
XLA Ops:
  0.6 8.7 %collective-permute-start.9 = (f32[2,64,1024]{2,1,0:T(8,128)}, f32[2,64,1024]{2,1,0:T(8,128)S(1)}, u32[]{:S(2)}, u32[]{:S(2)}) collective-permute-start(f32[2,64,1024]{2,1,0:T(8,128)} %bitcast.16), channel_id=1, source_target_pairs={{0,1},{1,0},{2,3},{3,2},{4,5},{5,4},{6,7},{7,6},{8,9},{9,8},{10,11... | collective-permute-start | bytes 1572872 | tf_op jit(solution)/shard_map/ppermute | solution.py:221
  9.4 5.8 %collective-permute-start.1 = (f32[2,64,1024]{2,1,0:T(8,128)}, f32[2,64,1024]{2,1,0:T(8,128)S(1)}, u32[]{:S(2)}, u32[]{:S(2)}) collective-permute-start(f32[2,64,1024]{2,1,0:T(8,128)} %bitcast.17), channel_id=1, source_target_pairs={{0,2},{1,31},{2,4},{3,1},{4,6},{5,3},{6,8},{7,5},{8,10},{9,7},{10,... | collective-permute-start | bytes 1572872 | tf_op jit(solution)/shard_map/ppermute | solution.py:226
  15.2 0.0 collective-permute-done.9.refs_9_
  15.2 0.0 copy-start.9
  15.2 2.6 %collective-permute-start.10 = (f32[2,64,1024]{2,1,0:T(8,128)S(1)}, f32[2,64,1024]{2,1,0:T(8,128)S(1)}, u32[]{:S(2)}, u32[]{:S(2)}) collective-permute-start(f32[2,64,1024]{2,1,0:T(8,128)S(1)} %collective-permute-done.9.refs_9_), channel_id=1, source_target_pairs={{0,2},{1,31},{2,4},{3,1},{4,6},{5,3},{6,8},{7,5},{8,10},{9,7},{10,... | collective-permute-start | bytes 1572872 | tf_op jit(solution)/shard_map/ppermute | solution.py:228
  17.8 3.8 %collective-permute-done.1.refs_0_.refs_1_ = f32[2,64,1024]{2,1,0:T(8,128)S(1)} collective-permute-done((f32[2,64,1024]{2,1,0:T(8,128)}, f32[2,64,1024]{2,1,0:T(8,128)S(1)}, u32[]{:S(2)}, u32[]{:S(2)}) %collective-permute-start.1) | collective-permute-done | bytes 524320 | tf_op jit(solution)/shard_map/ppermute | solution.py:226
  21.6 4.9 %collective-permute-start.2 = (f32[2,64,1024]{2,1,0:T(8,128)S(1)}, f32[2,64,1024]{2,1,0:T(8,128)S(1)}, u32[]{:S(2)}, u32[]{:S(2)}) collective-permute-start(f32[2,64,1024]{2,1,0:T(8,128)S(1)} %collective-permute-done.1.refs_0_.refs_1_), channel_id=1, source_target_pairs={{0,2},{1,31},{2,4},{3,1},{4,6},{5,3},{6,8},{7,5},{8,10},{9,7},{10,... | collective-permute-start | bytes 1572872 | tf_op jit(solution)/shard_map/ppermute | solution.py:226
  26.5 0.6 collective-permute-done.10.refs_7_.refs_10_
  27.1 5.0 %collective-permute-start.11 = (f32[2,64,1024]{2,1,0:T(8,128)S(1)}, f32[2,64,1024]{2,1,0:T(8,128)S(1)}, u32[]{:S(2)}, u32[]{:S(2)}) collective-permute-start(f32[2,64,1024]{2,1,0:T(8,128)S(1)} %collective-permute-done.10.refs_7_.refs_10_), channel_id=1, source_target_pairs={{0,2},{1,31},{2,4},{3,1},{4,6},{5,3},{6,8},{7,5},{8,10},{9,7},{10,... | collective-permute-start | bytes 1572872 | tf_op jit(solution)/shard_map/ppermute | solution.py:228
  32.1 0.6 collective-permute-done.2.refs_1_.refs_2_
  32.7 5.0 %collective-permute-start.3 = (f32[2,64,1024]{2,1,0:T(8,128)S(1)}, f32[2,64,1024]{2,1,0:T(8,128)S(1)}, u32[]{:S(2)}, u32[]{:S(2)}) collective-permute-start(f32[2,64,1024]{2,1,0:T(8,128)S(1)} %collective-permute-done.2.refs_1_.refs_2_), channel_id=1, source_target_pairs={{0,2},{1,31},{2,4},{3,1},{4,6},{5,3},{6,8},{7,5},{8,10},{9,7},{10,... | collective-permute-start | bytes 1572872 | tf_op jit(solution)/shard_map/ppermute | solution.py:226
  37.7 0.6 collective-permute-done.11.refs_8_.refs_11_
  38.3 5.0 %collective-permute-start.12 = (f32[2,64,1024]{2,1,0:T(8,128)S(1)}, f32[2,64,1024]{2,1,0:T(8,128)S(1)}, u32[]{:S(2)}, u32[]{:S(2)}) collective-permute-start(f32[2,64,1024]{2,1,0:T(8,128)S(1)} %collective-permute-done.11.refs_8_.refs_11_), channel_id=1, source_target_pairs={{0,2},{1,31},{2,4},{3,1},{4,6},{5,3},{6,8},{7,5},{8,10},{9,7},{10,... | collective-permute-start | bytes 1572872 | tf_op jit(solution)/shard_map/ppermute | solution.py:228
  43.4 0.6 collective-permute-done.3.refs_2_.refs_3_
  44.0 5.0 %collective-permute-start.4 = (f32[2,64,1024]{2,1,0:T(8,128)S(1)}, f32[2,64,1024]{2,1,0:T(8,128)}, u32[]{:S(2)}, u32[]{:S(2)}) collective-permute-start(f32[2,64,1024]{2,1,0:T(8,128)S(1)} %collective-permute-done.3.refs_2_.refs_3_), channel_id=1, source_target_pairs={{0,2},{1,31},{2,4},{3,1},{4,6},{5,3},{6,8},{7,5},{8,10},{9,7},{10,... | collective-permute-start | bytes 1572872 | tf_op jit(solution)/shard_map/ppermute | solution.py:226
  49.0 0.6 collective-permute-done.12.refs_9_.refs_12_
  49.6 5.0 %collective-permute-start.13 = (f32[2,64,1024]{2,1,0:T(8,128)S(1)}, f32[2,64,1024]{2,1,0:T(8,128)}, u32[]{:S(2)}, u32[]{:S(2)}) collective-permute-start(f32[2,64,1024]{2,1,0:T(8,128)S(1)} %collective-permute-done.12.refs_9_.refs_12_), channel_id=1, source_target_pairs={{0,2},{1,31},{2,4},{3,1},{4,6},{5,3},{6,8},{7,5},{8,10},{9,7},{10,... | collective-permute-start | bytes 1572872 | tf_op jit(solution)/shard_map/ppermute | solution.py:228
  54.6 4.8 %collective-permute-start.20 = (f32[2,64,1024]{2,1,0:T(8,128)}, f32[2,64,1024]{2,1,0:T(8,128)}, u32[]{:S(2)}, u32[]{:S(2)}) collective-permute-start(f32[2,64,1024]{2,1,0:T(8,128)} %bitcast.19), channel_id=1, source_target_pairs={{0,64},{1,257},{32,96},{33,289},{64,0},{65,321},{96,32},{97,353},{... | collective-permute-start | bytes 1572872 | tf_op jit(solution)/shard_map/ppermute | solution.py:229
  59.4 2.7 %collective-permute-start.21 = (f32[2,64,1024]{2,1,0:T(8,128)}, f32[2,64,1024]{2,1,0:T(8,128)}, u32[]{:S(2)}, u32[]{:S(2)}) collective-permute-start(f32[2,64,1024]{2,1,0:T(8,128)} %bitcast.20), channel_id=1, source_target_pairs={{0,96},{1,385},{32,0},{33,417},{64,32},{65,449},{96,64},{97,481},{... | collective-permute-start | bytes 1572872 | tf_op jit(solution)/shard_map/ppermute | solution.py:229
  62.1 2.6 %collective-permute-start.19 = (f32[2,64,1024]{2,1,0:T(8,128)}, f32[2,64,1024]{2,1,0:T(8,128)}, u32[]{:S(2)}, u32[]{:S(2)}) collective-permute-start(f32[2,64,1024]{2,1,0:T(8,128)} %bitcast.21), channel_id=1, source_target_pairs={{0,32},{1,129},{32,64},{33,161},{64,96},{65,193},{96,0},{97,225},{... | collective-permute-start | bytes 1572872 | tf_op jit(solution)/shard_map/ppermute | solution.py:229
  64.7 0.0 collective-permute-done.4.refs_3_.refs_4_
  64.8 1.9 %collective-permute-start.5 = (f32[2,64,1024]{2,1,0:T(8,128)}, f32[2,64,1024]{2,1,0:T(8,128)}, u32[]{:S(2)}, u32[]{:S(2)}) collective-permute-start(f32[2,64,1024]{2,1,0:T(8,128)} %collective-permute-done.4.refs_3_.refs_4_), channel_id=1, source_target_pairs={{0,2},{1,31},{2,4},{3,1},{4,6},{5,3},{6,8},{7,5},{8,10},{9,7},{10,... | collective-permute-start | bytes 1572872 | tf_op jit(solution)/shard_map/ppermute | solution.py:226
  66.7 0.0 collective-permute-done.13.refs_10_.refs_13_
  66.7 0.0 copy-done.9
  66.7 2.4 %collective-permute-start.14 = (f32[2,64,1024]{2,1,0:T(8,128)}, f32[2,64,1024]{2,1,0:T(8,128)}, u32[]{:S(2)}, u32[]{:S(2)}) collective-permute-start(f32[2,64,1024]{2,1,0:T(8,128)} %collective-permute-done.13.refs_10_.refs_13_), channel_id=1, source_target_pairs={{0,2},{1,31},{2,4},{3,1},{4,6},{5,3},{6,8},{7,5},{8,10},{9,7},{10,... | collective-permute-start | bytes 1572872 | tf_op jit(solution)/shard_map/ppermute | solution.py:228
  69.2 0.8 concatenate.3.info
  69.9 0.0 collective-permute-done.20
  69.9 2.4 %collective-permute-start = (s32[37]{0:T(128)S(1)}, s32[37]{0:T(128)S(1)}, u32[]{:S(2)}, u32[]{:S(2)}) collective-permute-start(s32[37]{0:T(128)S(1)} %concatenate.3.info), channel_id=1, source_target_pairs={{0,1},{1,0},{2,3},{3,2},{4,5},{5,4},{6,7},{7,6},{8,9},{9,8},{10,11... | collective-permute-start | bytes 452 | tf_op jit(solution)/shard_map/ppermute | solution.py:231
  72.3 0.4 collective-permute-done.21
  72.6 1.2 collective-permute-done.19
  73.9 1.7 %pad_maximum_fusion.u0 = f32[4,2,64,1024]{3,2,1,0:T(8,128)S(1)} fusion(f32[1,2,64,1024]{3,2,1,0:T(8,128)} %bitcast.11, f32[1,2,64,1024]{3,2,1,0:T(8,128)} %bitcast.10, f32[1,2,64,1024]{3,2,1,0:T(8,128)} %bitcast.9, f32[1,2,64,1024]{3,2,1,0:T(8,128)} %bitcast.22), kind=kLoop, calls=%fused_computation | loop fusion | flops 1572864 | bytes 4194304 | tf_op jit(solution)/shard_map/stack | solution.py:229
  75.5 0.0 copy-done.1
  75.5 0.0 copy-done.2
  75.6 0.0 copy-done.3
  75.6 3.1 %collective-permute-start.22 = (f32[4,2,64,1024]{3,2,1,0:T(8,128)S(1)}, f32[4,2,64,1024]{3,2,1,0:T(8,128)S(1)}, u32[]{:S(2)}, u32[]{:S(2)}) collective-permute-start(f32[4,2,64,1024]{3,2,1,0:T(8,128)S(1)} %pad_maximum_fusion.u0), channel_id=1, source_target_pairs={{0,128},{1,33},{32,160},{33,65},{64,192},{65,97},{96,224},{97,1},{... | collective-permute-start | bytes 6291464 | tf_op jit(solution)/shard_map/ppermute | solution.py:230
  78.7 4.4 %collective-permute-start.23 = (f32[4,2,64,1024]{3,2,1,0:T(8,128)S(1)}, f32[4,2,64,1024]{3,2,1,0:T(8,128)S(1)}, u32[]{:S(2)}, u32[]{:S(2)}) collective-permute-start(f32[4,2,64,1024]{3,2,1,0:T(8,128)S(1)} %pad_maximum_fusion.u0), channel_id=1, source_target_pairs={{0,256},{1,65},{32,288},{33,97},{64,320},{65,1},{96,352},{97,33},{... | collective-permute-start | bytes 6291464 | tf_op jit(solution)/shard_map/ppermute | solution.py:230
  83.1 0.0 collective-permute-done.other
  83.1 3.1 %collective-permute-start.24 = (f32[4,2,64,1024]{3,2,1,0:T(8,128)S(1)}, f32[4,2,64,1024]{3,2,1,0:T(8,128)S(1)}, u32[]{:S(2)}, u32[]{:S(2)}) collective-permute-start(f32[4,2,64,1024]{3,2,1,0:T(8,128)S(1)} %pad_maximum_fusion.u0), channel_id=1, source_target_pairs={{0,384},{1,97},{32,416},{33,1},{64,448},{65,33},{96,480},{97,65},{... | collective-permute-start | bytes 6291464 | tf_op jit(solution)/shard_map/ppermute | solution.py:230
  86.2 0.0 collective-permute-done.5.refs_4_.refs_5_
  86.2 1.9 %collective-permute-start.6 = (f32[2,64,1024]{2,1,0:T(8,128)}, f32[2,64,1024]{2,1,0:T(8,128)S(1)}, u32[]{:S(2)}, u32[]{:S(2)}) collective-permute-start(f32[2,64,1024]{2,1,0:T(8,128)} %collective-permute-done.5.refs_4_.refs_5_), channel_id=1, source_target_pairs={{0,2},{1,31},{2,4},{3,1},{4,6},{5,3},{6,8},{7,5},{8,10},{9,7},{10,... | collective-permute-start | bytes 1572872 | tf_op jit(solution)/shard_map/ppermute | solution.py:226
  88.1 0.0 collective-permute-done.14.refs_11_.refs_14_
  88.1 3.5 %collective-permute-start.15 = (f32[2,64,1024]{2,1,0:T(8,128)}, f32[2,64,1024]{2,1,0:T(8,128)S(1)}, u32[]{:S(2)}, u32[]{:S(2)}) collective-permute-start(f32[2,64,1024]{2,1,0:T(8,128)} %collective-permute-done.14.refs_11_.refs_14_), channel_id=1, source_target_pairs={{0,2},{1,31},{2,4},{3,1},{4,6},{5,3},{6,8},{7,5},{8,10},{9,7},{10,... | collective-permute-start | bytes 1572872 | tf_op jit(solution)/shard_map/ppermute | solution.py:228
  91.6 5.0 %collective-permute-done.6.refs_5_.refs_6_ = f32[2,64,1024]{2,1,0:T(8,128)S(1)} collective-permute-done((f32[2,64,1024]{2,1,0:T(8,128)}, f32[2,64,1024]{2,1,0:T(8,128)S(1)}, u32[]{:S(2)}, u32[]{:S(2)}) %collective-permute-start.6) | collective-permute-done | bytes 524320 | tf_op jit(solution)/shard_map/ppermute | solution.py:226
  96.6 3.1 %collective-permute-start.7 = (f32[2,64,1024]{2,1,0:T(8,128)S(1)}, f32[2,64,1024]{2,1,0:T(8,128)S(1)}, u32[]{:S(2)}, u32[]{:S(2)}) collective-permute-start(f32[2,64,1024]{2,1,0:T(8,128)S(1)} %collective-permute-done.6.refs_5_.refs_6_), channel_id=1, source_target_pairs={{0,2},{1,31},{2,4},{3,1},{4,6},{5,3},{6,8},{7,5},{8,10},{9,7},{10,... | collective-permute-start | bytes 1572872 | tf_op jit(solution)/shard_map/ppermute | solution.py:226
  99.7 2.5 %collective-permute-done.15.refs_12_.refs_15_ = f32[2,64,1024]{2,1,0:T(8,128)S(1)} collective-permute-done((f32[2,64,1024]{2,1,0:T(8,128)}, f32[2,64,1024]{2,1,0:T(8,128)S(1)}, u32[]{:S(2)}, u32[]{:S(2)}) %collective-permute-start.15) | collective-permute-done | bytes 524320 | tf_op jit(solution)/shard_map/ppermute | solution.py:228
  102.2 3.1 %collective-permute-start.16 = (f32[2,64,1024]{2,1,0:T(8,128)S(1)}, f32[2,64,1024]{2,1,0:T(8,128)S(1)}, u32[]{:S(2)}, u32[]{:S(2)}) collective-permute-start(f32[2,64,1024]{2,1,0:T(8,128)S(1)} %collective-permute-done.15.refs_12_.refs_15_), channel_id=1, source_target_pairs={{0,2},{1,31},{2,4},{3,1},{4,6},{5,3},{6,8},{7,5},{8,10},{9,7},{10,... | collective-permute-start | bytes 1572872 | tf_op jit(solution)/shard_map/ppermute | solution.py:228
  105.4 2.5 %collective-permute-done.7.refs_6_.refs_7_ = f32[2,64,1024]{2,1,0:T(8,128)S(1)} collective-permute-done((f32[2,64,1024]{2,1,0:T(8,128)S(1)}, f32[2,64,1024]{2,1,0:T(8,128)S(1)}, u32[]{:S(2)}, u32[]{:S(2)}) %collective-permute-start.7) | collective-permute-done | bytes 524320 | tf_op jit(solution)/shard_map/ppermute | solution.py:226
  107.8 5.6 %collective-permute-done.16.refs_13_.refs_16_ = f32[2,64,1024]{2,1,0:T(8,128)S(1)} collective-permute-done((f32[2,64,1024]{2,1,0:T(8,128)S(1)}, f32[2,64,1024]{2,1,0:T(8,128)S(1)}, u32[]{:S(2)}, u32[]{:S(2)}) %collective-permute-start.16) | collective-permute-done | bytes 524320 | tf_op jit(solution)/shard_map/ppermute | solution.py:228
  113.5 2.7 %shard_map.77 = f32[4,2,64,1024]{3,2,1,0:T(8,128)S(1)} custom-call(s32[37]{0:T(128)S(1)} %concatenate.3.info, s32[37]{0:T(128)S(1)} %collective-permute-done.other, f32[2,64,1024]{2,1,0:T(8,128)} %copy-done.1, f32[2,64,1024]{2,1,0:T(8,128)} %copy-done.3, f32[2,64,1024]{2,1,0:T(8,128)} %copy-done.5, f32[2,64,1024]{2,1,0:T(8,128)} %collective-permute-done.4.refs_3_.refs_4_, ...), custom_call_target="tpu_custom_call" | custom-call | tf_op jit(solution)/shard_map/pallas_call | solution.py:244
  116.2 0.0 copy-start
  116.2 6.8 %collective-permute-start.17 = (f32[4,2,64,1024]{3,2,1,0:T(8,128)S(1)}, f32[4,2,64,1024]{3,2,1,0:T(8,128)S(1)}, u32[]{:S(2)}, u32[]{:S(2)}) collective-permute-start(f32[4,2,64,1024]{3,2,1,0:T(8,128)S(1)} %shard_map.77), channel_id=1, source_target_pairs={{0,1},{1,0},{2,3},{3,2},{4,5},{5,4},{6,7},{7,6},{8,9},{9,8},{10,11... | collective-permute-start | bytes 6291464 | tf_op jit(solution)/shard_map/ppermute | solution.py:244
  123.0 0.0 collective-permute-done.22.u1
  123.0 4.3 %collective-permute-done.23.u2 = f32[4,2,64,1024]{3,2,1,0:T(8,128)S(1)} collective-permute-done((f32[4,2,64,1024]{3,2,1,0:T(8,128)S(1)}, f32[4,2,64,1024]{3,2,1,0:T(8,128)S(1)}, u32[]{:S(2)}, u32[]{:S(2)}) %collective-permute-start.23) | collective-permute-done | bytes 2097184 | tf_op jit(solution)/shard_map/ppermute | solution.py:230
  127.3 1.6 collective-permute-done.24.u3
  128.9 0.7 shard_map.78
  129.6 4.7 %collective-permute-start.25 = (f32[2,2,64,1024]{3,2,1,0:T(8,128)S(1)}, f32[2,2,64,1024]{3,2,1,0:T(8,128)S(1)}, u32[]{:S(2)}, u32[]{:S(2)}) collective-permute-start(f32[2,2,64,1024]{3,2,1,0:T(8,128)S(1)} %shard_map.78), channel_id=1, source_target_pairs={{0,1},{1,0},{2,3},{3,2},{4,5},{5,4},{6,7},{7,6},{8,9},{9,8},{10,11... | collective-permute-start | bytes 3145736 | tf_op jit(solution)/shard_map/ppermute | solution.py:241
  134.3 4.9 %collective-permute-start.8 = (f32[2,64,1024]{2,1,0:T(8,128)S(1)}, f32[2,64,1024]{2,1,0:T(8,128)S(1)}, u32[]{:S(2)}, u32[]{:S(2)}) collective-permute-start(f32[2,64,1024]{2,1,0:T(8,128)S(1)} %collective-permute-done.7.refs_6_.refs_7_), channel_id=1, source_target_pairs={{0,2},{1,31},{2,4},{3,1},{4,6},{5,3},{6,8},{7,5},{8,10},{9,7},{10,... | collective-permute-start | bytes 1572872 | tf_op jit(solution)/shard_map/ppermute | solution.py:226
  139.2 6.1 %collective-permute-done.8.refs_8_ = f32[2,64,1024]{2,1,0:T(8,128)S(1)} collective-permute-done((f32[2,64,1024]{2,1,0:T(8,128)S(1)}, f32[2,64,1024]{2,1,0:T(8,128)S(1)}, u32[]{:S(2)}, u32[]{:S(2)}) %collective-permute-start.8) | collective-permute-done | bytes 524320 | tf_op jit(solution)/shard_map/ppermute | solution.py:226
  145.3 3.2 %collective-permute-start.18 = (f32[2,64,1024]{2,1,0:T(8,128)S(1)}, f32[2,64,1024]{2,1,0:T(8,128)S(1)}, u32[]{:S(2)}, u32[]{:S(2)}) collective-permute-start(f32[2,64,1024]{2,1,0:T(8,128)S(1)} %collective-permute-done.8.refs_8_), channel_id=1, source_target_pairs={{0,1},{1,0},{2,3},{3,2},{4,5},{5,4},{6,7},{7,6},{8,9},{9,8},{10,11... | collective-permute-start | bytes 1572872 | tf_op jit(solution)/shard_map/ppermute | solution.py:245
  148.5 0.0 collective-permute-done.25.up_in
  148.5 2.0 %shard_map.79 = (f32[4,64,1024]{2,1,0:T(8,128)S(1)}, f32[4,64,1024]{2,1,0:T(8,128)S(1)}, f32[64,256]{1,0:T(8,128)S(1)}) custom-call(s32[37]{0:T(128)S(1)} %concatenate.3.info, f32[4,2,64,1024]{3,2,1,0:T(8,128)S(1)} %pad_maximum_fusion.u0, f32[4,2,64,1024]{3,2,1,0:T(8,128)S(1)} %collective-permute-done.22.u1, ...), custom_call_target="tpu_custom_call" | custom-call | tf_op jit(solution)/shard_map/pallas_call | solution.py:252
  150.5 0.0 collective-permute-done.18.refs_18_
  150.5 0.0 collective-permute-done.17.refs_17_
  150.5 10.8 %shard_map.80 = (f32[64,1024]{1,0:T(8,128)}, f32[64,1024]{1,0:T(8,128)}) custom-call(s32[37]{0:T(128)S(1)} %concatenate.3.info, s32[37]{0:T(128)S(1)} %collective-permute-done.other, f32[2,64,1024]{2,1,0:T(8,128)} %bitcast.18, f32[2,64,1024]{2,1,0:T(8,128)} %copy-done.1, f32[2,64,1024]{2,1,0:T(8,128)} %copy-done.3, f32[2,64,1024]{2,1,0:T(8,128)} %copy-done.5, ...), custom_call_target="tpu_custom_call" | custom-call | tf_op jit(solution)/shard_map/pallas_call | solution.py:255
  (14 shorter events, 0.0 us)
Async XLA Ops:
  0.6 14.5 %collective-permute-start.9 = (f32[2,64,1024]{2,1,0:T(8,128)}, f32[2,64,1024]{2,1,0:T(8,128)S(1)}, u32[]{:S(2)}, u32[]{:S(2)}) collective-permute-start(f32[2,64,1024]{2,1,0:T(8,128)} %bitcast.16), channel_id=1, source_target_pairs={{0,1},{1,0},{2,3},{3,2},{4,5},{5,4},{6,7},{7,6},{8,9},{9,8},{10,11... | collective-permute-start | bytes 1572872 | tf_op jit(solution)/shard_map/ppermute | solution.py:221
  9.4 12.2 %collective-permute-start.1 = (f32[2,64,1024]{2,1,0:T(8,128)}, f32[2,64,1024]{2,1,0:T(8,128)S(1)}, u32[]{:S(2)}, u32[]{:S(2)}) collective-permute-start(f32[2,64,1024]{2,1,0:T(8,128)} %bitcast.17), channel_id=1, source_target_pairs={{0,2},{1,31},{2,4},{3,1},{4,6},{5,3},{6,8},{7,5},{8,10},{9,7},{10,... | collective-permute-start | bytes 1572872 | tf_op jit(solution)/shard_map/ppermute | solution.py:226
  15.2 51.5 %copy-start.9 = (f32[2,64,1024]{2,1,0:T(8,128)}, f32[2,64,1024]{2,1,0:T(8,128)S(1)}, u32[]{:S(2)}) copy-start(f32[2,64,1024]{2,1,0:T(8,128)S(1)} %collective-permute-done.9.refs_9_) | copy-start | bytes 1572868
  15.2 11.9 %collective-permute-start.10 = (f32[2,64,1024]{2,1,0:T(8,128)S(1)}, f32[2,64,1024]{2,1,0:T(8,128)S(1)}, u32[]{:S(2)}, u32[]{:S(2)}) collective-permute-start(f32[2,64,1024]{2,1,0:T(8,128)S(1)} %collective-permute-done.9.refs_9_), channel_id=1, source_target_pairs={{0,2},{1,31},{2,4},{3,1},{4,6},{5,3},{6,8},{7,5},{8,10},{9,7},{10,... | collective-permute-start | bytes 1572872 | tf_op jit(solution)/shard_map/ppermute | solution.py:228
  21.6 53.9 %copy-start.1 = (f32[2,64,1024]{2,1,0:T(8,128)}, f32[2,64,1024]{2,1,0:T(8,128)S(1)}, u32[]{:S(2)}) copy-start(f32[2,64,1024]{2,1,0:T(8,128)S(1)} %collective-permute-done.1.refs_0_.refs_1_) | copy-start | bytes 1572868
  21.6 11.1 %collective-permute-start.2 = (f32[2,64,1024]{2,1,0:T(8,128)S(1)}, f32[2,64,1024]{2,1,0:T(8,128)S(1)}, u32[]{:S(2)}, u32[]{:S(2)}) collective-permute-start(f32[2,64,1024]{2,1,0:T(8,128)S(1)} %collective-permute-done.1.refs_0_.refs_1_), channel_id=1, source_target_pairs={{0,2},{1,31},{2,4},{3,1},{4,6},{5,3},{6,8},{7,5},{8,10},{9,7},{10,... | collective-permute-start | bytes 1572872 | tf_op jit(solution)/shard_map/ppermute | solution.py:226
  27.1 48.4 %copy-start.2 = (f32[2,64,1024]{2,1,0:T(8,128)}, f32[2,64,1024]{2,1,0:T(8,128)S(1)}, u32[]{:S(2)}) copy-start(f32[2,64,1024]{2,1,0:T(8,128)S(1)} %collective-permute-done.10.refs_7_.refs_10_) | copy-start | bytes 1572868
  27.1 11.2 %collective-permute-start.11 = (f32[2,64,1024]{2,1,0:T(8,128)S(1)}, f32[2,64,1024]{2,1,0:T(8,128)S(1)}, u32[]{:S(2)}, u32[]{:S(2)}) collective-permute-start(f32[2,64,1024]{2,1,0:T(8,128)S(1)} %collective-permute-done.10.refs_7_.refs_10_), channel_id=1, source_target_pairs={{0,2},{1,31},{2,4},{3,1},{4,6},{5,3},{6,8},{7,5},{8,10},{9,7},{10,... | collective-permute-start | bytes 1572872 | tf_op jit(solution)/shard_map/ppermute | solution.py:228
  32.7 42.8 %copy-start.3 = (f32[2,64,1024]{2,1,0:T(8,128)}, f32[2,64,1024]{2,1,0:T(8,128)S(1)}, u32[]{:S(2)}) copy-start(f32[2,64,1024]{2,1,0:T(8,128)S(1)} %collective-permute-done.2.refs_1_.refs_2_) | copy-start | bytes 1572868
  32.7 11.2 %collective-permute-start.3 = (f32[2,64,1024]{2,1,0:T(8,128)S(1)}, f32[2,64,1024]{2,1,0:T(8,128)S(1)}, u32[]{:S(2)}, u32[]{:S(2)}) collective-permute-start(f32[2,64,1024]{2,1,0:T(8,128)S(1)} %collective-permute-done.2.refs_1_.refs_2_), channel_id=1, source_target_pairs={{0,2},{1,31},{2,4},{3,1},{4,6},{5,3},{6,8},{7,5},{8,10},{9,7},{10,... | collective-permute-start | bytes 1572872 | tf_op jit(solution)/shard_map/ppermute | solution.py:226
  38.3 37.2 %copy-start.4 = (f32[2,64,1024]{2,1,0:T(8,128)}, f32[2,64,1024]{2,1,0:T(8,128)S(1)}, u32[]{:S(2)}) copy-start(f32[2,64,1024]{2,1,0:T(8,128)S(1)} %collective-permute-done.11.refs_8_.refs_11_) | copy-start | bytes 1572868
  38.3 11.2 %collective-permute-start.12 = (f32[2,64,1024]{2,1,0:T(8,128)S(1)}, f32[2,64,1024]{2,1,0:T(8,128)S(1)}, u32[]{:S(2)}, u32[]{:S(2)}) collective-permute-start(f32[2,64,1024]{2,1,0:T(8,128)S(1)} %collective-permute-done.11.refs_8_.refs_11_), channel_id=1, source_target_pairs={{0,2},{1,31},{2,4},{3,1},{4,6},{5,3},{6,8},{7,5},{8,10},{9,7},{10,... | collective-permute-start | bytes 1572872 | tf_op jit(solution)/shard_map/ppermute | solution.py:228
  44.0 31.6 %copy-start.5 = (f32[2,64,1024]{2,1,0:T(8,128)}, f32[2,64,1024]{2,1,0:T(8,128)S(1)}, u32[]{:S(2)}) copy-start(f32[2,64,1024]{2,1,0:T(8,128)S(1)} %collective-permute-done.3.refs_2_.refs_3_) | copy-start | bytes 1572868
  44.0 20.8 %collective-permute-start.4 = (f32[2,64,1024]{2,1,0:T(8,128)S(1)}, f32[2,64,1024]{2,1,0:T(8,128)}, u32[]{:S(2)}, u32[]{:S(2)}) collective-permute-start(f32[2,64,1024]{2,1,0:T(8,128)S(1)} %collective-permute-done.3.refs_2_.refs_3_), channel_id=1, source_target_pairs={{0,2},{1,31},{2,4},{3,1},{4,6},{5,3},{6,8},{7,5},{8,10},{9,7},{10,... | collective-permute-start | bytes 1572872 | tf_op jit(solution)/shard_map/ppermute | solution.py:226
  49.6 26.0 %copy-start.6 = (f32[2,64,1024]{2,1,0:T(8,128)}, f32[2,64,1024]{2,1,0:T(8,128)S(1)}, u32[]{:S(2)}) copy-start(f32[2,64,1024]{2,1,0:T(8,128)S(1)} %collective-permute-done.12.refs_9_.refs_12_) | copy-start | bytes 1572868
  49.6 17.1 %collective-permute-start.13 = (f32[2,64,1024]{2,1,0:T(8,128)S(1)}, f32[2,64,1024]{2,1,0:T(8,128)}, u32[]{:S(2)}, u32[]{:S(2)}) collective-permute-start(f32[2,64,1024]{2,1,0:T(8,128)S(1)} %collective-permute-done.12.refs_9_.refs_12_), channel_id=1, source_target_pairs={{0,2},{1,31},{2,4},{3,1},{4,6},{5,3},{6,8},{7,5},{8,10},{9,7},{10,... | collective-permute-start | bytes 1572872 | tf_op jit(solution)/shard_map/ppermute | solution.py:228
  54.6 15.3 %collective-permute-start.20 = (f32[2,64,1024]{2,1,0:T(8,128)}, f32[2,64,1024]{2,1,0:T(8,128)}, u32[]{:S(2)}, u32[]{:S(2)}) collective-permute-start(f32[2,64,1024]{2,1,0:T(8,128)} %bitcast.19), channel_id=1, source_target_pairs={{0,64},{1,257},{32,96},{33,289},{64,0},{65,321},{96,32},{97,353},{... | collective-permute-start | bytes 1572872 | tf_op jit(solution)/shard_map/ppermute | solution.py:229
  59.4 13.2 %collective-permute-start.21 = (f32[2,64,1024]{2,1,0:T(8,128)}, f32[2,64,1024]{2,1,0:T(8,128)}, u32[]{:S(2)}, u32[]{:S(2)}) collective-permute-start(f32[2,64,1024]{2,1,0:T(8,128)} %bitcast.20), channel_id=1, source_target_pairs={{0,96},{1,385},{32,0},{33,417},{64,32},{65,449},{96,64},{97,481},{... | collective-permute-start | bytes 1572872 | tf_op jit(solution)/shard_map/ppermute | solution.py:229
  62.1 11.7 %collective-permute-start.19 = (f32[2,64,1024]{2,1,0:T(8,128)}, f32[2,64,1024]{2,1,0:T(8,128)}, u32[]{:S(2)}, u32[]{:S(2)}) collective-permute-start(f32[2,64,1024]{2,1,0:T(8,128)} %bitcast.21), channel_id=1, source_target_pairs={{0,32},{1,129},{32,64},{33,161},{64,96},{65,193},{96,0},{97,225},{... | collective-permute-start | bytes 1572872 | tf_op jit(solution)/shard_map/ppermute | solution.py:229
  64.8 21.4 %collective-permute-start.5 = (f32[2,64,1024]{2,1,0:T(8,128)}, f32[2,64,1024]{2,1,0:T(8,128)}, u32[]{:S(2)}, u32[]{:S(2)}) collective-permute-start(f32[2,64,1024]{2,1,0:T(8,128)} %collective-permute-done.4.refs_3_.refs_4_), channel_id=1, source_target_pairs={{0,2},{1,31},{2,4},{3,1},{4,6},{5,3},{6,8},{7,5},{8,10},{9,7},{10,... | collective-permute-start | bytes 1572872 | tf_op jit(solution)/shard_map/ppermute | solution.py:226
  66.7 21.4 %collective-permute-start.14 = (f32[2,64,1024]{2,1,0:T(8,128)}, f32[2,64,1024]{2,1,0:T(8,128)}, u32[]{:S(2)}, u32[]{:S(2)}) collective-permute-start(f32[2,64,1024]{2,1,0:T(8,128)} %collective-permute-done.13.refs_10_.refs_13_), channel_id=1, source_target_pairs={{0,2},{1,31},{2,4},{3,1},{4,6},{5,3},{6,8},{7,5},{8,10},{9,7},{10,... | collective-permute-start | bytes 1572872 | tf_op jit(solution)/shard_map/ppermute | solution.py:228
  69.9 13.2 %collective-permute-start = (s32[37]{0:T(128)S(1)}, s32[37]{0:T(128)S(1)}, u32[]{:S(2)}, u32[]{:S(2)}) collective-permute-start(s32[37]{0:T(128)S(1)} %concatenate.3.info), channel_id=1, source_target_pairs={{0,1},{1,0},{2,3},{3,2},{4,5},{5,4},{6,7},{7,6},{8,9},{9,8},{10,11... | collective-permute-start | bytes 452 | tf_op jit(solution)/shard_map/ppermute | solution.py:231
  75.6 47.4 %collective-permute-start.22 = (f32[4,2,64,1024]{3,2,1,0:T(8,128)S(1)}, f32[4,2,64,1024]{3,2,1,0:T(8,128)S(1)}, u32[]{:S(2)}, u32[]{:S(2)}) collective-permute-start(f32[4,2,64,1024]{3,2,1,0:T(8,128)S(1)} %pad_maximum_fusion.u0), channel_id=1, source_target_pairs={{0,128},{1,33},{32,160},{33,65},{64,192},{65,97},{96,224},{97,1},{... | collective-permute-start | bytes 6291464 | tf_op jit(solution)/shard_map/ppermute | solution.py:230
  78.7 48.6 %collective-permute-start.23 = (f32[4,2,64,1024]{3,2,1,0:T(8,128)S(1)}, f32[4,2,64,1024]{3,2,1,0:T(8,128)S(1)}, u32[]{:S(2)}, u32[]{:S(2)}) collective-permute-start(f32[4,2,64,1024]{3,2,1,0:T(8,128)S(1)} %pad_maximum_fusion.u0), channel_id=1, source_target_pairs={{0,256},{1,65},{32,288},{33,97},{64,320},{65,1},{96,352},{97,33},{... | collective-permute-start | bytes 6291464 | tf_op jit(solution)/shard_map/ppermute | solution.py:230
  83.1 45.8 %collective-permute-start.24 = (f32[4,2,64,1024]{3,2,1,0:T(8,128)S(1)}, f32[4,2,64,1024]{3,2,1,0:T(8,128)S(1)}, u32[]{:S(2)}, u32[]{:S(2)}) collective-permute-start(f32[4,2,64,1024]{3,2,1,0:T(8,128)S(1)} %pad_maximum_fusion.u0), channel_id=1, source_target_pairs={{0,384},{1,97},{32,416},{33,1},{64,448},{65,33},{96,480},{97,65},{... | collective-permute-start | bytes 6291464 | tf_op jit(solution)/shard_map/ppermute | solution.py:230
  86.2 10.4 %collective-permute-start.6 = (f32[2,64,1024]{2,1,0:T(8,128)}, f32[2,64,1024]{2,1,0:T(8,128)S(1)}, u32[]{:S(2)}, u32[]{:S(2)}) collective-permute-start(f32[2,64,1024]{2,1,0:T(8,128)} %collective-permute-done.5.refs_4_.refs_5_), channel_id=1, source_target_pairs={{0,2},{1,31},{2,4},{3,1},{4,6},{5,3},{6,8},{7,5},{8,10},{9,7},{10,... | collective-permute-start | bytes 1572872 | tf_op jit(solution)/shard_map/ppermute | solution.py:226
  88.1 14.1 %collective-permute-start.15 = (f32[2,64,1024]{2,1,0:T(8,128)}, f32[2,64,1024]{2,1,0:T(8,128)S(1)}, u32[]{:S(2)}, u32[]{:S(2)}) collective-permute-start(f32[2,64,1024]{2,1,0:T(8,128)} %collective-permute-done.14.refs_11_.refs_14_), channel_id=1, source_target_pairs={{0,2},{1,31},{2,4},{3,1},{4,6},{5,3},{6,8},{7,5},{8,10},{9,7},{10,... | collective-permute-start | bytes 1572872 | tf_op jit(solution)/shard_map/ppermute | solution.py:228
  96.6 16.9 %copy-start.7 = (f32[2,64,1024]{2,1,0:T(8,128)}, f32[2,64,1024]{2,1,0:T(8,128)S(1)}, u32[]{:S(2)}) copy-start(f32[2,64,1024]{2,1,0:T(8,128)S(1)} %collective-permute-done.6.refs_5_.refs_6_) | copy-start | bytes 1572868
  96.6 11.2 %collective-permute-start.7 = (f32[2,64,1024]{2,1,0:T(8,128)S(1)}, f32[2,64,1024]{2,1,0:T(8,128)S(1)}, u32[]{:S(2)}, u32[]{:S(2)}) collective-permute-start(f32[2,64,1024]{2,1,0:T(8,128)S(1)} %collective-permute-done.6.refs_5_.refs_6_), channel_id=1, source_target_pairs={{0,2},{1,31},{2,4},{3,1},{4,6},{5,3},{6,8},{7,5},{8,10},{9,7},{10,... | collective-permute-start | bytes 1572872 | tf_op jit(solution)/shard_map/ppermute | solution.py:226
  102.2 11.2 %copy-start.8 = (f32[2,64,1024]{2,1,0:T(8,128)}, f32[2,64,1024]{2,1,0:T(8,128)S(1)}, u32[]{:S(2)}) copy-start(f32[2,64,1024]{2,1,0:T(8,128)S(1)} %collective-permute-done.15.refs_12_.refs_15_) | copy-start | bytes 1572868
  102.2 11.2 %collective-permute-start.16 = (f32[2,64,1024]{2,1,0:T(8,128)S(1)}, f32[2,64,1024]{2,1,0:T(8,128)S(1)}, u32[]{:S(2)}, u32[]{:S(2)}) collective-permute-start(f32[2,64,1024]{2,1,0:T(8,128)S(1)} %collective-permute-done.15.refs_12_.refs_15_), channel_id=1, source_target_pairs={{0,2},{1,31},{2,4},{3,1},{4,6},{5,3},{6,8},{7,5},{8,10},{9,7},{10,... | collective-permute-start | bytes 1572872 | tf_op jit(solution)/shard_map/ppermute | solution.py:228
  116.2 32.3 %copy-start = (f32[1,1,2,64,1024]{4,3,2,1,0:T(8,128)S(1)}, f32[1,1,2,64,1024]{4,3,2,1,0:T(8,128)}, u32[]{:S(2)}) copy-start(f32[1,1,2,64,1024]{4,3,2,1,0:T(8,128)} %param.11) | copy-start | bytes 1572868
  116.2 34.3 %collective-permute-start.17 = (f32[4,2,64,1024]{3,2,1,0:T(8,128)S(1)}, f32[4,2,64,1024]{3,2,1,0:T(8,128)S(1)}, u32[]{:S(2)}, u32[]{:S(2)}) collective-permute-start(f32[4,2,64,1024]{3,2,1,0:T(8,128)S(1)} %shard_map.77), channel_id=1, source_target_pairs={{0,1},{1,0},{2,3},{3,2},{4,5},{5,4},{6,7},{7,6},{8,9},{9,8},{10,11... | collective-permute-start | bytes 6291464 | tf_op jit(solution)/shard_map/ppermute | solution.py:244
  129.6 18.9 %collective-permute-start.25 = (f32[2,2,64,1024]{3,2,1,0:T(8,128)S(1)}, f32[2,2,64,1024]{3,2,1,0:T(8,128)S(1)}, u32[]{:S(2)}, u32[]{:S(2)}) collective-permute-start(f32[2,2,64,1024]{3,2,1,0:T(8,128)S(1)} %shard_map.78), channel_id=1, source_target_pairs={{0,1},{1,0},{2,3},{3,2},{4,5},{5,4},{6,7},{7,6},{8,9},{9,8},{10,11... | collective-permute-start | bytes 3145736 | tf_op jit(solution)/shard_map/ppermute | solution.py:241
  134.3 11.0 %collective-permute-start.8 = (f32[2,64,1024]{2,1,0:T(8,128)S(1)}, f32[2,64,1024]{2,1,0:T(8,128)S(1)}, u32[]{:S(2)}, u32[]{:S(2)}) collective-permute-start(f32[2,64,1024]{2,1,0:T(8,128)S(1)} %collective-permute-done.7.refs_6_.refs_7_), channel_id=1, source_target_pairs={{0,2},{1,31},{2,4},{3,1},{4,6},{5,3},{6,8},{7,5},{8,10},{9,7},{10,... | collective-permute-start | bytes 1572872 | tf_op jit(solution)/shard_map/ppermute | solution.py:226
  145.3 5.2 %collective-permute-start.18 = (f32[2,64,1024]{2,1,0:T(8,128)S(1)}, f32[2,64,1024]{2,1,0:T(8,128)S(1)}, u32[]{:S(2)}, u32[]{:S(2)}) collective-permute-start(f32[2,64,1024]{2,1,0:T(8,128)S(1)} %collective-permute-done.8.refs_8_), channel_id=1, source_target_pairs={{0,1},{1,0},{2,3},{3,2},{4,5},{5,4},{6,7},{7,6},{8,9},{9,8},{10,11... | collective-permute-start | bytes 1572872 | tf_op jit(solution)/shard_map/ppermute | solution.py:245

commit v3 on v2

--- a/solution.py
+++ b/solution.py
@@ -11,7 +11,6 @@
 KD = 2
 CB = 8
 SIDE = 4
-HIGH = lax.Precision.HIGHEST
 UP_AT, TARGET_AT, ROW_AT, COL_AT, DEPTH_AT = 16, 32, 34, 35, 36
 
 
@@ -83,8 +82,16 @@
                 pltpu.make_async_copy(pieces[0], out.at[slot], sems.at[slot]).wait()
 
 
+def parts(x):
+    high = x.astype(jnp.bfloat16)
+    return high, (x - high.astype(jnp.float32)).astype(jnp.bfloat16)
+
+
 def dot(a, b, contract):
-    return lax.dot_general(a, b, ((contract[:1], contract[1:]), ((), ())), precision=HIGH, preferred_element_type=jnp.float32)
+    dims = ((contract[:1], contract[1:]), ((), ()))
+    one = lambda u, v: lax.dot_general(u, v, dims, preferred_element_type=jnp.float32)
+    (a_high, a_low), (b_high, b_low) = parts(a), parts(b)
+    return one(a_high, b_high) + (one(a_high, b_low) + one(a_low, b_high))
 
 
 def inverse_factor(gram):
@@ -187,18 +194,17 @@
     for slot in range(slots):
         for copy in copies(own[0], slot):
             copy.wait()
-    x_all = xs[...].reshape(slots * n, size)
-    q_all = qs[...].reshape(slots * n, size)
     middles = [dot(ys[i], ps[i], (1, 1)) for i in range(slots)]
-    folded = jnp.concatenate([dot(tested[:, i * n : i * n + n], middles[i], (1, 1)) for i in range(slots)], axis=1)
-    sample = dot(folded, x_all, (1, 0))
-    inner = dot(sample, x_all, (1, 1))
-    turned = jnp.concatenate([dot(inner[:, i * n : i * n + n], middles[i], (1, 0)) for i in range(slots)], axis=1)
-    project = dot(turned, q_all, (1, 0))
+    folded = [dot(tested[:, i * n : i * n + n], middles[i], (1, 1)) for i in range(slots)]
+    sample = dot(jnp.concatenate(folded, axis=1), xs[...].reshape(slots * n, size), (1, 0))
     inverse = inverse_factor(dot(sample, sample, (1, 1)))
+    turned = jnp.concatenate([dot(dot(sample, xs[i], (1, 1)), middles[i], (1, 0)) for i in range(slots)], axis=1)
     root = math.sqrt(size)
     basis_out[...] = dot(inverse * root, sample, (1, 0))
-    weights_out[...] = dot(inverse * (1 / root), project, (1, 0))
+    wide = size // 4
+    for at in range(0, size, wide):
+        project = dot(turned, qs[:, :, at : at + wide].reshape(slots * n, wide), (1, 0))
+        weights_out[:, at : at + wide] = dot(inverse * (1 / root), project, (1, 0))
 
 
 def local_kernel(kernel, in_spaces, out_shape, out_space, scratch, mebibytes=1):

time: 162 us -> 159 us (0.981)
  Pallas kernels: 16.1 us -> 12.4 us
    pallas_call x1, Pallas kernels: 10.8 us -> 7.5 us  [pieces_and_tile(): whole(info, other, *own_held, *across_held, left_in, last_in, *up_sides)]
  transfers between devices with their start and end apart: 26 -> 26, of which waited for: 15 -> 15; matrix products, arithmetic and copies ran while one was open for 1% -> 2% of each run, Pallas kernels for 3% -> 3%
where the time goes in v3:
time: 159 us; the launch traced here: 158 us
  starting transfers between devices  106 us (67%)
  waiting for transfers between devices  36 us (23%)
  Pallas kernels  12.4 us (8%)
  other arithmetic  1.65 us (1%)
    ppermute x8, starting transfers between devices, pieces_and_tile(): own_pieces.append(lax.ppermute(own_pieces[-1], ('col', 'depth'), shift))  32.5 us
    ppermute x7, starting transfers between devices, pieces_and_tile(): lax.ppermute(across_pieces[-1], ('col', 'depth'), shift)  26.7 us
    ppermute x8, waiting for transfers between devices, pieces_and_tile(): own_pieces.append(lax.ppermute(own_pieces[-1], ('col', 'depth'), shift))  18.6 us
    ppermute x3, starting transfers between devices, pieces_and_tile(): lax.ppermute(block, ('row', 'depth'), xy_shift(s, 1))  10.5 us
    ppermute x3, starting transfers between devices, pieces_and_tile(): lax.ppermute(up, ('row', 'depth'), xy_shift(s, 0))  10.1 us
    ppermute x7, waiting for transfers between devices, pieces_and_tile(): lax.ppermute(across_pieces[-1], ('col', 'depth'), shift)  9.89 us
    ppermute x1, starting transfers between devices, pieces_and_tile(): across = lax.ppermute(own, 'depth', SWAP)  8.75 us
    pallas_call x1, Pallas kernels, pieces_and_tile(): whole(info, other, *own_held, *across_held, left_in, last_in, *up_sides)  7.5 us
  transfers between devices with their start and end apart: 26, of which 15 were waited for; matrix products, arithmetic and copies ran while one was open for 2% of the time, Pallas kernels for 3%

profile of v3, /device:TPU:1, one launch (start us, length us, event | category | flops | bytes accessed | tf_op | source)
XLA Modules:
  0.0 157.5 jit_solution(4950541516891418208)
XLA Ops:
  0.6 8.7 %collective-permute-start.9 = (f32[2,64,1024]{2,1,0:T(8,128)}, f32[2,64,1024]{2,1,0:T(8,128)S(1)}, u32[]{:S(2)}, u32[]{:S(2)}) collective-permute-start(f32[2,64,1024]{2,1,0:T(8,128)} %bitcast.16), channel_id=1, source_target_pairs={{0,1},{1,0},{2,3},{3,2},{4,5},{5,4},{6,7},{7,6},{8,9},{9,8},{10,11... | collective-permute-start | bytes 1572872 | tf_op jit(solution)/shard_map/ppermute | solution.py:227
  9.4 5.8 %collective-permute-start.1 = (f32[2,64,1024]{2,1,0:T(8,128)}, f32[2,64,1024]{2,1,0:T(8,128)S(1)}, u32[]{:S(2)}, u32[]{:S(2)}) collective-permute-start(f32[2,64,1024]{2,1,0:T(8,128)} %bitcast.17), channel_id=1, source_target_pairs={{0,2},{1,31},{2,4},{3,1},{4,6},{5,3},{6,8},{7,5},{8,10},{9,7},{10,... | collective-permute-start | bytes 1572872 | tf_op jit(solution)/shard_map/ppermute | solution.py:232
  15.2 0.0 collective-permute-done.9.refs_9_
  15.2 0.0 copy-start.9
  15.2 2.6 %collective-permute-start.10 = (f32[2,64,1024]{2,1,0:T(8,128)S(1)}, f32[2,64,1024]{2,1,0:T(8,128)S(1)}, u32[]{:S(2)}, u32[]{:S(2)}) collective-permute-start(f32[2,64,1024]{2,1,0:T(8,128)S(1)} %collective-permute-done.9.refs_9_), channel_id=1, source_target_pairs={{0,2},{1,31},{2,4},{3,1},{4,6},{5,3},{6,8},{7,5},{8,10},{9,7},{10,... | collective-permute-start | bytes 1572872 | tf_op jit(solution)/shard_map/ppermute | solution.py:234
  17.8 3.8 %collective-permute-done.1.refs_0_.refs_1_ = f32[2,64,1024]{2,1,0:T(8,128)S(1)} collective-permute-done((f32[2,64,1024]{2,1,0:T(8,128)}, f32[2,64,1024]{2,1,0:T(8,128)S(1)}, u32[]{:S(2)}, u32[]{:S(2)}) %collective-permute-start.1) | collective-permute-done | bytes 524320 | tf_op jit(solution)/shard_map/ppermute | solution.py:232
  21.6 4.9 %collective-permute-start.2 = (f32[2,64,1024]{2,1,0:T(8,128)S(1)}, f32[2,64,1024]{2,1,0:T(8,128)S(1)}, u32[]{:S(2)}, u32[]{:S(2)}) collective-permute-start(f32[2,64,1024]{2,1,0:T(8,128)S(1)} %collective-permute-done.1.refs_0_.refs_1_), channel_id=1, source_target_pairs={{0,2},{1,31},{2,4},{3,1},{4,6},{5,3},{6,8},{7,5},{8,10},{9,7},{10,... | collective-permute-start | bytes 1572872 | tf_op jit(solution)/shard_map/ppermute | solution.py:232
  26.5 0.6 collective-permute-done.10.refs_7_.refs_10_
  27.1 5.0 %collective-permute-start.11 = (f32[2,64,1024]{2,1,0:T(8,128)S(1)}, f32[2,64,1024]{2,1,0:T(8,128)S(1)}, u32[]{:S(2)}, u32[]{:S(2)}) collective-permute-start(f32[2,64,1024]{2,1,0:T(8,128)S(1)} %collective-permute-done.10.refs_7_.refs_10_), channel_id=1, source_target_pairs={{0,2},{1,31},{2,4},{3,1},{4,6},{5,3},{6,8},{7,5},{8,10},{9,7},{10,... | collective-permute-start | bytes 1572872 | tf_op jit(solution)/shard_map/ppermute | solution.py:234
  32.1 0.6 collective-permute-done.2.refs_1_.refs_2_
  32.7 5.0 %collective-permute-start.3 = (f32[2,64,1024]{2,1,0:T(8,128)S(1)}, f32[2,64,1024]{2,1,0:T(8,128)S(1)}, u32[]{:S(2)}, u32[]{:S(2)}) collective-permute-start(f32[2,64,1024]{2,1,0:T(8,128)S(1)} %collective-permute-done.2.refs_1_.refs_2_), channel_id=1, source_target_pairs={{0,2},{1,31},{2,4},{3,1},{4,6},{5,3},{6,8},{7,5},{8,10},{9,7},{10,... | collective-permute-start | bytes 1572872 | tf_op jit(solution)/shard_map/ppermute | solution.py:232
  37.7 0.6 collective-permute-done.11.refs_8_.refs_11_
  38.3 5.0 %collective-permute-start.12 = (f32[2,64,1024]{2,1,0:T(8,128)S(1)}, f32[2,64,1024]{2,1,0:T(8,128)S(1)}, u32[]{:S(2)}, u32[]{:S(2)}) collective-permute-start(f32[2,64,1024]{2,1,0:T(8,128)S(1)} %collective-permute-done.11.refs_8_.refs_11_), channel_id=1, source_target_pairs={{0,2},{1,31},{2,4},{3,1},{4,6},{5,3},{6,8},{7,5},{8,10},{9,7},{10,... | collective-permute-start | bytes 1572872 | tf_op jit(solution)/shard_map/ppermute | solution.py:234
  43.4 0.6 collective-permute-done.3.refs_2_.refs_3_
  44.0 5.0 %collective-permute-start.4 = (f32[2,64,1024]{2,1,0:T(8,128)S(1)}, f32[2,64,1024]{2,1,0:T(8,128)}, u32[]{:S(2)}, u32[]{:S(2)}) collective-permute-start(f32[2,64,1024]{2,1,0:T(8,128)S(1)} %collective-permute-done.3.refs_2_.refs_3_), channel_id=1, source_target_pairs={{0,2},{1,31},{2,4},{3,1},{4,6},{5,3},{6,8},{7,5},{8,10},{9,7},{10,... | collective-permute-start | bytes 1572872 | tf_op jit(solution)/shard_map/ppermute | solution.py:232
  49.0 0.6 collective-permute-done.12.refs_9_.refs_12_
  49.6 5.0 %collective-permute-start.13 = (f32[2,64,1024]{2,1,0:T(8,128)S(1)}, f32[2,64,1024]{2,1,0:T(8,128)}, u32[]{:S(2)}, u32[]{:S(2)}) collective-permute-start(f32[2,64,1024]{2,1,0:T(8,128)S(1)} %collective-permute-done.12.refs_9_.refs_12_), channel_id=1, source_target_pairs={{0,2},{1,31},{2,4},{3,1},{4,6},{5,3},{6,8},{7,5},{8,10},{9,7},{10,... | collective-permute-start | bytes 1572872 | tf_op jit(solution)/shard_map/ppermute | solution.py:234
  54.6 4.8 %collective-permute-start.20 = (f32[2,64,1024]{2,1,0:T(8,128)}, f32[2,64,1024]{2,1,0:T(8,128)}, u32[]{:S(2)}, u32[]{:S(2)}) collective-permute-start(f32[2,64,1024]{2,1,0:T(8,128)} %bitcast.19), channel_id=1, source_target_pairs={{0,64},{1,257},{32,96},{33,289},{64,0},{65,321},{96,32},{97,353},{... | collective-permute-start | bytes 1572872 | tf_op jit(solution)/shard_map/ppermute | solution.py:235
  59.4 2.7 %collective-permute-start.21 = (f32[2,64,1024]{2,1,0:T(8,128)}, f32[2,64,1024]{2,1,0:T(8,128)}, u32[]{:S(2)}, u32[]{:S(2)}) collective-permute-start(f32[2,64,1024]{2,1,0:T(8,128)} %bitcast.20), channel_id=1, source_target_pairs={{0,96},{1,385},{32,0},{33,417},{64,32},{65,449},{96,64},{97,481},{... | collective-permute-start | bytes 1572872 | tf_op jit(solution)/shard_map/ppermute | solution.py:235
  62.1 2.6 %collective-permute-start.19 = (f32[2,64,1024]{2,1,0:T(8,128)}, f32[2,64,1024]{2,1,0:T(8,128)}, u32[]{:S(2)}, u32[]{:S(2)}) collective-permute-start(f32[2,64,1024]{2,1,0:T(8,128)} %bitcast.21), channel_id=1, source_target_pairs={{0,32},{1,129},{32,64},{33,161},{64,96},{65,193},{96,0},{97,225},{... | collective-permute-start | bytes 1572872 | tf_op jit(solution)/shard_map/ppermute | solution.py:235
  64.7 0.0 collective-permute-done.4.refs_3_.refs_4_
  64.8 1.9 %collective-permute-start.5 = (f32[2,64,1024]{2,1,0:T(8,128)}, f32[2,64,1024]{2,1,0:T(8,128)}, u32[]{:S(2)}, u32[]{:S(2)}) collective-permute-start(f32[2,64,1024]{2,1,0:T(8,128)} %collective-permute-done.4.refs_3_.refs_4_), channel_id=1, source_target_pairs={{0,2},{1,31},{2,4},{3,1},{4,6},{5,3},{6,8},{7,5},{8,10},{9,7},{10,... | collective-permute-start | bytes 1572872 | tf_op jit(solution)/shard_map/ppermute | solution.py:232
  66.7 0.0 collective-permute-done.13.refs_10_.refs_13_
  66.7 0.0 copy-done.9
  66.7 2.4 %collective-permute-start.14 = (f32[2,64,1024]{2,1,0:T(8,128)}, f32[2,64,1024]{2,1,0:T(8,128)}, u32[]{:S(2)}, u32[]{:S(2)}) collective-permute-start(f32[2,64,1024]{2,1,0:T(8,128)} %collective-permute-done.13.refs_10_.refs_13_), channel_id=1, source_target_pairs={{0,2},{1,31},{2,4},{3,1},{4,6},{5,3},{6,8},{7,5},{8,10},{9,7},{10,... | collective-permute-start | bytes 1572872 | tf_op jit(solution)/shard_map/ppermute | solution.py:234
  69.2 0.8 concatenate.3.info
  69.9 0.0 collective-permute-done.20
  69.9 2.4 %collective-permute-start = (s32[37]{0:T(128)S(1)}, s32[37]{0:T(128)S(1)}, u32[]{:S(2)}, u32[]{:S(2)}) collective-permute-start(s32[37]{0:T(128)S(1)} %concatenate.3.info), channel_id=1, source_target_pairs={{0,1},{1,0},{2,3},{3,2},{4,5},{5,4},{6,7},{7,6},{8,9},{9,8},{10,11... | collective-permute-start | bytes 452 | tf_op jit(solution)/shard_map/ppermute | solution.py:237
  72.3 0.4 collective-permute-done.21
  72.6 1.2 collective-permute-done.19
  73.9 1.7 %pad_maximum_fusion.u0 = f32[4,2,64,1024]{3,2,1,0:T(8,128)S(1)} fusion(f32[1,2,64,1024]{3,2,1,0:T(8,128)} %bitcast.11, f32[1,2,64,1024]{3,2,1,0:T(8,128)} %bitcast.10, f32[1,2,64,1024]{3,2,1,0:T(8,128)} %bitcast.9, f32[1,2,64,1024]{3,2,1,0:T(8,128)} %bitcast.22), kind=kLoop, calls=%fused_computation | loop fusion | flops 1572864 | bytes 4194304 | tf_op jit(solution)/shard_map/stack | solution.py:235
  75.5 0.0 copy-done.1
  75.5 0.0 copy-done.2
  75.6 0.0 copy-done.3
  75.6 3.1 %collective-permute-start.22 = (f32[4,2,64,1024]{3,2,1,0:T(8,128)S(1)}, f32[4,2,64,1024]{3,2,1,0:T(8,128)S(1)}, u32[]{:S(2)}, u32[]{:S(2)}) collective-permute-start(f32[4,2,64,1024]{3,2,1,0:T(8,128)S(1)} %pad_maximum_fusion.u0), channel_id=1, source_target_pairs={{0,128},{1,33},{32,160},{33,65},{64,192},{65,97},{96,224},{97,1},{... | collective-permute-start | bytes 6291464 | tf_op jit(solution)/shard_map/ppermute | solution.py:236
  78.7 4.4 %collective-permute-start.23 = (f32[4,2,64,1024]{3,2,1,0:T(8,128)S(1)}, f32[4,2,64,1024]{3,2,1,0:T(8,128)S(1)}, u32[]{:S(2)}, u32[]{:S(2)}) collective-permute-start(f32[4,2,64,1024]{3,2,1,0:T(8,128)S(1)} %pad_maximum_fusion.u0), channel_id=1, source_target_pairs={{0,256},{1,65},{32,288},{33,97},{64,320},{65,1},{96,352},{97,33},{... | collective-permute-start | bytes 6291464 | tf_op jit(solution)/shard_map/ppermute | solution.py:236
  83.1 0.0 collective-permute-done.other
  83.1 3.1 %collective-permute-start.24 = (f32[4,2,64,1024]{3,2,1,0:T(8,128)S(1)}, f32[4,2,64,1024]{3,2,1,0:T(8,128)S(1)}, u32[]{:S(2)}, u32[]{:S(2)}) collective-permute-start(f32[4,2,64,1024]{3,2,1,0:T(8,128)S(1)} %pad_maximum_fusion.u0), channel_id=1, source_target_pairs={{0,384},{1,97},{32,416},{33,1},{64,448},{65,33},{96,480},{97,65},{... | collective-permute-start | bytes 6291464 | tf_op jit(solution)/shard_map/ppermute | solution.py:236
  86.2 0.0 collective-permute-done.5.refs_4_.refs_5_
  86.2 1.9 %collective-permute-start.6 = (f32[2,64,1024]{2,1,0:T(8,128)}, f32[2,64,1024]{2,1,0:T(8,128)S(1)}, u32[]{:S(2)}, u32[]{:S(2)}) collective-permute-start(f32[2,64,1024]{2,1,0:T(8,128)} %collective-permute-done.5.refs_4_.refs_5_), channel_id=1, source_target_pairs={{0,2},{1,31},{2,4},{3,1},{4,6},{5,3},{6,8},{7,5},{8,10},{9,7},{10,... | collective-permute-start | bytes 1572872 | tf_op jit(solution)/shard_map/ppermute | solution.py:232
  88.1 0.0 collective-permute-done.14.refs_11_.refs_14_
  88.1 3.5 %collective-permute-start.15 = (f32[2,64,1024]{2,1,0:T(8,128)}, f32[2,64,1024]{2,1,0:T(8,128)S(1)}, u32[]{:S(2)}, u32[]{:S(2)}) collective-permute-start(f32[2,64,1024]{2,1,0:T(8,128)} %collective-permute-done.14.refs_11_.refs_14_), channel_id=1, source_target_pairs={{0,2},{1,31},{2,4},{3,1},{4,6},{5,3},{6,8},{7,5},{8,10},{9,7},{10,... | collective-permute-start | bytes 1572872 | tf_op jit(solution)/shard_map/ppermute | solution.py:234
  91.6 5.0 %collective-permute-done.6.refs_5_.refs_6_ = f32[2,64,1024]{2,1,0:T(8,128)S(1)} collective-permute-done((f32[2,64,1024]{2,1,0:T(8,128)}, f32[2,64,1024]{2,1,0:T(8,128)S(1)}, u32[]{:S(2)}, u32[]{:S(2)}) %collective-permute-start.6) | collective-permute-done | bytes 524320 | tf_op jit(solution)/shard_map/ppermute | solution.py:232
  96.6 3.1 %collective-permute-start.7 = (f32[2,64,1024]{2,1,0:T(8,128)S(1)}, f32[2,64,1024]{2,1,0:T(8,128)S(1)}, u32[]{:S(2)}, u32[]{:S(2)}) collective-permute-start(f32[2,64,1024]{2,1,0:T(8,128)S(1)} %collective-permute-done.6.refs_5_.refs_6_), channel_id=1, source_target_pairs={{0,2},{1,31},{2,4},{3,1},{4,6},{5,3},{6,8},{7,5},{8,10},{9,7},{10,... | collective-permute-start | bytes 1572872 | tf_op jit(solution)/shard_map/ppermute | solution.py:232
  99.7 2.5 %collective-permute-done.15.refs_12_.refs_15_ = f32[2,64,1024]{2,1,0:T(8,128)S(1)} collective-permute-done((f32[2,64,1024]{2,1,0:T(8,128)}, f32[2,64,1024]{2,1,0:T(8,128)S(1)}, u32[]{:S(2)}, u32[]{:S(2)}) %collective-permute-start.15) | collective-permute-done | bytes 524320 | tf_op jit(solution)/shard_map/ppermute | solution.py:234
  102.2 3.1 %collective-permute-start.16 = (f32[2,64,1024]{2,1,0:T(8,128)S(1)}, f32[2,64,1024]{2,1,0:T(8,128)S(1)}, u32[]{:S(2)}, u32[]{:S(2)}) collective-permute-start(f32[2,64,1024]{2,1,0:T(8,128)S(1)} %collective-permute-done.15.refs_12_.refs_15_), channel_id=1, source_target_pairs={{0,2},{1,31},{2,4},{3,1},{4,6},{5,3},{6,8},{7,5},{8,10},{9,7},{10,... | collective-permute-start | bytes 1572872 | tf_op jit(solution)/shard_map/ppermute | solution.py:234
  105.4 2.5 %collective-permute-done.7.refs_6_.refs_7_ = f32[2,64,1024]{2,1,0:T(8,128)S(1)} collective-permute-done((f32[2,64,1024]{2,1,0:T(8,128)S(1)}, f32[2,64,1024]{2,1,0:T(8,128)S(1)}, u32[]{:S(2)}, u32[]{:S(2)}) %collective-permute-start.7) | collective-permute-done | bytes 524320 | tf_op jit(solution)/shard_map/ppermute | solution.py:232
  107.8 5.6 %collective-permute-done.16.refs_13_.refs_16_ = f32[2,64,1024]{2,1,0:T(8,128)S(1)} collective-permute-done((f32[2,64,1024]{2,1,0:T(8,128)S(1)}, f32[2,64,1024]{2,1,0:T(8,128)S(1)}, u32[]{:S(2)}, u32[]{:S(2)}) %collective-permute-start.16) | collective-permute-done | bytes 524320 | tf_op jit(solution)/shard_map/ppermute | solution.py:234
  113.5 2.7 %shard_map.77 = f32[4,2,64,1024]{3,2,1,0:T(8,128)S(1)} custom-call(s32[37]{0:T(128)S(1)} %concatenate.3.info, s32[37]{0:T(128)S(1)} %collective-permute-done.other, f32[2,64,1024]{2,1,0:T(8,128)} %copy-done.1, f32[2,64,1024]{2,1,0:T(8,128)} %copy-done.3, f32[2,64,1024]{2,1,0:T(8,128)} %copy-done.5, f32[2,64,1024]{2,1,0:T(8,128)} %collective-permute-done.4.refs_3_.refs_4_, ...), custom_call_target="tpu_custom_call" | custom-call | tf_op jit(solution)/shard_map/pallas_call | solution.py:250
  116.2 0.0 copy-start
  116.2 6.8 %collective-permute-start.17 = (f32[4,2,64,1024]{3,2,1,0:T(8,128)S(1)}, f32[4,2,64,1024]{3,2,1,0:T(8,128)S(1)}, u32[]{:S(2)}, u32[]{:S(2)}) collective-permute-start(f32[4,2,64,1024]{3,2,1,0:T(8,128)S(1)} %shard_map.77), channel_id=1, source_target_pairs={{0,1},{1,0},{2,3},{3,2},{4,5},{5,4},{6,7},{7,6},{8,9},{9,8},{10,11... | collective-permute-start | bytes 6291464 | tf_op jit(solution)/shard_map/ppermute | solution.py:250
  123.0 0.0 collective-permute-done.22.u1
  123.0 4.3 %collective-permute-done.23.u2 = f32[4,2,64,1024]{3,2,1,0:T(8,128)S(1)} collective-permute-done((f32[4,2,64,1024]{3,2,1,0:T(8,128)S(1)}, f32[4,2,64,1024]{3,2,1,0:T(8,128)S(1)}, u32[]{:S(2)}, u32[]{:S(2)}) %collective-permute-start.23) | collective-permute-done | bytes 2097184 | tf_op jit(solution)/shard_map/ppermute | solution.py:236
  127.3 1.6 collective-permute-done.24.u3
  128.9 0.7 shard_map.78
  129.6 4.7 %collective-permute-start.25 = (f32[2,2,64,1024]{3,2,1,0:T(8,128)S(1)}, f32[2,2,64,1024]{3,2,1,0:T(8,128)S(1)}, u32[]{:S(2)}, u32[]{:S(2)}) collective-permute-start(f32[2,2,64,1024]{3,2,1,0:T(8,128)S(1)} %shard_map.78), channel_id=1, source_target_pairs={{0,1},{1,0},{2,3},{3,2},{4,5},{5,4},{6,7},{7,6},{8,9},{9,8},{10,11... | collective-permute-start | bytes 3145736 | tf_op jit(solution)/shard_map/ppermute | solution.py:247
  134.3 4.9 %collective-permute-start.8 = (f32[2,64,1024]{2,1,0:T(8,128)S(1)}, f32[2,64,1024]{2,1,0:T(8,128)S(1)}, u32[]{:S(2)}, u32[]{:S(2)}) collective-permute-start(f32[2,64,1024]{2,1,0:T(8,128)S(1)} %collective-permute-done.7.refs_6_.refs_7_), channel_id=1, source_target_pairs={{0,2},{1,31},{2,4},{3,1},{4,6},{5,3},{6,8},{7,5},{8,10},{9,7},{10,... | collective-permute-start | bytes 1572872 | tf_op jit(solution)/shard_map/ppermute | solution.py:232
  139.2 6.1 %collective-permute-done.8.refs_8_ = f32[2,64,1024]{2,1,0:T(8,128)S(1)} collective-permute-done((f32[2,64,1024]{2,1,0:T(8,128)S(1)}, f32[2,64,1024]{2,1,0:T(8,128)S(1)}, u32[]{:S(2)}, u32[]{:S(2)}) %collective-permute-start.8) | collective-permute-done | bytes 524320 | tf_op jit(solution)/shard_map/ppermute | solution.py:232
  145.3 3.2 %collective-permute-start.18 = (f32[2,64,1024]{2,1,0:T(8,128)S(1)}, f32[2,64,1024]{2,1,0:T(8,128)S(1)}, u32[]{:S(2)}, u32[]{:S(2)}) collective-permute-start(f32[2,64,1024]{2,1,0:T(8,128)S(1)} %collective-permute-done.8.refs_8_), channel_id=1, source_target_pairs={{0,1},{1,0},{2,3},{3,2},{4,5},{5,4},{6,7},{7,6},{8,9},{9,8},{10,11... | collective-permute-start | bytes 1572872 | tf_op jit(solution)/shard_map/ppermute | solution.py:251
  148.5 0.0 collective-permute-done.25.up_in
  148.5 1.5 shard_map.79
  150.0 0.0 collective-permute-done.18.refs_18_
  150.0 0.0 collective-permute-done.17.refs_17_
  150.0 7.5 %shard_map.80 = (f32[64,1024]{1,0:T(8,128)}, f32[64,1024]{1,0:T(8,128)}) custom-call(s32[37]{0:T(128)S(1)} %concatenate.3.info, s32[37]{0:T(128)S(1)} %collective-permute-done.other, f32[2,64,1024]{2,1,0:T(8,128)} %bitcast.18, f32[2,64,1024]{2,1,0:T(8,128)} %copy-done.1, f32[2,64,1024]{2,1,0:T(8,128)} %copy-done.3, f32[2,64,1024]{2,1,0:T(8,128)} %copy-done.5, ...), custom_call_target="tpu_custom_call" | custom-call | tf_op jit(solution)/shard_map/pallas_call | solution.py:261
  (14 shorter events, 0.0 us)
Async XLA Ops:
  0.6 14.5 %collective-permute-start.9 = (f32[2,64,1024]{2,1,0:T(8,128)}, f32[2,64,1024]{2,1,0:T(8,128)S(1)}, u32[]{:S(2)}, u32[]{:S(2)}) collective-permute-start(f32[2,64,1024]{2,1,0:T(8,128)} %bitcast.16), channel_id=1, source_target_pairs={{0,1},{1,0},{2,3},{3,2},{4,5},{5,4},{6,7},{7,6},{8,9},{9,8},{10,11... | collective-permute-start | bytes 1572872 | tf_op jit(solution)/shard_map/ppermute | solution.py:227
  9.4 12.2 %collective-permute-start.1 = (f32[2,64,1024]{2,1,0:T(8,128)}, f32[2,64,1024]{2,1,0:T(8,128)S(1)}, u32[]{:S(2)}, u32[]{:S(2)}) collective-permute-start(f32[2,64,1024]{2,1,0:T(8,128)} %bitcast.17), channel_id=1, source_target_pairs={{0,2},{1,31},{2,4},{3,1},{4,6},{5,3},{6,8},{7,5},{8,10},{9,7},{10,... | collective-permute-start | bytes 1572872 | tf_op jit(solution)/shard_map/ppermute | solution.py:232
  15.2 51.5 %copy-start.9 = (f32[2,64,1024]{2,1,0:T(8,128)}, f32[2,64,1024]{2,1,0:T(8,128)S(1)}, u32[]{:S(2)}) copy-start(f32[2,64,1024]{2,1,0:T(8,128)S(1)} %collective-permute-done.9.refs_9_) | copy-start | bytes 1572868
  15.2 11.9 %collective-permute-start.10 = (f32[2,64,1024]{2,1,0:T(8,128)S(1)}, f32[2,64,1024]{2,1,0:T(8,128)S(1)}, u32[]{:S(2)}, u32[]{:S(2)}) collective-permute-start(f32[2,64,1024]{2,1,0:T(8,128)S(1)} %collective-permute-done.9.refs_9_), channel_id=1, source_target_pairs={{0,2},{1,31},{2,4},{3,1},{4,6},{5,3},{6,8},{7,5},{8,10},{9,7},{10,... | collective-permute-start | bytes 1572872 | tf_op jit(solution)/shard_map/ppermute | solution.py:234
  21.6 53.9 %copy-start.1 = (f32[2,64,1024]{2,1,0:T(8,128)}, f32[2,64,1024]{2,1,0:T(8,128)S(1)}, u32[]{:S(2)}) copy-start(f32[2,64,1024]{2,1,0:T(8,128)S(1)} %collective-permute-done.1.refs_0_.refs_1_) | copy-start | bytes 1572868
  21.6 11.1 %collective-permute-start.2 = (f32[2,64,1024]{2,1,0:T(8,128)S(1)}, f32[2,64,1024]{2,1,0:T(8,128)S(1)}, u32[]{:S(2)}, u32[]{:S(2)}) collective-permute-start(f32[2,64,1024]{2,1,0:T(8,128)S(1)} %collective-permute-done.1.refs_0_.refs_1_), channel_id=1, source_target_pairs={{0,2},{1,31},{2,4},{3,1},{4,6},{5,3},{6,8},{7,5},{8,10},{9,7},{10,... | collective-permute-start | bytes 1572872 | tf_op jit(solution)/shard_map/ppermute | solution.py:232
  27.1 48.4 %copy-start.2 = (f32[2,64,1024]{2,1,0:T(8,128)}, f32[2,64,1024]{2,1,0:T(8,128)S(1)}, u32[]{:S(2)}) copy-start(f32[2,64,1024]{2,1,0:T(8,128)S(1)} %collective-permute-done.10.refs_7_.refs_10_) | copy-start | bytes 1572868
  27.1 11.2 %collective-permute-start.11 = (f32[2,64,1024]{2,1,0:T(8,128)S(1)}, f32[2,64,1024]{2,1,0:T(8,128)S(1)}, u32[]{:S(2)}, u32[]{:S(2)}) collective-permute-start(f32[2,64,1024]{2,1,0:T(8,128)S(1)} %collective-permute-done.10.refs_7_.refs_10_), channel_id=1, source_target_pairs={{0,2},{1,31},{2,4},{3,1},{4,6},{5,3},{6,8},{7,5},{8,10},{9,7},{10,... | collective-permute-start | bytes 1572872 | tf_op jit(solution)/shard_map/ppermute | solution.py:234
  32.7 42.8 %copy-start.3 = (f32[2,64,1024]{2,1,0:T(8,128)}, f32[2,64,1024]{2,1,0:T(8,128)S(1)}, u32[]{:S(2)}) copy-start(f32[2,64,1024]{2,1,0:T(8,128)S(1)} %collective-permute-done.2.refs_1_.refs_2_) | copy-start | bytes 1572868
  32.7 11.2 %collective-permute-start.3 = (f32[2,64,1024]{2,1,0:T(8,128)S(1)}, f32[2,64,1024]{2,1,0:T(8,128)S(1)}, u32[]{:S(2)}, u32[]{:S(2)}) collective-permute-start(f32[2,64,1024]{2,1,0:T(8,128)S(1)} %collective-permute-done.2.refs_1_.refs_2_), channel_id=1, source_target_pairs={{0,2},{1,31},{2,4},{3,1},{4,6},{5,3},{6,8},{7,5},{8,10},{9,7},{10,... | collective-permute-start | bytes 1572872 | tf_op jit(solution)/shard_map/ppermute | solution.py:232
  38.3 37.2 %copy-start.4 = (f32[2,64,1024]{2,1,0:T(8,128)}, f32[2,64,1024]{2,1,0:T(8,128)S(1)}, u32[]{:S(2)}) copy-start(f32[2,64,1024]{2,1,0:T(8,128)S(1)} %collective-permute-done.11.refs_8_.refs_11_) | copy-start | bytes 1572868
  38.3 11.2 %collective-permute-start.12 = (f32[2,64,1024]{2,1,0:T(8,128)S(1)}, f32[2,64,1024]{2,1,0:T(8,128)S(1)}, u32[]{:S(2)}, u32[]{:S(2)}) collective-permute-start(f32[2,64,1024]{2,1,0:T(8,128)S(1)} %collective-permute-done.11.refs_8_.refs_11_), channel_id=1, source_target_pairs={{0,2},{1,31},{2,4},{3,1},{4,6},{5,3},{6,8},{7,5},{8,10},{9,7},{10,... | collective-permute-start | bytes 1572872 | tf_op jit(solution)/shard_map/ppermute | solution.py:234
  44.0 31.6 %copy-start.5 = (f32[2,64,1024]{2,1,0:T(8,128)}, f32[2,64,1024]{2,1,0:T(8,128)S(1)}, u32[]{:S(2)}) copy-start(f32[2,64,1024]{2,1,0:T(8,128)S(1)} %collective-permute-done.3.refs_2_.refs_3_) | copy-start | bytes 1572868
  44.0 20.8 %collective-permute-start.4 = (f32[2,64,1024]{2,1,0:T(8,128)S(1)}, f32[2,64,1024]{2,1,0:T(8,128)}, u32[]{:S(2)}, u32[]{:S(2)}) collective-permute-start(f32[2,64,1024]{2,1,0:T(8,128)S(1)} %collective-permute-done.3.refs_2_.refs_3_), channel_id=1, source_target_pairs={{0,2},{1,31},{2,4},{3,1},{4,6},{5,3},{6,8},{7,5},{8,10},{9,7},{10,... | collective-permute-start | bytes 1572872 | tf_op jit(solution)/shard_map/ppermute | solution.py:232
  49.6 26.0 %copy-start.6 = (f32[2,64,1024]{2,1,0:T(8,128)}, f32[2,64,1024]{2,1,0:T(8,128)S(1)}, u32[]{:S(2)}) copy-start(f32[2,64,1024]{2,1,0:T(8,128)S(1)} %collective-permute-done.12.refs_9_.refs_12_) | copy-start | bytes 1572868
  49.6 17.1 %collective-permute-start.13 = (f32[2,64,1024]{2,1,0:T(8,128)S(1)}, f32[2,64,1024]{2,1,0:T(8,128)}, u32[]{:S(2)}, u32[]{:S(2)}) collective-permute-start(f32[2,64,1024]{2,1,0:T(8,128)S(1)} %collective-permute-done.12.refs_9_.refs_12_), channel_id=1, source_target_pairs={{0,2},{1,31},{2,4},{3,1},{4,6},{5,3},{6,8},{7,5},{8,10},{9,7},{10,... | collective-permute-start | bytes 1572872 | tf_op jit(solution)/shard_map/ppermute | solution.py:234
  54.6 15.3 %collective-permute-start.20 = (f32[2,64,1024]{2,1,0:T(8,128)}, f32[2,64,1024]{2,1,0:T(8,128)}, u32[]{:S(2)}, u32[]{:S(2)}) collective-permute-start(f32[2,64,1024]{2,1,0:T(8,128)} %bitcast.19), channel_id=1, source_target_pairs={{0,64},{1,257},{32,96},{33,289},{64,0},{65,321},{96,32},{97,353},{... | collective-permute-start | bytes 1572872 | tf_op jit(solution)/shard_map/ppermute | solution.py:235
  59.4 13.2 %collective-permute-start.21 = (f32[2,64,1024]{2,1,0:T(8,128)}, f32[2,64,1024]{2,1,0:T(8,128)}, u32[]{:S(2)}, u32[]{:S(2)}) collective-permute-start(f32[2,64,1024]{2,1,0:T(8,128)} %bitcast.20), channel_id=1, source_target_pairs={{0,96},{1,385},{32,0},{33,417},{64,32},{65,449},{96,64},{97,481},{... | collective-permute-start | bytes 1572872 | tf_op jit(solution)/shard_map/ppermute | solution.py:235
  62.1 11.7 %collective-permute-start.19 = (f32[2,64,1024]{2,1,0:T(8,128)}, f32[2,64,1024]{2,1,0:T(8,128)}, u32[]{:S(2)}, u32[]{:S(2)}) collective-permute-start(f32[2,64,1024]{2,1,0:T(8,128)} %bitcast.21), channel_id=1, source_target_pairs={{0,32},{1,129},{32,64},{33,161},{64,96},{65,193},{96,0},{97,225},{... | collective-permute-start | bytes 1572872 | tf_op jit(solution)/shard_map/ppermute | solution.py:235
  64.8 21.4 %collective-permute-start.5 = (f32[2,64,1024]{2,1,0:T(8,128)}, f32[2,64,1024]{2,1,0:T(8,128)}, u32[]{:S(2)}, u32[]{:S(2)}) collective-permute-start(f32[2,64,1024]{2,1,0:T(8,128)} %collective-permute-done.4.refs_3_.refs_4_), channel_id=1, source_target_pairs={{0,2},{1,31},{2,4},{3,1},{4,6},{5,3},{6,8},{7,5},{8,10},{9,7},{10,... | collective-permute-start | bytes 1572872 | tf_op jit(solution)/shard_map/ppermute | solution.py:232
  66.7 21.4 %collective-permute-start.14 = (f32[2,64,1024]{2,1,0:T(8,128)}, f32[2,64,1024]{2,1,0:T(8,128)}, u32[]{:S(2)}, u32[]{:S(2)}) collective-permute-start(f32[2,64,1024]{2,1,0:T(8,128)} %collective-permute-done.13.refs_10_.refs_13_), channel_id=1, source_target_pairs={{0,2},{1,31},{2,4},{3,1},{4,6},{5,3},{6,8},{7,5},{8,10},{9,7},{10,... | collective-permute-start | bytes 1572872 | tf_op jit(solution)/shard_map/ppermute | solution.py:234
  69.9 13.2 %collective-permute-start = (s32[37]{0:T(128)S(1)}, s32[37]{0:T(128)S(1)}, u32[]{:S(2)}, u32[]{:S(2)}) collective-permute-start(s32[37]{0:T(128)S(1)} %concatenate.3.info), channel_id=1, source_target_pairs={{0,1},{1,0},{2,3},{3,2},{4,5},{5,4},{6,7},{7,6},{8,9},{9,8},{10,11... | collective-permute-start | bytes 452 | tf_op jit(solution)/shard_map/ppermute | solution.py:237
  75.6 47.4 %collective-permute-start.22 = (f32[4,2,64,1024]{3,2,1,0:T(8,128)S(1)}, f32[4,2,64,1024]{3,2,1,0:T(8,128)S(1)}, u32[]{:S(2)}, u32[]{:S(2)}) collective-permute-start(f32[4,2,64,1024]{3,2,1,0:T(8,128)S(1)} %pad_maximum_fusion.u0), channel_id=1, source_target_pairs={{0,128},{1,33},{32,160},{33,65},{64,192},{65,97},{96,224},{97,1},{... | collective-permute-start | bytes 6291464 | tf_op jit(solution)/shard_map/ppermute | solution.py:236
  78.7 48.6 %collective-permute-start.23 = (f32[4,2,64,1024]{3,2,1,0:T(8,128)S(1)}, f32[4,2,64,1024]{3,2,1,0:T(8,128)S(1)}, u32[]{:S(2)}, u32[]{:S(2)}) collective-permute-start(f32[4,2,64,1024]{3,2,1,0:T(8,128)S(1)} %pad_maximum_fusion.u0), channel_id=1, source_target_pairs={{0,256},{1,65},{32,288},{33,97},{64,320},{65,1},{96,352},{97,33},{... | collective-permute-start | bytes 6291464 | tf_op jit(solution)/shard_map/ppermute | solution.py:236
  83.1 45.8 %collective-permute-start.24 = (f32[4,2,64,1024]{3,2,1,0:T(8,128)S(1)}, f32[4,2,64,1024]{3,2,1,0:T(8,128)S(1)}, u32[]{:S(2)}, u32[]{:S(2)}) collective-permute-start(f32[4,2,64,1024]{3,2,1,0:T(8,128)S(1)} %pad_maximum_fusion.u0), channel_id=1, source_target_pairs={{0,384},{1,97},{32,416},{33,1},{64,448},{65,33},{96,480},{97,65},{... | collective-permute-start | bytes 6291464 | tf_op jit(solution)/shard_map/ppermute | solution.py:236
  86.2 10.4 %collective-permute-start.6 = (f32[2,64,1024]{2,1,0:T(8,128)}, f32[2,64,1024]{2,1,0:T(8,128)S(1)}, u32[]{:S(2)}, u32[]{:S(2)}) collective-permute-start(f32[2,64,1024]{2,1,0:T(8,128)} %collective-permute-done.5.refs_4_.refs_5_), channel_id=1, source_target_pairs={{0,2},{1,31},{2,4},{3,1},{4,6},{5,3},{6,8},{7,5},{8,10},{9,7},{10,... | collective-permute-start | bytes 1572872 | tf_op jit(solution)/shard_map/ppermute | solution.py:232
  88.1 14.1 %collective-permute-start.15 = (f32[2,64,1024]{2,1,0:T(8,128)}, f32[2,64,1024]{2,1,0:T(8,128)S(1)}, u32[]{:S(2)}, u32[]{:S(2)}) collective-permute-start(f32[2,64,1024]{2,1,0:T(8,128)} %collective-permute-done.14.refs_11_.refs_14_), channel_id=1, source_target_pairs={{0,2},{1,31},{2,4},{3,1},{4,6},{5,3},{6,8},{7,5},{8,10},{9,7},{10,... | collective-permute-start | bytes 1572872 | tf_op jit(solution)/shard_map/ppermute | solution.py:234
  96.6 16.9 %copy-start.7 = (f32[2,64,1024]{2,1,0:T(8,128)}, f32[2,64,1024]{2,1,0:T(8,128)S(1)}, u32[]{:S(2)}) copy-start(f32[2,64,1024]{2,1,0:T(8,128)S(1)} %collective-permute-done.6.refs_5_.refs_6_) | copy-start | bytes 1572868
  96.6 11.2 %collective-permute-start.7 = (f32[2,64,1024]{2,1,0:T(8,128)S(1)}, f32[2,64,1024]{2,1,0:T(8,128)S(1)}, u32[]{:S(2)}, u32[]{:S(2)}) collective-permute-start(f32[2,64,1024]{2,1,0:T(8,128)S(1)} %collective-permute-done.6.refs_5_.refs_6_), channel_id=1, source_target_pairs={{0,2},{1,31},{2,4},{3,1},{4,6},{5,3},{6,8},{7,5},{8,10},{9,7},{10,... | collective-permute-start | bytes 1572872 | tf_op jit(solution)/shard_map/ppermute | solution.py:232
  102.2 11.2 %copy-start.8 = (f32[2,64,1024]{2,1,0:T(8,128)}, f32[2,64,1024]{2,1,0:T(8,128)S(1)}, u32[]{:S(2)}) copy-start(f32[2,64,1024]{2,1,0:T(8,128)S(1)} %collective-permute-done.15.refs_12_.refs_15_) | copy-start | bytes 1572868
  102.2 11.2 %collective-permute-start.16 = (f32[2,64,1024]{2,1,0:T(8,128)S(1)}, f32[2,64,1024]{2,1,0:T(8,128)S(1)}, u32[]{:S(2)}, u32[]{:S(2)}) collective-permute-start(f32[2,64,1024]{2,1,0:T(8,128)S(1)} %collective-permute-done.15.refs_12_.refs_15_), channel_id=1, source_target_pairs={{0,2},{1,31},{2,4},{3,1},{4,6},{5,3},{6,8},{7,5},{8,10},{9,7},{10,... | collective-permute-start | bytes 1572872 | tf_op jit(solution)/shard_map/ppermute | solution.py:234
  116.2 32.3 %copy-start = (f32[1,1,2,64,1024]{4,3,2,1,0:T(8,128)S(1)}, f32[1,1,2,64,1024]{4,3,2,1,0:T(8,128)}, u32[]{:S(2)}) copy-start(f32[1,1,2,64,1024]{4,3,2,1,0:T(8,128)} %param.11) | copy-start | bytes 1572868
  116.2 33.8 %collective-permute-start.17 = (f32[4,2,64,1024]{3,2,1,0:T(8,128)S(1)}, f32[4,2,64,1024]{3,2,1,0:T(8,128)S(1)}, u32[]{:S(2)}, u32[]{:S(2)}) collective-permute-start(f32[4,2,64,1024]{3,2,1,0:T(8,128)S(1)} %shard_map.77), channel_id=1, source_target_pairs={{0,1},{1,0},{2,3},{3,2},{4,5},{5,4},{6,7},{7,6},{8,9},{9,8},{10,11... | collective-permute-start | bytes 6291464 | tf_op jit(solution)/shard_map/ppermute | solution.py:250
  129.6 18.9 %collective-permute-start.25 = (f32[2,2,64,1024]{3,2,1,0:T(8,128)S(1)}, f32[2,2,64,1024]{3,2,1,0:T(8,128)S(1)}, u32[]{:S(2)}, u32[]{:S(2)}) collective-permute-start(f32[2,2,64,1024]{3,2,1,0:T(8,128)S(1)} %shard_map.78), channel_id=1, source_target_pairs={{0,1},{1,0},{2,3},{3,2},{4,5},{5,4},{6,7},{7,6},{8,9},{9,8},{10,11... | collective-permute-start | bytes 3145736 | tf_op jit(solution)/shard_map/ppermute | solution.py:247
  134.3 11.0 %collective-permute-start.8 = (f32[2,64,1024]{2,1,0:T(8,128)S(1)}, f32[2,64,1024]{2,1,0:T(8,128)S(1)}, u32[]{:S(2)}, u32[]{:S(2)}) collective-permute-start(f32[2,64,1024]{2,1,0:T(8,128)S(1)} %collective-permute-done.7.refs_6_.refs_7_), channel_id=1, source_target_pairs={{0,2},{1,31},{2,4},{3,1},{4,6},{5,3},{6,8},{7,5},{8,10},{9,7},{10,... | collective-permute-start | bytes 1572872 | tf_op jit(solution)/shard_map/ppermute | solution.py:232
  145.3 4.8 %collective-permute-start.18 = (f32[2,64,1024]{2,1,0:T(8,128)S(1)}, f32[2,64,1024]{2,1,0:T(8,128)S(1)}, u32[]{:S(2)}, u32[]{:S(2)}) collective-permute-start(f32[2,64,1024]{2,1,0:T(8,128)S(1)} %collective-permute-done.8.refs_8_), channel_id=1, source_target_pairs={{0,1},{1,0},{2,3},{3,2},{4,5},{5,4},{6,7},{7,6},{8,9},{9,8},{10,11... | collective-permute-start | bytes 1572872 | tf_op jit(solution)/shard_map/ppermute | solution.py:251

commit v4 on v3

--- a/solution.py
+++ b/solution.py
@@ -14,8 +14,8 @@
 UP_AT, TARGET_AT, ROW_AT, COL_AT, DEPTH_AT = 16, 32, 34, 35, 36
 
 
-def z_shift(n_col):
-    return [(c * 2 + d, ((c + (1 - 2 * d)) % n_col) * 2 + d) for c in range(n_col) for d in (0, 1)]
+def z_shift(n_col, crossing=0):
+    return [(c * 2 + (d ^ crossing), ((c + (1 - 2 * d)) % n_col) * 2 + d) for c in range(n_col) for d in (0, 1)]
 
 
 def xy_shift(step, phase):
@@ -64,20 +64,25 @@
 
 
 def left_choice_kernel(info, other, *refs):
-    own, across, out, sems = refs[:7], refs[7:14], refs[14], refs[15]
+    own, across, out, sems = refs[:8], refs[8:15], refs[15], refs[16]
     tile = info[TARGET_AT + 1 - info[DEPTH_AT]]
     b = tile // CB
     for kind, (table, pieces) in enumerate(((info, own), (other, across))):
         for k in range(KD):
             slot = (1 - kind) * KD + k
             s = ring_steps(info, table[b * KD + k])
-            for i in range(7):
-
-                @pl.when(s == i + 1)
+            for i, piece in enumerate(pieces):
+
+                @pl.when(s == i + kind)
                 def _():
-                    pltpu.make_async_copy(pieces[i], out.at[slot], sems.at[slot]).start()
-
-            @pl.when((s >= 1) & (s <= 7))
+                    pltpu.make_async_copy(piece, out.at[slot], sems.at[slot]).start()
+
+    for kind, (table, pieces) in enumerate(((info, own), (other, across))):
+        for k in range(KD):
+            slot = (1 - kind) * KD + k
+            s = ring_steps(info, table[b * KD + k])
+
+            @pl.when((s >= kind) & (s <= 7))
             def _():
                 pltpu.make_async_copy(pieces[0], out.at[slot], sems.at[slot]).wait()
 
@@ -163,10 +168,10 @@
 
 
 def tile_kernel(info, other, *refs):
-    own, across = refs[:9], refs[9:17]
-    left_in, last_in, ps, qs, tested = refs[17:22]
-    basis_out, weights_out = refs[22:24]
-    xs, ys, left_sems = refs[24:]
+    own, across = refs[:9], refs[9:16]
+    left_in, last_in, ps, qs, tested = refs[16:21]
+    basis_out, weights_out = refs[21:23]
+    xs, ys, left_sems = refs[23:]
     b = info[TARGET_AT + info[DEPTH_AT]] // CB
     slots, n, size = xs.shape
 
@@ -187,10 +192,10 @@
             slot = kind * KD + k
             s = ring_steps(info, table[b * KD + k])
             for i, piece in enumerate(pieces):
-                start(s == i, piece, slot)
+                start(s == i + kind, piece, slot)
             if kind == 1:
                 start(s == 8, last_in, slot)
-            start(s > 8, left_in.at[slot], slot)
+            start((s > 8) | (s < kind), left_in.at[slot], slot)
     for slot in range(slots):
         for copy in copies(own[0], slot):
             copy.wait()
@@ -224,20 +229,18 @@
     pair = own.shape
     places = jnp.stack([lax.axis_index(a).astype(jnp.int32) for a in ("row", "col", "depth")])
     info = jnp.concatenate([left_home[0, 0], up_home[0, 0], targets[0, 0], places])
-    across = lax.ppermute(own, "depth", SWAP)
-    own_pieces, across_pieces = [own], [across]
-    shift = z_shift(n_col)
-    half = n_col // 2
+    axes, shift, half = ("col", "depth"), z_shift(n_col), n_col // 2
+    own_pieces, across_pieces = [own], [lax.ppermute(own, axes, z_shift(n_col, 1))]
     for step in range(1, half + 1):
-        own_pieces.append(lax.ppermute(own_pieces[-1], ("col", "depth"), shift))
-        if step < half:
-            across_pieces.append(lax.ppermute(across_pieces[-1], ("col", "depth"), shift))
+        own_pieces.append(lax.ppermute(own_pieces[-1], axes, shift))
+        if 1 < step < half:
+            across_pieces.append(lax.ppermute(across_pieces[-1], axes, shift))
     block = jnp.stack([up] + [lax.ppermute(up, ("row", "depth"), xy_shift(s, 0)) for s in range(1, SIDE)])
     ups = [block] + [lax.ppermute(block, ("row", "depth"), xy_shift(s, 1)) for s in range(1, SIDE)]
     other = lax.ppermute(info, "depth", SWAP)
 
-    early = lambda pieces: [pltpu.with_memory_space_constraint(x, pltpu.HBM) for x in pieces[:7]] + pieces[7:]
-    own_held, across_held = early(own_pieces), early(across_pieces)
+    early = lambda pieces, n: [pltpu.with_memory_space_constraint(x, pltpu.HBM) for x in pieces[:n]] + pieces[n:]
+    own_held, across_held = early(own_pieces, 7), early(across_pieces, 6)
     f32 = jnp.float32
     smem, hbm, vmem = pltpu.SMEM, pltpu.HBM, pltpu.VMEM
     slots = 2 * KD
@@ -246,8 +249,8 @@
     up_choice = local_kernel(up_choice_kernel, [smem] + [hbm] * SIDE, choice, hbm, [dma((KD,))])
     up_in = lax.ppermute(up_choice(info, *ups), "depth", SWAP)
     choice = jax.ShapeDtypeStruct((slots, *pair), f32)
-    left_choice = local_kernel(left_choice_kernel, [smem] * 2 + [hbm] * 14, choice, hbm, [dma((slots,))])
-    left_in = lax.ppermute(left_choice(info, other, *own_held[1:8], *across_held[1:8]), "depth", SWAP)
+    left_choice = local_kernel(left_choice_kernel, [smem] * 2 + [hbm] * 15, choice, hbm, [dma((slots,))])
+    left_in = lax.ppermute(left_choice(info, other, *own_held[:8], *across_held), "depth", SWAP)
     last_in = lax.ppermute(own_pieces[8], "depth", SWAP)
 
     flat = pair[1:]
@@ -257,7 +260,7 @@
     up_part = local_kernel(up_kernel, [smem] + [hbm] * (SIDE + 2), (stack, stack, square), vmem, scratch, 6)
     up_sides = up_part(info, *ups, up_in, test)
     scratch = [vmem(stack.shape, f32)] * 2 + [dma((slots, 2))]
-    whole = local_kernel(tile_kernel, [smem] * 2 + [hbm] * 19 + [vmem] * 3, (tile, tile), vmem, scratch, 12)
+    whole = local_kernel(tile_kernel, [smem] * 2 + [hbm] * 18 + [vmem] * 3, (tile, tile), vmem, scratch, 12)
     basis, weights = whole(info, other, *own_held, *across_held, left_in, last_in, *up_sides)
     return basis[None, None, None], weights[None, None, None]
 

time: 159 us -> 160 us (level)
  starting transfers between devices: 106 us -> 113 us
  waiting for transfers between devices: 36 us -> 31.4 us
    ppermute x17 -> x16, starting transfers between devices: 74.7 us -> 78.4 us  [the longest x8 42.7 us: pieces_and_tile(): own_pieces.append(lax.ppermute(own_pieces[-1], axes, shift))]
    ppermute x1, starting transfers between devices: 2.36 us -> 5.08 us  [pieces_and_tile(): other = lax.ppermute(info, 'depth', SWAP)]
    ppermute x17 -> x16, waiting for transfers between devices: 28.5 us -> 27.1 us  [the longest x8 19.8 us: pieces_and_tile(): own_pieces.append(lax.ppermute(own_pieces[-1], axes, shift))]
  transfers between devices with their start and end apart: 26 -> 25, of which waited for: 15 -> 12; matrix products, arithmetic and copies ran while one was open for 2% -> 2% of each run, Pallas kernels for 3% -> 3%
where the time goes in v4:
time: 160 us; the launch traced here: 159 us
  starting transfers between devices  113 us (71%)
  waiting for transfers between devices  31.4 us (20%)
  Pallas kernels  11.5 us (7%)
  other arithmetic  1.65 us (1%)
    ppermute x8, starting transfers between devices, pieces_and_tile(): own_pieces.append(lax.ppermute(own_pieces[-1], axes, shift))  42.7 us
    ppermute x6, starting transfers between devices, pieces_and_tile(): across_pieces.append(lax.ppermute(across_pieces[-1], axes, shift))  23.9 us
    ppermute x8, waiting for transfers between devices, pieces_and_tile(): own_pieces.append(lax.ppermute(own_pieces[-1], axes, shift))  19.8 us
    ppermute x3, starting transfers between devices, pieces_and_tile(): lax.ppermute(up, ('row', 'depth'), xy_shift(s, 0))  10.1 us
    ppermute x3, starting transfers between devices, pieces_and_tile(): lax.ppermute(block, ('row', 'depth'), xy_shift(s, 1))  9.91 us
    ppermute x1, starting transfers between devices, pieces_and_tile(): lax.ppermute(left_choice(info, other, *own_held[:8], *across_held), 'dept...  9.85 us
    pallas_call x1, Pallas kernels, pieces_and_tile(): whole(info, other, *own_held, *across_held, left_in, last_in, *up_sides)  7.49 us
    ppermute x6, waiting for transfers between devices, pieces_and_tile(): across_pieces.append(lax.ppermute(across_pieces[-1], axes, shift))  7.29 us
  transfers between devices with their start and end apart: 25, of which 12 were waited for; matrix products, arithmetic and copies ran while one was open for 2% of the time, Pallas kernels for 3%

profile of v4, /device:TPU:1, one launch (start us, length us, event | category | flops | bytes accessed | tf_op | source)
XLA Modules:
  0.0 159.4 jit_solution(5006519417134199955)
XLA Ops:
  0.6 11.9 %collective-permute-start.1 = (f32[2,64,1024]{2,1,0:T(8,128)}, f32[2,64,1024]{2,1,0:T(8,128)S(1)}, u32[]{:S(2)}, u32[]{:S(2)}) collective-permute-start(f32[2,64,1024]{2,1,0:T(8,128)} %bitcast.16), channel_id=1, source_target_pairs={{0,2},{1,31},{2,4},{3,1},{4,6},{5,3},{6,8},{7,5},{8,10},{9,7},{10,... | collective-permute-start | bytes 1572872 | tf_op jit(solution)/shard_map/ppermute | solution.py:235
  12.6 1.9 %collective-permute-start.9 = (f32[2,64,1024]{2,1,0:T(8,128)}, f32[2,64,1024]{2,1,0:T(8,128)S(1)}, u32[]{:S(2)}, u32[]{:S(2)}) collective-permute-start(f32[2,64,1024]{2,1,0:T(8,128)} %bitcast.17), channel_id=1, source_target_pairs={{1,2},{0,31},{3,4},{2,1},{5,6},{4,3},{7,8},{6,5},{9,10},{8,7},{11,... | collective-permute-start | bytes 1572872 | tf_op jit(solution)/shard_map/ppermute | solution.py:233
  14.5 6.9 %collective-permute-done.1.refs_1_ = f32[2,64,1024]{2,1,0:T(8,128)S(1)} collective-permute-done((f32[2,64,1024]{2,1,0:T(8,128)}, f32[2,64,1024]{2,1,0:T(8,128)S(1)}, u32[]{:S(2)}, u32[]{:S(2)}) %collective-permute-start.1) | collective-permute-done | bytes 524320 | tf_op jit(solution)/shard_map/ppermute | solution.py:235
  21.4 4.9 %collective-permute-start.2 = (f32[2,64,1024]{2,1,0:T(8,128)S(1)}, f32[2,64,1024]{2,1,0:T(8,128)S(1)}, u32[]{:S(2)}, u32[]{:S(2)}) collective-permute-start(f32[2,64,1024]{2,1,0:T(8,128)S(1)} %collective-permute-done.1.refs_1_), channel_id=1, source_target_pairs={{0,2},{1,31},{2,4},{3,1},{4,6},{5,3},{6,8},{7,5},{8,10},{9,7},{10,... | collective-permute-start | bytes 1572872 | tf_op jit(solution)/shard_map/ppermute | solution.py:235
  26.3 0.0 collective-permute-done.9.refs_8_.refs_9_
  26.3 0.0 copy-start.2
  26.3 3.2 %collective-permute-start.10 = (f32[2,64,1024]{2,1,0:T(8,128)S(1)}, f32[2,64,1024]{2,1,0:T(8,128)S(1)}, u32[]{:S(2)}, u32[]{:S(2)}) collective-permute-start(f32[2,64,1024]{2,1,0:T(8,128)S(1)} %collective-permute-done.9.refs_8_.refs_9_), channel_id=1, source_target_pairs={{0,2},{1,31},{2,4},{3,1},{4,6},{5,3},{6,8},{7,5},{8,10},{9,7},{10,... | collective-permute-start | bytes 1572872 | tf_op jit(solution)/shard_map/ppermute | solution.py:237
  29.5 2.9 %collective-permute-done.2.refs_2_ = f32[2,64,1024]{2,1,0:T(8,128)S(1)} collective-permute-done((f32[2,64,1024]{2,1,0:T(8,128)S(1)}, f32[2,64,1024]{2,1,0:T(8,128)S(1)}, u32[]{:S(2)}, u32[]{:S(2)}) %collective-permute-start.2) | collective-permute-done | bytes 524320 | tf_op jit(solution)/shard_map/ppermute | solution.py:235
  32.4 5.0 %collective-permute-start.3 = (f32[2,64,1024]{2,1,0:T(8,128)S(1)}, f32[2,64,1024]{2,1,0:T(8,128)S(1)}, u32[]{:S(2)}, u32[]{:S(2)}) collective-permute-start(f32[2,64,1024]{2,1,0:T(8,128)S(1)} %collective-permute-done.2.refs_2_), channel_id=1, source_target_pairs={{0,2},{1,31},{2,4},{3,1},{4,6},{5,3},{6,8},{7,5},{8,10},{9,7},{10,... | collective-permute-start | bytes 1572872 | tf_op jit(solution)/shard_map/ppermute | solution.py:235
  37.4 0.6 collective-permute-done.10.refs_9_.refs_10_
  38.0 5.0 %collective-permute-start.11 = (f32[2,64,1024]{2,1,0:T(8,128)S(1)}, f32[2,64,1024]{2,1,0:T(8,128)S(1)}, u32[]{:S(2)}, u32[]{:S(2)}) collective-permute-start(f32[2,64,1024]{2,1,0:T(8,128)S(1)} %collective-permute-done.10.refs_9_.refs_10_), channel_id=1, source_target_pairs={{0,2},{1,31},{2,4},{3,1},{4,6},{5,3},{6,8},{7,5},{8,10},{9,7},{10,... | collective-permute-start | bytes 1572872 | tf_op jit(solution)/shard_map/ppermute | solution.py:237
  43.1 0.6 collective-permute-done.3.refs_3_
  43.7 5.0 %collective-permute-start.4 = (f32[2,64,1024]{2,1,0:T(8,128)S(1)}, f32[2,64,1024]{2,1,0:T(8,128)}, u32[]{:S(2)}, u32[]{:S(2)}) collective-permute-start(f32[2,64,1024]{2,1,0:T(8,128)S(1)} %collective-permute-done.3.refs_3_), channel_id=1, source_target_pairs={{0,2},{1,31},{2,4},{3,1},{4,6},{5,3},{6,8},{7,5},{8,10},{9,7},{10,... | collective-permute-start | bytes 1572872 | tf_op jit(solution)/shard_map/ppermute | solution.py:235
  48.7 0.6 collective-permute-done.11.refs_10_.refs_11_
  49.3 5.0 %collective-permute-start.12 = (f32[2,64,1024]{2,1,0:T(8,128)S(1)}, f32[2,64,1024]{2,1,0:T(8,128)}, u32[]{:S(2)}, u32[]{:S(2)}) collective-permute-start(f32[2,64,1024]{2,1,0:T(8,128)S(1)} %collective-permute-done.11.refs_10_.refs_11_), channel_id=1, source_target_pairs={{0,2},{1,31},{2,4},{3,1},{4,6},{5,3},{6,8},{7,5},{8,10},{9,7},{10,... | collective-permute-start | bytes 1572872 | tf_op jit(solution)/shard_map/ppermute | solution.py:237
  54.3 4.8 %collective-permute-start.19 = (f32[2,64,1024]{2,1,0:T(8,128)}, f32[2,64,1024]{2,1,0:T(8,128)}, u32[]{:S(2)}, u32[]{:S(2)}) collective-permute-start(f32[2,64,1024]{2,1,0:T(8,128)} %bitcast.20), channel_id=1, source_target_pairs={{0,64},{1,257},{32,96},{33,289},{64,0},{65,321},{96,32},{97,353},{... | collective-permute-start | bytes 1572872 | tf_op jit(solution)/shard_map/ppermute | solution.py:238
  59.1 2.7 %collective-permute-start.20 = (f32[2,64,1024]{2,1,0:T(8,128)}, f32[2,64,1024]{2,1,0:T(8,128)}, u32[]{:S(2)}, u32[]{:S(2)}) collective-permute-start(f32[2,64,1024]{2,1,0:T(8,128)} %bitcast.21), channel_id=1, source_target_pairs={{0,96},{1,385},{32,0},{33,417},{64,32},{65,449},{96,64},{97,481},{... | collective-permute-start | bytes 1572872 | tf_op jit(solution)/shard_map/ppermute | solution.py:238
  61.8 2.6 %collective-permute-start.18 = (f32[2,64,1024]{2,1,0:T(8,128)}, f32[2,64,1024]{2,1,0:T(8,128)}, u32[]{:S(2)}, u32[]{:S(2)}) collective-permute-start(f32[2,64,1024]{2,1,0:T(8,128)} %bitcast.22), channel_id=1, source_target_pairs={{0,32},{1,129},{32,64},{33,161},{64,96},{65,193},{96,0},{97,225},{... | collective-permute-start | bytes 1572872 | tf_op jit(solution)/shard_map/ppermute | solution.py:238
  64.4 0.0 collective-permute-done.4.refs_4_
  64.4 1.9 %collective-permute-start.5 = (f32[2,64,1024]{2,1,0:T(8,128)}, f32[2,64,1024]{2,1,0:T(8,128)}, u32[]{:S(2)}, u32[]{:S(2)}) collective-permute-start(f32[2,64,1024]{2,1,0:T(8,128)} %collective-permute-done.4.refs_4_), channel_id=1, source_target_pairs={{0,2},{1,31},{2,4},{3,1},{4,6},{5,3},{6,8},{7,5},{8,10},{9,7},{10,... | collective-permute-start | bytes 1572872 | tf_op jit(solution)/shard_map/ppermute | solution.py:235
  66.4 0.0 collective-permute-done.12.refs_11_.refs_12_
  66.4 1.9 %collective-permute-start.13 = (f32[2,64,1024]{2,1,0:T(8,128)}, f32[2,64,1024]{2,1,0:T(8,128)}, u32[]{:S(2)}, u32[]{:S(2)}) collective-permute-start(f32[2,64,1024]{2,1,0:T(8,128)} %collective-permute-done.12.refs_11_.refs_12_), channel_id=1, source_target_pairs={{0,2},{1,31},{2,4},{3,1},{4,6},{5,3},{6,8},{7,5},{8,10},{9,7},{10,... | collective-permute-start | bytes 1572872 | tf_op jit(solution)/shard_map/ppermute | solution.py:237
  68.3 0.8 concatenate.3.info
  69.1 0.0 collective-permute-done.19
  69.1 5.1 %collective-permute-start = (s32[37]{0:T(128)S(1)}, s32[37]{0:T(128)S(1)}, u32[]{:S(2)}, u32[]{:S(2)}) collective-permute-start(s32[37]{0:T(128)S(1)} %concatenate.3.info), channel_id=1, source_target_pairs={{0,1},{1,0},{2,3},{3,2},{4,5},{5,4},{6,7},{7,6},{8,9},{9,8},{10,11... | collective-permute-start | bytes 452 | tf_op jit(solution)/shard_map/ppermute | solution.py:240
  74.2 0.0 collective-permute-done.20
  74.2 0.0 collective-permute-done.18
  74.2 1.7 %pad_maximum_fusion.u0 = f32[4,2,64,1024]{3,2,1,0:T(8,128)S(1)} fusion(f32[1,2,64,1024]{3,2,1,0:T(8,128)} %bitcast.11, f32[1,2,64,1024]{3,2,1,0:T(8,128)} %bitcast.10, f32[1,2,64,1024]{3,2,1,0:T(8,128)} %bitcast.9, f32[1,2,64,1024]{3,2,1,0:T(8,128)} %bitcast.23), kind=kLoop, calls=%fused_computation | loop fusion | flops 1572864 | bytes 4194304 | tf_op jit(solution)/shard_map/stack | solution.py:238
  75.9 0.0 copy-done.1
  75.9 0.0 copy-done.2
  75.9 0.0 copy-done.3
  75.9 0.0 copy-done.4
  75.9 0.0 copy-done.5
  75.9 0.0 copy-done.6
  75.9 2.5 %collective-permute-start.21 = (f32[4,2,64,1024]{3,2,1,0:T(8,128)S(1)}, f32[4,2,64,1024]{3,2,1,0:T(8,128)S(1)}, u32[]{:S(2)}, u32[]{:S(2)}) collective-permute-start(f32[4,2,64,1024]{3,2,1,0:T(8,128)S(1)} %pad_maximum_fusion.u0), channel_id=1, source_target_pairs={{0,128},{1,33},{32,160},{33,65},{64,192},{65,97},{96,224},{97,1},{... | collective-permute-start | bytes 6291464 | tf_op jit(solution)/shard_map/ppermute | solution.py:239
  78.4 4.6 %collective-permute-start.22 = (f32[4,2,64,1024]{3,2,1,0:T(8,128)S(1)}, f32[4,2,64,1024]{3,2,1,0:T(8,128)S(1)}, u32[]{:S(2)}, u32[]{:S(2)}) collective-permute-start(f32[4,2,64,1024]{3,2,1,0:T(8,128)S(1)} %pad_maximum_fusion.u0), channel_id=1, source_target_pairs={{0,256},{1,65},{32,288},{33,97},{64,320},{65,1},{96,352},{97,33},{... | collective-permute-start | bytes 6291464 | tf_op jit(solution)/shard_map/ppermute | solution.py:239
  83.0 0.0 collective-permute-done.other
  83.0 2.8 %collective-permute-start.23 = (f32[4,2,64,1024]{3,2,1,0:T(8,128)S(1)}, f32[4,2,64,1024]{3,2,1,0:T(8,128)S(1)}, u32[]{:S(2)}, u32[]{:S(2)}) collective-permute-start(f32[4,2,64,1024]{3,2,1,0:T(8,128)S(1)} %pad_maximum_fusion.u0), channel_id=1, source_target_pairs={{0,384},{1,97},{32,416},{33,1},{64,448},{65,33},{96,480},{97,65},{... | collective-permute-start | bytes 6291464 | tf_op jit(solution)/shard_map/ppermute | solution.py:239
  85.9 0.0 collective-permute-done.5.refs_5_
  85.9 3.9 %collective-permute-start.6 = (f32[2,64,1024]{2,1,0:T(8,128)}, f32[2,64,1024]{2,1,0:T(8,128)S(1)}, u32[]{:S(2)}, u32[]{:S(2)}) collective-permute-start(f32[2,64,1024]{2,1,0:T(8,128)} %collective-permute-done.5.refs_5_), channel_id=1, source_target_pairs={{0,2},{1,31},{2,4},{3,1},{4,6},{5,3},{6,8},{7,5},{8,10},{9,7},{10,... | collective-permute-start | bytes 1572872 | tf_op jit(solution)/shard_map/ppermute | solution.py:235
  89.8 0.0 collective-permute-done.13.refs_12_.refs_13_
  89.8 3.6 %collective-permute-start.14 = (f32[2,64,1024]{2,1,0:T(8,128)}, f32[2,64,1024]{2,1,0:T(8,128)S(1)}, u32[]{:S(2)}, u32[]{:S(2)}) collective-permute-start(f32[2,64,1024]{2,1,0:T(8,128)} %collective-permute-done.13.refs_12_.refs_13_), channel_id=1, source_target_pairs={{0,2},{1,31},{2,4},{3,1},{4,6},{5,3},{6,8},{7,5},{8,10},{9,7},{10,... | collective-permute-start | bytes 1572872 | tf_op jit(solution)/shard_map/ppermute | solution.py:237
  93.5 2.8 %collective-permute-done.6.refs_6_ = f32[2,64,1024]{2,1,0:T(8,128)S(1)} collective-permute-done((f32[2,64,1024]{2,1,0:T(8,128)}, f32[2,64,1024]{2,1,0:T(8,128)S(1)}, u32[]{:S(2)}, u32[]{:S(2)}) %collective-permute-start.6) | collective-permute-done | bytes 524320 | tf_op jit(solution)/shard_map/ppermute | solution.py:235
  96.3 5.1 %collective-permute-start.7 = (f32[2,64,1024]{2,1,0:T(8,128)S(1)}, f32[2,64,1024]{2,1,0:T(8,128)S(1)}, u32[]{:S(2)}, u32[]{:S(2)}) collective-permute-start(f32[2,64,1024]{2,1,0:T(8,128)S(1)} %collective-permute-done.6.refs_6_), channel_id=1, source_target_pairs={{0,2},{1,31},{2,4},{3,1},{4,6},{5,3},{6,8},{7,5},{8,10},{9,7},{10,... | collective-permute-start | bytes 1572872 | tf_op jit(solution)/shard_map/ppermute | solution.py:235
  101.4 0.5 collective-permute-done.14.refs_13_.refs_14_
  101.9 5.1 %collective-permute-start.15 = (f32[2,64,1024]{2,1,0:T(8,128)S(1)}, f32[2,64,1024]{2,1,0:T(8,128)S(1)}, u32[]{:S(2)}, u32[]{:S(2)}) collective-permute-start(f32[2,64,1024]{2,1,0:T(8,128)S(1)} %collective-permute-done.14.refs_13_.refs_14_), channel_id=1, source_target_pairs={{0,2},{1,31},{2,4},{3,1},{4,6},{5,3},{6,8},{7,5},{8,10},{9,7},{10,... | collective-permute-start | bytes 1572872 | tf_op jit(solution)/shard_map/ppermute | solution.py:237
  107.1 0.5 collective-permute-done.7.refs_7_
  107.5 5.6 %collective-permute-done.15.refs_14_.refs_15_ = f32[2,64,1024]{2,1,0:T(8,128)S(1)} collective-permute-done((f32[2,64,1024]{2,1,0:T(8,128)S(1)}, f32[2,64,1024]{2,1,0:T(8,128)S(1)}, u32[]{:S(2)}, u32[]{:S(2)}) %collective-permute-start.15) | collective-permute-done | bytes 524320 | tf_op jit(solution)/shard_map/ppermute | solution.py:237
  113.2 1.8 %shard_map.77 = f32[4,2,64,1024]{3,2,1,0:T(8,128)S(1)} custom-call(s32[37]{0:T(128)S(1)} %concatenate.3.info, s32[37]{0:T(128)S(1)} %collective-permute-done.other, f32[2,64,1024]{2,1,0:T(8,128)} %bitcast.18, f32[2,64,1024]{2,1,0:T(8,128)} %copy-done.1, f32[2,64,1024]{2,1,0:T(8,128)} %copy-done.3, f32[2,64,1024]{2,1,0:T(8,128)} %copy-done.5, ...), custom_call_target="tpu_custom_call" | custom-call | tf_op jit(solution)/shard_map/pallas_call | solution.py:253
  115.0 0.0 copy-start
  115.0 9.8 %collective-permute-start.16 = (f32[4,2,64,1024]{3,2,1,0:T(8,128)S(1)}, f32[4,2,64,1024]{3,2,1,0:T(8,128)S(1)}, u32[]{:S(2)}, u32[]{:S(2)}) collective-permute-start(f32[4,2,64,1024]{3,2,1,0:T(8,128)S(1)} %shard_map.77), channel_id=1, source_target_pairs={{0,1},{1,0},{2,3},{3,2},{4,5},{5,4},{6,7},{7,6},{8,9},{9,8},{10,11... | collective-permute-start | bytes 6291464 | tf_op jit(solution)/shard_map/ppermute | solution.py:253
  124.9 0.0 collective-permute-done.21.u1
  124.9 2.4 %collective-permute-done.22.u2 = f32[4,2,64,1024]{3,2,1,0:T(8,128)S(1)} collective-permute-done((f32[4,2,64,1024]{3,2,1,0:T(8,128)S(1)}, f32[4,2,64,1024]{3,2,1,0:T(8,128)S(1)}, u32[]{:S(2)}, u32[]{:S(2)}) %collective-permute-start.22) | collective-permute-done | bytes 2097184 | tf_op jit(solution)/shard_map/ppermute | solution.py:239
  127.2 2.0 %collective-permute-done.23.u3 = f32[4,2,64,1024]{3,2,1,0:T(8,128)S(1)} collective-permute-done((f32[4,2,64,1024]{3,2,1,0:T(8,128)S(1)}, f32[4,2,64,1024]{3,2,1,0:T(8,128)S(1)}, u32[]{:S(2)}, u32[]{:S(2)}) %collective-permute-start.23) | collective-permute-done | bytes 2097184 | tf_op jit(solution)/shard_map/ppermute | solution.py:239
  129.2 0.7 shard_map.78
  129.9 6.3 %collective-permute-start.24 = (f32[2,2,64,1024]{3,2,1,0:T(8,128)S(1)}, f32[2,2,64,1024]{3,2,1,0:T(8,128)S(1)}, u32[]{:S(2)}, u32[]{:S(2)}) collective-permute-start(f32[2,2,64,1024]{3,2,1,0:T(8,128)S(1)} %shard_map.78), channel_id=1, source_target_pairs={{0,1},{1,0},{2,3},{3,2},{4,5},{5,4},{6,7},{7,6},{8,9},{9,8},{10,11... | collective-permute-start | bytes 3145736 | tf_op jit(solution)/shard_map/ppermute | solution.py:250
  136.2 4.9 %collective-permute-start.8 = (f32[2,64,1024]{2,1,0:T(8,128)S(1)}, f32[2,64,1024]{2,1,0:T(8,128)S(1)}, u32[]{:S(2)}, u32[]{:S(2)}) collective-permute-start(f32[2,64,1024]{2,1,0:T(8,128)S(1)} %collective-permute-done.7.refs_7_), channel_id=1, source_target_pairs={{0,2},{1,31},{2,4},{3,1},{4,6},{5,3},{6,8},{7,5},{8,10},{9,7},{10,... | collective-permute-start | bytes 1572872 | tf_op jit(solution)/shard_map/ppermute | solution.py:235
  141.0 6.1 %collective-permute-done.8.refs_8_ = f32[2,64,1024]{2,1,0:T(8,128)S(1)} collective-permute-done((f32[2,64,1024]{2,1,0:T(8,128)S(1)}, f32[2,64,1024]{2,1,0:T(8,128)S(1)}, u32[]{:S(2)}, u32[]{:S(2)}) %collective-permute-start.8) | collective-permute-done | bytes 524320 | tf_op jit(solution)/shard_map/ppermute | solution.py:235
  147.2 3.2 %collective-permute-start.17 = (f32[2,64,1024]{2,1,0:T(8,128)S(1)}, f32[2,64,1024]{2,1,0:T(8,128)S(1)}, u32[]{:S(2)}, u32[]{:S(2)}) collective-permute-start(f32[2,64,1024]{2,1,0:T(8,128)S(1)} %collective-permute-done.8.refs_8_), channel_id=1, source_target_pairs={{0,1},{1,0},{2,3},{3,2},{4,5},{5,4},{6,7},{7,6},{8,9},{9,8},{10,11... | collective-permute-start | bytes 1572872 | tf_op jit(solution)/shard_map/ppermute | solution.py:254
  150.4 0.0 collective-permute-done.24.up_in
  150.4 1.5 shard_map.79
  151.9 0.0 collective-permute-done.17.refs_17_
  151.9 0.0 collective-permute-done.16.refs_16_
  151.9 7.5 %shard_map.80 = (f32[64,1024]{1,0:T(8,128)}, f32[64,1024]{1,0:T(8,128)}) custom-call(s32[37]{0:T(128)S(1)} %concatenate.3.info, s32[37]{0:T(128)S(1)} %collective-permute-done.other, f32[2,64,1024]{2,1,0:T(8,128)} %bitcast.19, f32[2,64,1024]{2,1,0:T(8,128)} %copy-done.1, f32[2,64,1024]{2,1,0:T(8,128)} %copy-done.3, f32[2,64,1024]{2,1,0:T(8,128)} %copy-done.5, ...), custom_call_target="tpu_custom_call" | custom-call | tf_op jit(solution)/shard_map/pallas_call | solution.py:264
  (10 shorter events, 0.0 us)
Async XLA Ops:
  0.6 20.8 %collective-permute-start.1 = (f32[2,64,1024]{2,1,0:T(8,128)}, f32[2,64,1024]{2,1,0:T(8,128)S(1)}, u32[]{:S(2)}, u32[]{:S(2)}) collective-permute-start(f32[2,64,1024]{2,1,0:T(8,128)} %bitcast.16), channel_id=1, source_target_pairs={{0,2},{1,31},{2,4},{3,1},{4,6},{5,3},{6,8},{7,5},{8,10},{9,7},{10,... | collective-permute-start | bytes 1572872 | tf_op jit(solution)/shard_map/ppermute | solution.py:235
  12.6 13.7 %collective-permute-start.9 = (f32[2,64,1024]{2,1,0:T(8,128)}, f32[2,64,1024]{2,1,0:T(8,128)S(1)}, u32[]{:S(2)}, u32[]{:S(2)}) collective-permute-start(f32[2,64,1024]{2,1,0:T(8,128)} %bitcast.17), channel_id=1, source_target_pairs={{1,2},{0,31},{3,4},{2,1},{5,6},{4,3},{7,8},{6,5},{9,10},{8,7},{11,... | collective-permute-start | bytes 1572872 | tf_op jit(solution)/shard_map/ppermute | solution.py:233
  21.4 54.5 %copy-start.1 = (f32[2,64,1024]{2,1,0:T(8,128)}, f32[2,64,1024]{2,1,0:T(8,128)S(1)}, u32[]{:S(2)}) copy-start(f32[2,64,1024]{2,1,0:T(8,128)S(1)} %collective-permute-done.1.refs_1_) | copy-start | bytes 1572868
  21.4 11.0 %collective-permute-start.2 = (f32[2,64,1024]{2,1,0:T(8,128)S(1)}, f32[2,64,1024]{2,1,0:T(8,128)S(1)}, u32[]{:S(2)}, u32[]{:S(2)}) collective-permute-start(f32[2,64,1024]{2,1,0:T(8,128)S(1)} %collective-permute-done.1.refs_1_), channel_id=1, source_target_pairs={{0,2},{1,31},{2,4},{3,1},{4,6},{5,3},{6,8},{7,5},{8,10},{9,7},{10,... | collective-permute-start | bytes 1572872 | tf_op jit(solution)/shard_map/ppermute | solution.py:235
  26.3 49.5 %copy-start.2 = (f32[2,64,1024]{2,1,0:T(8,128)}, f32[2,64,1024]{2,1,0:T(8,128)S(1)}, u32[]{:S(2)}) copy-start(f32[2,64,1024]{2,1,0:T(8,128)S(1)} %collective-permute-done.9.refs_8_.refs_9_) | copy-start | bytes 1572868
  26.3 11.7 %collective-permute-start.10 = (f32[2,64,1024]{2,1,0:T(8,128)S(1)}, f32[2,64,1024]{2,1,0:T(8,128)S(1)}, u32[]{:S(2)}, u32[]{:S(2)}) collective-permute-start(f32[2,64,1024]{2,1,0:T(8,128)S(1)} %collective-permute-done.9.refs_8_.refs_9_), channel_id=1, source_target_pairs={{0,2},{1,31},{2,4},{3,1},{4,6},{5,3},{6,8},{7,5},{8,10},{9,7},{10,... | collective-permute-start | bytes 1572872 | tf_op jit(solution)/shard_map/ppermute | solution.py:237
  32.4 43.5 %copy-start.3 = (f32[2,64,1024]{2,1,0:T(8,128)}, f32[2,64,1024]{2,1,0:T(8,128)S(1)}, u32[]{:S(2)}) copy-start(f32[2,64,1024]{2,1,0:T(8,128)S(1)} %collective-permute-done.2.refs_2_) | copy-start | bytes 1572868
  32.4 11.2 %collective-permute-start.3 = (f32[2,64,1024]{2,1,0:T(8,128)S(1)}, f32[2,64,1024]{2,1,0:T(8,128)S(1)}, u32[]{:S(2)}, u32[]{:S(2)}) collective-permute-start(f32[2,64,1024]{2,1,0:T(8,128)S(1)} %collective-permute-done.2.refs_2_), channel_id=1, source_target_pairs={{0,2},{1,31},{2,4},{3,1},{4,6},{5,3},{6,8},{7,5},{8,10},{9,7},{10,... | collective-permute-start | bytes 1572872 | tf_op jit(solution)/shard_map/ppermute | solution.py:235
  38.0 37.9 %copy-start.4 = (f32[2,64,1024]{2,1,0:T(8,128)}, f32[2,64,1024]{2,1,0:T(8,128)S(1)}, u32[]{:S(2)}) copy-start(f32[2,64,1024]{2,1,0:T(8,128)S(1)} %collective-permute-done.10.refs_9_.refs_10_) | copy-start | bytes 1572868
  38.0 11.2 %collective-permute-start.11 = (f32[2,64,1024]{2,1,0:T(8,128)S(1)}, f32[2,64,1024]{2,1,0:T(8,128)S(1)}, u32[]{:S(2)}, u32[]{:S(2)}) collective-permute-start(f32[2,64,1024]{2,1,0:T(8,128)S(1)} %collective-permute-done.10.refs_9_.refs_10_), channel_id=1, source_target_pairs={{0,2},{1,31},{2,4},{3,1},{4,6},{5,3},{6,8},{7,5},{8,10},{9,7},{10,... | collective-permute-start | bytes 1572872 | tf_op jit(solution)/shard_map/ppermute | solution.py:237
  43.6 32.2 %copy-start.5 = (f32[2,64,1024]{2,1,0:T(8,128)}, f32[2,64,1024]{2,1,0:T(8,128)S(1)}, u32[]{:S(2)}) copy-start(f32[2,64,1024]{2,1,0:T(8,128)S(1)} %collective-permute-done.3.refs_3_) | copy-start | bytes 1572868
  43.7 20.8 %collective-permute-start.4 = (f32[2,64,1024]{2,1,0:T(8,128)S(1)}, f32[2,64,1024]{2,1,0:T(8,128)}, u32[]{:S(2)}, u32[]{:S(2)}) collective-permute-start(f32[2,64,1024]{2,1,0:T(8,128)S(1)} %collective-permute-done.3.refs_3_), channel_id=1, source_target_pairs={{0,2},{1,31},{2,4},{3,1},{4,6},{5,3},{6,8},{7,5},{8,10},{9,7},{10,... | collective-permute-start | bytes 1572872 | tf_op jit(solution)/shard_map/ppermute | solution.py:235
  49.3 26.6 %copy-start.6 = (f32[2,64,1024]{2,1,0:T(8,128)}, f32[2,64,1024]{2,1,0:T(8,128)S(1)}, u32[]{:S(2)}) copy-start(f32[2,64,1024]{2,1,0:T(8,128)S(1)} %collective-permute-done.11.refs_10_.refs_11_) | copy-start | bytes 1572868
  49.3 17.1 %collective-permute-start.12 = (f32[2,64,1024]{2,1,0:T(8,128)S(1)}, f32[2,64,1024]{2,1,0:T(8,128)}, u32[]{:S(2)}, u32[]{:S(2)}) collective-permute-start(f32[2,64,1024]{2,1,0:T(8,128)S(1)} %collective-permute-done.11.refs_10_.refs_11_), channel_id=1, source_target_pairs={{0,2},{1,31},{2,4},{3,1},{4,6},{5,3},{6,8},{7,5},{8,10},{9,7},{10,... | collective-permute-start | bytes 1572872 | tf_op jit(solution)/shard_map/ppermute | solution.py:237
  54.3 14.8 %collective-permute-start.19 = (f32[2,64,1024]{2,1,0:T(8,128)}, f32[2,64,1024]{2,1,0:T(8,128)}, u32[]{:S(2)}, u32[]{:S(2)}) collective-permute-start(f32[2,64,1024]{2,1,0:T(8,128)} %bitcast.20), channel_id=1, source_target_pairs={{0,64},{1,257},{32,96},{33,289},{64,0},{65,321},{96,32},{97,353},{... | collective-permute-start | bytes 1572872 | tf_op jit(solution)/shard_map/ppermute | solution.py:238
  59.1 15.1 %collective-permute-start.20 = (f32[2,64,1024]{2,1,0:T(8,128)}, f32[2,64,1024]{2,1,0:T(8,128)}, u32[]{:S(2)}, u32[]{:S(2)}) collective-permute-start(f32[2,64,1024]{2,1,0:T(8,128)} %bitcast.21), channel_id=1, source_target_pairs={{0,96},{1,385},{32,0},{33,417},{64,32},{65,449},{96,64},{97,481},{... | collective-permute-start | bytes 1572872 | tf_op jit(solution)/shard_map/ppermute | solution.py:238
  61.8 12.4 %collective-permute-start.18 = (f32[2,64,1024]{2,1,0:T(8,128)}, f32[2,64,1024]{2,1,0:T(8,128)}, u32[]{:S(2)}, u32[]{:S(2)}) collective-permute-start(f32[2,64,1024]{2,1,0:T(8,128)} %bitcast.22), channel_id=1, source_target_pairs={{0,32},{1,129},{32,64},{33,161},{64,96},{65,193},{96,0},{97,225},{... | collective-permute-start | bytes 1572872 | tf_op jit(solution)/shard_map/ppermute | solution.py:238
  64.4 21.4 %collective-permute-start.5 = (f32[2,64,1024]{2,1,0:T(8,128)}, f32[2,64,1024]{2,1,0:T(8,128)}, u32[]{:S(2)}, u32[]{:S(2)}) collective-permute-start(f32[2,64,1024]{2,1,0:T(8,128)} %collective-permute-done.4.refs_4_), channel_id=1, source_target_pairs={{0,2},{1,31},{2,4},{3,1},{4,6},{5,3},{6,8},{7,5},{8,10},{9,7},{10,... | collective-permute-start | bytes 1572872 | tf_op jit(solution)/shard_map/ppermute | solution.py:235
  66.4 23.4 %collective-permute-start.13 = (f32[2,64,1024]{2,1,0:T(8,128)}, f32[2,64,1024]{2,1,0:T(8,128)}, u32[]{:S(2)}, u32[]{:S(2)}) collective-permute-start(f32[2,64,1024]{2,1,0:T(8,128)} %collective-permute-done.12.refs_11_.refs_12_), channel_id=1, source_target_pairs={{0,2},{1,31},{2,4},{3,1},{4,6},{5,3},{6,8},{7,5},{8,10},{9,7},{10,... | collective-permute-start | bytes 1572872 | tf_op jit(solution)/shard_map/ppermute | solution.py:237
  69.1 13.9 %collective-permute-start = (s32[37]{0:T(128)S(1)}, s32[37]{0:T(128)S(1)}, u32[]{:S(2)}, u32[]{:S(2)}) collective-permute-start(s32[37]{0:T(128)S(1)} %concatenate.3.info), channel_id=1, source_target_pairs={{0,1},{1,0},{2,3},{3,2},{4,5},{5,4},{6,7},{7,6},{8,9},{9,8},{10,11... | collective-permute-start | bytes 452 | tf_op jit(solution)/shard_map/ppermute | solution.py:240
  75.9 49.0 %collective-permute-start.21 = (f32[4,2,64,1024]{3,2,1,0:T(8,128)S(1)}, f32[4,2,64,1024]{3,2,1,0:T(8,128)S(1)}, u32[]{:S(2)}, u32[]{:S(2)}) collective-permute-start(f32[4,2,64,1024]{3,2,1,0:T(8,128)S(1)} %pad_maximum_fusion.u0), channel_id=1, source_target_pairs={{0,128},{1,33},{32,160},{33,65},{64,192},{65,97},{96,224},{97,1},{... | collective-permute-start | bytes 6291464 | tf_op jit(solution)/shard_map/ppermute | solution.py:239
  78.4 48.8 %collective-permute-start.22 = (f32[4,2,64,1024]{3,2,1,0:T(8,128)S(1)}, f32[4,2,64,1024]{3,2,1,0:T(8,128)S(1)}, u32[]{:S(2)}, u32[]{:S(2)}) collective-permute-start(f32[4,2,64,1024]{3,2,1,0:T(8,128)S(1)} %pad_maximum_fusion.u0), channel_id=1, source_target_pairs={{0,256},{1,65},{32,288},{33,97},{64,320},{65,1},{96,352},{97,33},{... | collective-permute-start | bytes 6291464 | tf_op jit(solution)/shard_map/ppermute | solution.py:239
  83.0 46.2 %collective-permute-start.23 = (f32[4,2,64,1024]{3,2,1,0:T(8,128)S(1)}, f32[4,2,64,1024]{3,2,1,0:T(8,128)S(1)}, u32[]{:S(2)}, u32[]{:S(2)}) collective-permute-start(f32[4,2,64,1024]{3,2,1,0:T(8,128)S(1)} %pad_maximum_fusion.u0), channel_id=1, source_target_pairs={{0,384},{1,97},{32,416},{33,1},{64,448},{65,33},{96,480},{97,65},{... | collective-permute-start | bytes 6291464 | tf_op jit(solution)/shard_map/ppermute | solution.py:239
  85.9 10.4 %collective-permute-start.6 = (f32[2,64,1024]{2,1,0:T(8,128)}, f32[2,64,1024]{2,1,0:T(8,128)S(1)}, u32[]{:S(2)}, u32[]{:S(2)}) collective-permute-start(f32[2,64,1024]{2,1,0:T(8,128)} %collective-permute-done.5.refs_5_), channel_id=1, source_target_pairs={{0,2},{1,31},{2,4},{3,1},{4,6},{5,3},{6,8},{7,5},{8,10},{9,7},{10,... | collective-permute-start | bytes 1572872 | tf_op jit(solution)/shard_map/ppermute | solution.py:235
  89.8 12.1 %collective-permute-start.14 = (f32[2,64,1024]{2,1,0:T(8,128)}, f32[2,64,1024]{2,1,0:T(8,128)S(1)}, u32[]{:S(2)}, u32[]{:S(2)}) collective-permute-start(f32[2,64,1024]{2,1,0:T(8,128)} %collective-permute-done.13.refs_12_.refs_13_), channel_id=1, source_target_pairs={{0,2},{1,31},{2,4},{3,1},{4,6},{5,3},{6,8},{7,5},{8,10},{9,7},{10,... | collective-permute-start | bytes 1572872 | tf_op jit(solution)/shard_map/ppermute | solution.py:237
  96.3 16.9 %copy-start.7 = (f32[2,64,1024]{2,1,0:T(8,128)}, f32[2,64,1024]{2,1,0:T(8,128)S(1)}, u32[]{:S(2)}) copy-start(f32[2,64,1024]{2,1,0:T(8,128)S(1)} %collective-permute-done.6.refs_6_) | copy-start | bytes 1572868
  96.3 11.2 %collective-permute-start.7 = (f32[2,64,1024]{2,1,0:T(8,128)S(1)}, f32[2,64,1024]{2,1,0:T(8,128)S(1)}, u32[]{:S(2)}, u32[]{:S(2)}) collective-permute-start(f32[2,64,1024]{2,1,0:T(8,128)S(1)} %collective-permute-done.6.refs_6_), channel_id=1, source_target_pairs={{0,2},{1,31},{2,4},{3,1},{4,6},{5,3},{6,8},{7,5},{8,10},{9,7},{10,... | collective-permute-start | bytes 1572872 | tf_op jit(solution)/shard_map/ppermute | solution.py:235
  101.9 11.3 %copy-start.8 = (f32[2,64,1024]{2,1,0:T(8,128)}, f32[2,64,1024]{2,1,0:T(8,128)S(1)}, u32[]{:S(2)}) copy-start(f32[2,64,1024]{2,1,0:T(8,128)S(1)} %collective-permute-done.14.refs_13_.refs_14_) | copy-start | bytes 1572868
  101.9 11.2 %collective-permute-start.15 = (f32[2,64,1024]{2,1,0:T(8,128)S(1)}, f32[2,64,1024]{2,1,0:T(8,128)S(1)}, u32[]{:S(2)}, u32[]{:S(2)}) collective-permute-start(f32[2,64,1024]{2,1,0:T(8,128)S(1)} %collective-permute-done.14.refs_13_.refs_14_), channel_id=1, source_target_pairs={{0,2},{1,31},{2,4},{3,1},{4,6},{5,3},{6,8},{7,5},{8,10},{9,7},{10,... | collective-permute-start | bytes 1572872 | tf_op jit(solution)/shard_map/ppermute | solution.py:237
  115.0 35.4 %copy-start = (f32[1,1,2,64,1024]{4,3,2,1,0:T(8,128)S(1)}, f32[1,1,2,64,1024]{4,3,2,1,0:T(8,128)}, u32[]{:S(2)}) copy-start(f32[1,1,2,64,1024]{4,3,2,1,0:T(8,128)} %param.11) | copy-start | bytes 1572868
  115.0 36.9 %collective-permute-start.16 = (f32[4,2,64,1024]{3,2,1,0:T(8,128)S(1)}, f32[4,2,64,1024]{3,2,1,0:T(8,128)S(1)}, u32[]{:S(2)}, u32[]{:S(2)}) collective-permute-start(f32[4,2,64,1024]{3,2,1,0:T(8,128)S(1)} %shard_map.77), channel_id=1, source_target_pairs={{0,1},{1,0},{2,3},{3,2},{4,5},{5,4},{6,7},{7,6},{8,9},{9,8},{10,11... | collective-permute-start | bytes 6291464 | tf_op jit(solution)/shard_map/ppermute | solution.py:253
  129.9 20.5 %collective-permute-start.24 = (f32[2,2,64,1024]{3,2,1,0:T(8,128)S(1)}, f32[2,2,64,1024]{3,2,1,0:T(8,128)S(1)}, u32[]{:S(2)}, u32[]{:S(2)}) collective-permute-start(f32[2,2,64,1024]{3,2,1,0:T(8,128)S(1)} %shard_map.78), channel_id=1, source_target_pairs={{0,1},{1,0},{2,3},{3,2},{4,5},{5,4},{6,7},{7,6},{8,9},{9,8},{10,11... | collective-permute-start | bytes 3145736 | tf_op jit(solution)/shard_map/ppermute | solution.py:250
  136.2 11.0 %collective-permute-start.8 = (f32[2,64,1024]{2,1,0:T(8,128)S(1)}, f32[2,64,1024]{2,1,0:T(8,128)S(1)}, u32[]{:S(2)}, u32[]{:S(2)}) collective-permute-start(f32[2,64,1024]{2,1,0:T(8,128)S(1)} %collective-permute-done.7.refs_7_), channel_id=1, source_target_pairs={{0,2},{1,31},{2,4},{3,1},{4,6},{5,3},{6,8},{7,5},{8,10},{9,7},{10,... | collective-permute-start | bytes 1572872 | tf_op jit(solution)/shard_map/ppermute | solution.py:235
  147.2 4.8 %collective-permute-start.17 = (f32[2,64,1024]{2,1,0:T(8,128)S(1)}, f32[2,64,1024]{2,1,0:T(8,128)S(1)}, u32[]{:S(2)}, u32[]{:S(2)}) collective-permute-start(f32[2,64,1024]{2,1,0:T(8,128)S(1)} %collective-permute-done.8.refs_8_), channel_id=1, source_target_pairs={{0,1},{1,0},{2,3},{3,2},{4,5},{5,4},{6,7},{7,6},{8,9},{9,8},{10,11... | collective-permute-start | bytes 1572872 | tf_op jit(solution)/shard_map/ppermute | solution.py:254
